TPU v7x, 256 devices: a whole 4x4x8 slice. The times are simulated.
256 devices in a mesh: gx: 128 (over y_hi, x, z, core), gy: 2 (over y_lo).
Axes of the slice: x: 4, y: 4 (y_hi: 2, y_lo: 2; y = y_hi * 2 + y_lo), z: 8, core: 2. Of those that a mesh axis runs over, the one named last changes fastest.
Arguments:
- orbitals: float32 [2, 32, 8192, 256], P(None, None, 'gx', 'gy'), may hold values from -12 to 12
- potential: float32 [32, 8192, 256], P(None, 'gx', 'gy'), may hold values from 0.5 to 2
- shift_ratio: float32 [1], replicated, may hold values from 16 to 48
Outputs:
- orbitals_next: float32 [2, 32, 8192, 256], P(None, None, 'gx', 'gy')
All inputs are finite; a program needn't handle non-finite values.
Results may differ from a plain program's by a relative error of at most 0.0003.
Values sent between devices are 32-bit elements; how exact they have to be, the bound alone decides.
No kernel may reach another device: no remote copies, remote signals or barrier semaphores. Data moves between devices by JAX's collectives and lax.ppermute only.
A program may use at most 128 MiB of HBM per device.

v0:
```python
import functools

import jax
import jax.numpy as jnp
from jax import lax
from jax.sharding import Mesh
from jax.sharding import PartitionSpec as P

GX = ("gx_0", "gx_1", "gx_2", "gx_3")
GX_GY = ("gx_0", "gx_1", "gx_2", "gx_3", "gy")


TAU = 4.0
EPS = 1e-06
COUPLING_FIRST = 0.06
COUPLING_SECOND = 0.05
COUPLING_CROSS = 0.04


def with_halo(x, sides, width):
    edges = {}
    for axis, dim in sides:
        peers, length = (lax.axis_size(axis), x.shape[dim])
        up = [(i, (i + 1) % peers) for i in range(peers)]
        last = lax.slice_in_dim(x, length - width, length, axis=dim)
        initial = lax.slice_in_dim(x, 0, width, axis=dim)
        edges[dim] = (
            lax.ppermute(last, axis, up),
            lax.ppermute(initial, axis, [(b, a) for a, b in up]),
        )
    done = []
    for _, dim in sides:
        low, high = edges[dim]
        around = [(width, width) if d in done else (0, 0) for d in range(x.ndim)]
        x = jnp.concatenate([jnp.pad(low, around), x, jnp.pad(high, around)], axis=dim)
        done.append(dim)
    return x


def by_axis(x, axes):
    return functools.reduce(lax.psum, axes, x)


def hamiltonian(orbitals, padded, potential):
    neighbours = padded[:, :, 2:, 1:-1] + padded[:, :, :-2, 1:-1]
    neighbours = neighbours + padded[:, :, 1:-1, 2:] + padded[:, :, 1:-1, :-2]
    neighbours = neighbours + jnp.roll(orbitals, 1, axis=1) + jnp.roll(orbitals, -1, axis=1)
    laplace = neighbours - 6.0 * orbitals
    squares = orbitals * orbitals
    density_first = COUPLING_FIRST * squares[0] + COUPLING_CROSS * squares[1]
    density_second = COUPLING_CROSS * squares[0] + COUPLING_SECOND * squares[1]
    density = jnp.stack([density_first, density_second])
    return -0.5 * laplace + (potential[None] + density) * orbitals


def decay_tables(length, decay_rate):
    index = jnp.arange(length, dtype=jnp.int32)
    spacing = (index[:, None] - index[None, :]).astype(jnp.float32)
    lower = jnp.where(spacing >= 0.0, jnp.exp(-decay_rate * jnp.maximum(spacing, 0.0)), 0.0)
    return (lower, lower.T)


def local_sweeps(field, lower, upper):
    forward = jnp.einsum(
        "ic,...cy->...iy",
        lower,
        field,
        precision=lax.Precision.HIGHEST,
        preferred_element_type=jnp.float32,
    )
    backward = jnp.einsum(
        "ic,...cy->...iy",
        upper,
        field,
        precision=lax.Precision.HIGHEST,
        preferred_element_type=jnp.float32,
    )
    return (forward, backward)


def assemble(forward, backward, field, carry_forward, carry_backward, decay_rate):
    length = field.shape[-2]
    steps_in = jnp.arange(length, dtype=jnp.float32)
    rising = jnp.exp(-decay_rate * (steps_in + 1.0))[:, None]
    falling = jnp.exp(-decay_rate * (length - steps_in))[:, None]
    total_forward = forward + rising * carry_forward[..., None, :]
    total_backward = backward + falling * carry_backward[..., None, :]
    return jnp.tanh(0.5 * decay_rate) * (total_forward + total_backward - field)


def circular_weights(owners, count, block_decay, wrap_factor):
    others = jnp.arange(count, dtype=jnp.int32)
    ahead = jnp.mod(owners[:, None] - 1 - others[None, :], count).astype(jnp.float32)
    behind = jnp.mod(others[None, :] - 1 - owners[:, None], count).astype(jnp.float32)
    return (
        jnp.exp(-block_decay * ahead) / wrap_factor,
        jnp.exp(-block_decay * behind) / wrap_factor,
    )


def gathered_tips(residual, decay_rate, wrap_factor):
    width = residual.shape[2]
    groups = lax.axis_size(GX)
    lower, upper = decay_tables(width, decay_rate)
    forward, backward = local_sweeps(residual, lower, upper)
    tips = jnp.stack([forward[:, :, width - 1, :], backward[:, :, 0, :]])[None]
    every = lax.all_gather(tips, GX, axis=0, tiled=True)
    position = lax.axis_index(GX)
    ahead, behind = circular_weights(position[None], groups, decay_rate * width, wrap_factor)
    carry_forward = jnp.einsum(
        "k,kazy->azy",
        ahead[0],
        every[:, 0],
        precision=lax.Precision.HIGHEST,
        preferred_element_type=jnp.float32,
    )
    carry_backward = jnp.einsum(
        "k,kazy->azy",
        behind[0],
        every[:, 1],
        precision=lax.Precision.HIGHEST,
        preferred_element_type=jnp.float32,
    )
    return assemble(forward, backward, residual, carry_forward, carry_backward, decay_rate)


def shards(orbitals, potential, shift_ratio):
    groups = lax.axis_size(GX)
    columns = lax.axis_size("gy")
    padded = with_halo(orbitals, ((GX, 2), ("gy", 3)), 1)
    applied = hamiltonian(orbitals, padded, potential)
    cells = float(orbitals.shape[1] * orbitals.shape[2] * orbitals.shape[3] * groups * columns)
    sum_cross = jnp.sum(orbitals * applied, axis=(1, 2, 3))
    sum_square = jnp.sum(orbitals * orbitals, axis=(1, 2, 3))
    line_cells = orbitals.shape[2] * groups
    sigma = shift_ratio[0] / float(line_cells * line_cells)
    decay_rate = jnp.log1p(sigma + jnp.sqrt(sigma * (sigma + 2.0)))
    wrap_factor = -jnp.expm1(-decay_rate * line_cells)
    total_cross, total_square = (by_axis(sum_cross, GX_GY), by_axis(sum_square, GX_GY))
    mean_square = total_square / cells
    energy = total_cross / cells / (mean_square + EPS)
    residual = applied - energy[:, None, None, None] * orbitals
    direction = gathered_tips(residual, decay_rate, wrap_factor)
    update = orbitals - TAU * direction
    mass_update = jnp.sum(update * update, axis=(1, 2, 3))
    total_update = by_axis(mass_update, GX_GY)
    ratio = jnp.sqrt(mean_square / (total_update / cells + EPS))
    return update * ratio[:, None, None, None]


def solution(mesh):
    split = Mesh(
        mesh.devices.reshape(2, 4, 8, 2, mesh.shape["gy"]), ("gx_0", "gx_1", "gx_2", "gx_3", "gy")
    )
    return jax.shard_map(
        shards,
        mesh=split,
        in_specs=(P(None, None, GX, "gy"), P(None, GX, "gy"), P()),
        out_specs=P(None, None, GX, "gy"),
        check_vma=False,
    )
```

profile of v0, /device:TPU:1, one launch (start us, length us, event | category | flops | bytes accessed | tf_op | source)
XLA Modules:
  0.0 278.2 jit_solution(18290218811083623917)
XLA Ops:
  6.5 0.0 all-gather.3.cloned.1.call-start
  6.5 5.0 %fusion.64 = (f32[2,32,64,1]{3,2,1,0:T(8,128)}, f32[2,32,64,1]{3,2,1,0:T(8,128)}) fusion(f32[2,32,64,128]{3,2,1,0:T(8,128)} %param.3), kind=kLoop, calls=%fused_computation.97 | loop fusion | bytes 65536 | tf_op jit(solution)/shard_map/slice | solution.py:26
  11.6 0.0 copy-start
  11.6 2.4 copy.21
  14.0 2.2 collective-permute-start.2
  16.2 2.3 copy.22
  18.4 0.1 collective-permute-start.3
  18.5 0.0 copy-done
  18.6 3.2 %collective-permute-start = (f32[2,32,1,128]{3,2,1,0:T(1,128)S(1)}, f32[2,32,1,128]{3,2,1,0:T(1,128)S(1)}, u32[]{:S(2)}, u32[]{:S(2)}) collective-permute-start(f32[2,32,1,128]{3,2,1,0:T(1,128)S(1)} %get-tuple-element.25), channel_id=1, source_target_pairs={{2,0},{4,2},{6,4},{8,6},{10,8},{12,10},{14,12},{16,14},{18,16},{20... | collective-permute-start | bytes 98312 | tf_op jit(solution)/shard_map/ppermute | solution.py:29
  21.7 0.0 collective-permute-start.1
  21.8 0.4 mul.191
  22.1 2.5 fusion.67
  24.7 1.4 multiply_add_fusion.1
  26.8 0.0 collective-permute-done.2
  26.8 2.0 copy.7
  28.8 0.0 collective-permute-done.3
  28.8 2.0 copy.9
  30.9 0.0 collective-permute-done
  30.9 0.0 collective-permute-done.1
  30.9 6.8 %multiply_reduce_fusion.2 = (f32[2]{0:T(128)S(1)}, f32[2]{0:T(128)S(1)}, f32[2,32,64,128]{3,2,1,0:T(8,128)}) fusion(f32[2,32,64,128]{3,2,1,0:T(8,128)S(1)} %copy-done, f32[1,32,64,128]{3,2,1,0:T(8,128)} %get-tuple-element.31, f32[1,32,64,128]{3,2,1,0:T(8,128)S(1)} %get-tuple-element.30, f32[32,64,128]{2,1,0:T(8,128)} %param.4, ...), kind=kLoop, calls=%fused_computation.96 | loop fusion | flops 16777212 | bytes 11632656 | tf_op jit(solution)/shard_map/reduce_sum | solution.py:134
  37.6 5.3 %all-reduce.6 = (f32[2]{0:T(128)S(1)}, f32[2]{0:T(128)S(1)}) all-reduce(f32[2]{0:T(128)S(1)} %get-tuple-element.6, f32[2]{0:T(128)S(1)} %get-tuple-element.5), channel_id=1, replica_groups=mesh['gx_0'=2,'gx_1'=4,'gx_2'=8,'gx_3'=2,'gy'=2] {'gx_0'}, use_global_device_ids=true, to_apply=%region_1.2 | all-reduce | flops 4 | bytes 32 | tf_op jit(solution)/shard_map/psum | solution.py:41
  42.9 8.6 %all-reduce.3 = (f32[2]{0:T(128)S(1)}, f32[2]{0:T(128)S(1)}) all-reduce(f32[2]{0:T(128)S(1)} %get-tuple-element.15, f32[2]{0:T(128)S(1)} %get-tuple-element.16), channel_id=1, replica_groups=mesh['gx_0'=2,'gx_1'=4,'gx_2'=8,'gx_3'=2,'gy'=2] {'gx_1'}, use_global_device_ids=true, to_apply=%region_2.3 | all-reduce | flops 4 | bytes 32 | tf_op jit(solution)/shard_map/psum | solution.py:41
  51.5 20.6 %all-reduce.2 = (f32[2]{0:T(128)S(1)}, f32[2]{0:T(128)S(1)}) all-reduce(f32[2]{0:T(128)S(1)} %get-tuple-element.9, f32[2]{0:T(128)S(1)} %get-tuple-element.10), channel_id=1, replica_groups=mesh['gx_0'=2,'gx_1'=4,'gx_2'=8,'gx_3'=2,'gy'=2] {'gx_2'}, use_global_device_ids=true, to_apply=%region_3.4 | all-reduce | flops 4 | bytes 32 | tf_op jit(solution)/shard_map/psum | solution.py:41
  72.1 3.8 %all-reduce.5 = (f32[2]{0:T(128)S(1)}, f32[2]{0:T(128)S(1)}) all-reduce(f32[2]{0:T(128)S(1)} %get-tuple-element.7, f32[2]{0:T(128)S(1)} %get-tuple-element.8), channel_id=1, replica_groups=mesh['gx_0'=2,'gx_1'=4,'gx_2'=8,'gx_3'=2,'gy'=2] {'gx_3'}, use_global_device_ids=true, to_apply=%region_4.5 | all-reduce | flops 4 | bytes 32 | tf_op jit(solution)/shard_map/psum | solution.py:41
  75.9 3.9 %all-reduce.4 = (f32[2]{0:T(128)S(1)}, f32[2]{0:T(128)S(1)}) all-reduce(f32[2]{0:T(128)S(1)} %get-tuple-element.13, f32[2]{0:T(128)S(1)} %get-tuple-element.14), channel_id=1, replica_groups=mesh['gx_0'=2,'gx_1'=4,'gx_2'=8,'gx_3'=2,'gy'=2] {'gy'}, use_global_device_ids=true, to_apply=%region_5.6 | all-reduce | flops 4 | bytes 32 | tf_op jit(solution)/shard_map/psum | solution.py:41
  79.8 0.0 copy-start.1
  79.8 4.0 %convolution_bitcast_fusion.1 = f32[2,32,64,128]{3,2,1,0:T(8,128)S(1)} fusion(f32[]{:T(128)S(6)} %neg.6, f32[2,32,64,128]{3,2,1,0:T(8,128)} %get-tuple-element.19, f32[2,32,64,128]{3,2,1,0:T(8,128)S(1)} %copy-done, f32[2]{0:T(128)S(1)} %add_divide_fusion.1), kind=kOutput, calls=%fused_computation.33 | convolution fusion | flops 403726336 | bytes 6291468 | tf_op jit(solution)/shard_map/ic,...cy->...iy/dot_general | solution.py:64
  83.8 0.0 copy-done.1
  83.8 0.0 copy-start.3
  83.8 2.3 convolution_bitcast_fusion
  86.1 0.0 copy-done.3
  86.1 0.0 copy-start.5
  86.2 1.3 copy-done.5
  87.5 0.6 pad_maximum_fusion.6
  88.1 0.0 all-gather.3.cloned.1.call-update
  88.2 125.2 %all-gather.3.cloned.1.call-done = f32[256,2,32,128]{3,2,1,0:T(8,128)} async-done(((f32[2,2,32,128]{3,2,1,0:T(8,128)}), f32[256,2,32,128]{3,2,1,0:T(8,128)}) %all-gather.3.cloned.1.call-update) | async-done | bytes 8388624 | tf_op jit(solution)/shard_map/all_gather | solution.py:107
  213.4 4.5 %slice_bitcast_fusion.1 = (f32[128,2,32,128]{3,2,1,0:T(8,128)S(1)}, f32[128,2,32,128]{3,2,1,0:T(8,128)S(1)}) fusion(f32[128,2,2,32,128]{4,3,2,1,0:T(8,128)} %bitcast.40), kind=kLoop, calls=%fused_computation.1 | loop fusion | bytes 16777216 | tf_op jit(solution)/shard_map/squeeze | solution.py:113
  218.0 0.0 copy-start.6
  218.0 4.3 %fusion = f32[1,2,32,128]{3,0,2,1:T(1,128)S(1)} fusion(f32[128,2,32,128]{3,2,1,0:T(8,128)S(1)} %get-tuple-element.21, s32[]{:T(128)S(6)} %add.186, f32[]{:T(128)S(6)} %neg.15, f32[]{:T(128)S(6)} %neg.14), kind=kOutput, calls=%fused_computation.2 | convolution fusion | flops 12584960 | bytes 4227084 | tf_op jit(solution)/shard_map/k,kazy->azy/dot_general | solution.py:117
  222.4 0.0 copy-start.2
  222.4 0.0 copy-start.4
  222.4 4.6 %fusion.2 = f32[1,2,32,128]{3,0,2,1:T(1,128)S(1)} fusion(f32[128,2,32,128]{3,2,1,0:T(8,128)S(1)} %get-tuple-element.20, f32[]{:T(128)S(6)} %neg.15, s32[]{:T(128)S(6)} %sub.101, f32[]{:T(128)S(6)} %neg.14), kind=kOutput, calls=%fused_computation.4 | convolution fusion | flops 12584832 | bytes 4227084 | tf_op jit(solution)/shard_map/k,kazy->azy/dot_general | solution.py:110
  226.9 0.0 copy-done.6
  226.9 0.0 copy-done.2
  226.9 0.0 copy-done.4
  227.0 2.5 multiply_reduce_fusion
  229.4 5.3 %psum.115 = f32[2]{0:T(128)S(1)} all-reduce(f32[2]{0:T(128)S(1)} %get-tuple-element.17), channel_id=1, replica_groups=mesh['gx_0'=2,'gx_1'=4,'gx_2'=8,'gx_3'=2,'gy'=2] {'gx_0'}, use_global_device_ids=true, to_apply=%region_13.14 | all-reduce | flops 2 | bytes 16 | tf_op jit(solution)/shard_map/psum | solution.py:41
  234.7 8.5 %psum.116 = f32[2]{0:T(128)S(1)} all-reduce(f32[2]{0:T(128)S(1)} %psum.115), channel_id=1, replica_groups=mesh['gx_0'=2,'gx_1'=4,'gx_2'=8,'gx_3'=2,'gy'=2] {'gx_1'}, use_global_device_ids=true, to_apply=%region_14.15 | all-reduce | flops 2 | bytes 16 | tf_op jit(solution)/shard_map/psum | solution.py:41
  243.2 11.8 %psum.117 = f32[2]{0:T(128)S(1)} all-reduce(f32[2]{0:T(128)S(1)} %psum.116), channel_id=1, replica_groups=mesh['gx_0'=2,'gx_1'=4,'gx_2'=8,'gx_3'=2,'gy'=2] {'gx_2'}, use_global_device_ids=true, to_apply=%region_15.16 | all-reduce | flops 2 | bytes 16 | tf_op jit(solution)/shard_map/psum | solution.py:41
  255.0 9.3 %psum.118 = f32[2]{0:T(128)S(1)} all-reduce(f32[2]{0:T(128)S(1)} %psum.117), channel_id=1, replica_groups=mesh['gx_0'=2,'gx_1'=4,'gx_2'=8,'gx_3'=2,'gy'=2] {'gx_3'}, use_global_device_ids=true, to_apply=%region_16.17 | all-reduce | flops 2 | bytes 16 | tf_op jit(solution)/shard_map/psum | solution.py:41
  264.3 3.8 %psum.119 = f32[2]{0:T(128)S(1)} all-reduce(f32[2]{0:T(128)S(1)} %psum.118), channel_id=1, replica_groups=mesh['gx_0'=2,'gx_1'=4,'gx_2'=8,'gx_3'=2,'gy'=2] {'gy'}, use_global_device_ids=true, to_apply=%region_17.18 | all-reduce | flops 2 | bytes 16 | tf_op jit(solution)/shard_map/psum | solution.py:41
  268.1 3.3 %broadcast_multiply_fusion = f32[2,32,64,128]{3,2,1,0:T(8,128)} fusion(f32[2,32,64,128]{3,2,1,0:T(8,128)} %get-tuple-element.18, f32[2]{0:T(128)S(1)} %fusion.40), kind=kLoop, calls=%fused_computation.34 | loop fusion | flops 524288 | bytes 4194312 | tf_op jit(solution)/shard_map/mul | solution.py:148
  (7 shorter events, 0.2 us)
Async XLA Ops:
  6.5 206.9 %all-gather.3.cloned.1.call-start = ((), (), s32[]{:S(2)}) async-start(), calls=%async_computation | async-start | bytes 8454144 | tf_op jit(solution)/shard_map/all_gather | solution.py:107
  11.6 6.9 %copy-start = (f32[2,32,64,128]{3,2,1,0:T(8,128)S(1)}, f32[2,32,64,128]{3,2,1,0:T(8,128)}, u32[]{:S(2)}) copy-start(f32[2,32,64,128]{3,2,1,0:T(8,128)} %param.3) | copy-start | bytes 6291460
  14.0 12.8 %collective-permute-start.2 = (f32[2,32,64,1]{2,1,3,0:T(8,128)S(1)}, f32[2,32,64,1]{2,1,3,0:T(8,128)S(1)}, u32[]{:S(2)}, u32[]{:S(2)}) collective-permute-start(f32[2,32,64,1]{2,1,3,0:T(8,128)S(1)} %copy.21), channel_id=1, source_target_pairs={{1,0},{0,1},{3,2},{2,3},{5,4},{4,5},{7,6},{6,7},{9,8},{8,9},{11,10... | collective-permute-start | bytes 49160 | tf_op jit(solution)/shard_map/ppermute | solution.py:29
  18.4 10.4 %collective-permute-start.3 = (f32[2,32,64,1]{2,1,3,0:T(8,128)S(1)}, f32[2,32,64,1]{2,1,3,0:T(8,128)S(1)}, u32[]{:S(2)}, u32[]{:S(2)}) collective-permute-start(f32[2,32,64,1]{2,1,3,0:T(8,128)S(1)} %copy.22), channel_id=1, source_target_pairs={{0,1},{1,0},{2,3},{3,2},{4,5},{5,4},{6,7},{7,6},{8,9},{9,8},{10,11... | collective-permute-start | bytes 49160 | tf_op jit(solution)/shard_map/ppermute | solution.py:28
  18.6 12.3 %collective-permute-start = (f32[2,32,1,128]{3,2,1,0:T(1,128)S(1)}, f32[2,32,1,128]{3,2,1,0:T(1,128)S(1)}, u32[]{:S(2)}, u32[]{:S(2)}) collective-permute-start(f32[2,32,1,128]{3,2,1,0:T(1,128)S(1)} %get-tuple-element.25), channel_id=1, source_target_pairs={{2,0},{4,2},{6,4},{8,6},{10,8},{12,10},{14,12},{16,14},{18,16},{20... | collective-permute-start | bytes 98312 | tf_op jit(solution)/shard_map/ppermute | solution.py:29
  21.7 9.1 %collective-permute-start.1 = (f32[2,32,1,128]{3,2,1,0:T(1,128)S(1)}, f32[2,32,1,128]{3,2,1,0:T(1,128)S(1)}, u32[]{:S(2)}, u32[]{:S(2)}) collective-permute-start(f32[2,32,1,128]{3,2,1,0:T(1,128)S(1)} %get-tuple-element.24), channel_id=1, source_target_pairs={{0,2},{2,4},{4,6},{6,8},{8,10},{10,12},{12,14},{14,16},{16,18},{18... | collective-permute-start | bytes 98312 | tf_op jit(solution)/shard_map/ppermute | solution.py:28
  79.8 4.0 %copy-start.1 = (f32[2,32,64,128]{3,2,1,0:T(8,128)S(1)}, f32[2,32,64,128]{3,2,1,0:T(8,128)}, u32[]{:S(2)}) copy-start(f32[2,32,64,128]{3,2,1,0:T(8,128)} %get-tuple-element.19) | copy-start | bytes 6291460
  83.8 2.3 copy-start.3
  86.1 1.3 copy-start.5
  218.0 8.9 %copy-start.6 = (f32[2,32,64,128]{3,2,1,0:T(8,128)S(1)}, f32[2,32,64,128]{3,2,1,0:T(8,128)}, u32[]{:S(2)}) copy-start(f32[2,32,64,128]{3,2,1,0:T(8,128)} %copy-done.5) | copy-start | bytes 6291460
  222.4 4.6 %copy-start.2 = (f32[2,32,64,128]{3,2,1,0:T(8,128)S(1)}, f32[2,32,64,128]{3,2,1,0:T(8,128)}, u32[]{:S(2)}) copy-start(f32[2,32,64,128]{3,2,1,0:T(8,128)} %get-tuple-element.19) | copy-start | bytes 6291460
  222.4 4.6 %copy-start.4 = (f32[2,32,64,128]{3,2,1,0:T(8,128)S(1)}, f32[2,32,64,128]{3,2,1,0:T(8,128)}, u32[]{:S(2)}) copy-start(f32[2,32,64,128]{3,2,1,0:T(8,128)} %copy-done.3) | copy-start | bytes 6291460
Sparse Core Ops, SparseCore 0:
  88.2 125.1 all-gather.2
where the time goes:
time: 279 us; the launch traced here: 278 us
  waiting for transfers between devices  125 us (45%)
  blocking collectives  80.8 us (29%)
  local copies, waits for them, and re-layouts  22.3 us (8%)
  matrix products  15.2 us (5%)
  other arithmetic  15 us (5%)
  between operations  14.4 us (5%)
  starting transfers between devices  5.43 us (2%)
    all_gather x1, waiting for transfers between devices, gathered_tips(): every = lax.all_gather(tips, GX, axis=0, tiled=True)  125 us
    psum x10, blocking collectives, by_axis(): return functools.reduce(lax.psum, axes, x)  80.8 us
    reduce_sum x1, other arithmetic, shards(): sum_square = jnp.sum(orbitals * orbitals, axis=(1, 2, 3))  6.79 us
    unnamed x16, local copies, waits for them, and re-layouts  5.97 us
  transfers between devices with their start and end apart: 5, of which 1 were waited for; matrix products, arithmetic and copies ran while one was open for 4% of the time, Pallas kernels for 0%

commit v1 on v0

v1 whole, which is shorter than its diff:
```python
import jax
import jax.numpy as jnp
from jax import lax
from jax.experimental import pallas as pl
from jax.experimental.pallas import tpu as pltpu
from jax.sharding import Mesh
from jax.sharding import PartitionSpec as P

GX = ("gx_0", "gx_1", "gx_2", "gx_3")
ALL = ("gx_0", "gx_1", "gx_2", "gx_3", "gy")

TAU = 4.0
EPS = 1e-06
COUPLING_FIRST = 0.06
COUPLING_SECOND = 0.05
COUPLING_CROSS = 0.04
HIGHEST = lax.Precision.HIGHEST

COMPS = 2
NZ = 32
NX = 64
NY = 128
LINES = COMPS * NZ
BLOCKS = 4
WIDE = NY // BLOCKS

VMEM = pl.BlockSpec(memory_space=pltpu.VMEM)
SMEM = pl.BlockSpec(memory_space=pltpu.SMEM)


def lane_of(shape):
    return lax.broadcasted_iota(jnp.int32, shape, 1)


def row_of(shape):
    return lax.broadcasted_iota(jnp.int32, shape, 0)


def plane(ref, comp, x):
    return ref[pl.ds(comp * NZ * NX + x, NZ, stride=NX), :]


def rows(x, comp):
    return pl.ds(pl.multiple_of(x * LINES + comp * NZ, NZ), NZ)


def extract_kernel(o_ref, edge_ref, first_ref, last_ref):
    lane = lane_of((NZ, NY))
    for comp in range(COMPS):
        def step(x, packed):
            rolled = pltpu.roll(plane(o_ref, comp, x), 2 * x + 1, 1)
            return jnp.where(lane // 2 == x, rolled, packed)

        packed = lax.fori_loop(0, NX, step, jnp.zeros((NZ, NY), jnp.float32), unroll=8)
        edge_ref[comp * NZ : (comp + 1) * NZ, :] = packed
        first_ref[comp * NZ : (comp + 1) * NZ, :] = plane(o_ref, comp, 0)
        last_ref[comp * NZ : (comp + 1) * NZ, :] = plane(o_ref, comp, NX - 1)


def sweep_kernel(rate_ref, gain_ref, sigma_ref, o_ref, v_ref, p_ref, q_ref, tips_ref, sums_ref, a_scr, fo_scr, fa_scr, tab_scr):
    rate = rate_ref[0]
    gain4 = TAU * gain_ref[0]
    keep = 1.0 - TAU * sigma_ref[0]
    decay = jnp.exp(jnp.full((NZ, NY), -rate, jnp.float32))
    index = row_of((NX, NY)).astype(jnp.float32)
    tab_scr[0] = jnp.exp(-rate * (index + 1.0))
    tab_scr[1] = jnp.exp(-rate * (float(NX) - index))
    zero = jnp.zeros((NZ, NY), jnp.float32)

    def ahead(x, carry):
        prev, fo, fa, cross, square = carry
        o = [plane(o_ref, c, x) for c in range(COMPS)]
        s0, s1 = o[0] * o[0], o[1] * o[1]
        base = v_ref[pl.ds(x, NZ, stride=NX), :] + 2.0
        density = [
            COUPLING_FIRST * s0 + COUPLING_CROSS * s1,
            COUPLING_CROSS * s0 + COUPLING_SECOND * s1,
        ]
        new_fo, new_fa, new_cross = [], [], []
        for c in range(COMPS):
            around = pltpu.roll(o[c], 1, 0) + pltpu.roll(o[c], NZ - 1, 0)
            left = jnp.where(lane == 0, 0.0, pltpu.roll(o[c], 1, 1))
            right = jnp.where(lane == NY - 1, 0.0, pltpu.roll(o[c], NY - 1, 1))
            a = (base + density[c]) * o[c] - 0.5 * (around + (left + right))
            new_cross.append(cross[c] + o[c] * ((a + o[c]) - prev[c]))
            f_o = decay * fo[c] + o[c]
            f_a = decay * fa[c] + a
            a_scr[rows(x, c), :] = a
            fo_scr[rows(x, c), :] = f_o
            fa_scr[rows(x, c), :] = f_a
            new_fo.append(f_o)
            new_fa.append(f_a)
        return (o, new_fo, new_fa, new_cross, [square[0] + s0, square[1] + s1])

    lane = lane_of((NZ, NY))
    two = [zero, zero]
    _, fo, fa, cross, square = lax.fori_loop(0, NX, ahead, (two, two, two, two, two), unroll=2)
    for c in range(COMPS):
        tips_ref[0, c * NZ : (c + 1) * NZ, :] = fo[c]
        tips_ref[2, c * NZ : (c + 1) * NZ, :] = fa[c]
        sums_ref[c : c + 1, :] = jnp.sum(cross[c], axis=0, keepdims=True)
        sums_ref[COMPS + c : COMPS + c + 1, :] = jnp.sum(square[c], axis=0, keepdims=True)

    for c in range(COMPS):
        def behind(k, carry):
            x = NX - 1 - k
            bo, ba, rq, sq, rp, sp = carry
            o, a = plane(o_ref, c, x), a_scr[rows(x, c), :]
            do, da = decay * bo, decay * ba
            q = gain4 * (fo_scr[rows(x, c), :] + do)
            p = keep * o - gain4 * (fa_scr[rows(x, c), :] + da)
            q_ref[rows(x, c), :] = q
            p_ref[rows(x, c), :] = p
            rise = tab_scr[0, pl.ds(x, 1), :]
            fall = tab_scr[1, pl.ds(x, 1), :]
            return (do + o, da + a, rq + rise * q, sq + fall * q, rp + rise * p, sp + fall * p)

        bo, ba, rq, sq, rp, sp = lax.fori_loop(0, NX, behind, (zero,) * 6, unroll=4)
        block = slice(c * NZ, (c + 1) * NZ)
        tips_ref[1, block, :] = bo
        tips_ref[3, block, :] = ba
        tips_ref[4, block, :] = rq
        tips_ref[5, block, :] = sq
        tips_ref[6, block, :] = rp
        tips_ref[7, block, :] = sp


def pair_matrix(weight, source):
    shape = (NY, NY)
    lane, parity = lane_of(shape), row_of(shape) % 2
    hit = ((lane == 0) & (parity == 0)) | ((lane == NY - 1) & (parity == 1))
    return jnp.where(hit, weight, 0.0)


def dot(a, b):
    return jnp.dot(a, b, precision=HIGHEST, preferred_element_type=jnp.float32)


def pack_kernel(rate_ref, gain_ref, tips_ref, sums_ref, edge_ref, halo_ref, first_ref, before_ref, msg_ref, edge_q_ref):
    rate = rate_ref[0]
    gain4 = TAU * gain_ref[0]
    halo = halo_ref[...]
    shape = (NY, NY)
    place = (row_of(shape) // 2).astype(jnp.float32)
    target = (lane_of(shape) // 2).astype(jnp.float32)
    near = jnp.exp(-rate * jnp.abs(place - target))
    swap = (row_of(shape) % 2) != (lane_of(shape) % 2)
    edge_q = gain4 * dot(halo, jnp.where(swap, near, 0.0))
    edge_q_ref[...] = edge_q
    rise = jnp.exp(-rate * (place + 1.0))
    fall = jnp.exp(-rate * (float(NX) - place))
    tip_f = jnp.exp(-rate * (float(NX - 1) - place))
    tip_b = jnp.exp(-rate * place)
    same = ((row_of(shape) % 2) == 1) & (lane_of(shape) == 0)
    same = same | (((row_of(shape) % 2) == 0) & (lane_of(shape) == NY - 1))
    tips = [tips_ref[k] for k in range(8)]
    tips[2] = tips[2] - 0.5 * dot(halo, pair_matrix(tip_f, None))
    tips[3] = tips[3] - 0.5 * dot(halo, pair_matrix(tip_b, None))
    tips[6] = tips[6] + 0.5 * dot(edge_q, jnp.where(same, rise, 0.0))
    tips[7] = tips[7] + 0.5 * dot(edge_q, jnp.where(same, fall, 0.0))

    lane = lane_of((LINES, NY))
    even = lane % 2 == 0
    swapped = jnp.where(even, pltpu.roll(halo, NY - 1, 1), pltpu.roll(halo, 1, 1))
    extra = -0.5 * (edge_ref[...] * swapped) - first_ref[...] * before_ref[...]
    row_lane = lane_of((1, NY))
    scalars = jnp.zeros((1, NY), jnp.float32)
    for c in range(COMPS):
        cross = sums_ref[c : c + 1, :] + jnp.sum(extra[c * NZ : (c + 1) * NZ, :], axis=0, keepdims=True)
        scalars = jnp.where(row_lane == c, jnp.sum(cross, axis=1, keepdims=True), scalars)
        square = jnp.sum(sums_ref[COMPS + c : COMPS + c + 1, :], axis=1, keepdims=True)
        scalars = jnp.where(row_lane == COMPS + c, square, scalars)
    everyone = jnp.broadcast_to(scalars, (LINES, NY))

    slot = lane // WIDE
    for j in range(BLOCKS):
        for g in range(2):
            line = None
            for k in range(4):
                shift = (WIDE * (k - j)) % NY
                piece = tips[4 * g + k]
                piece = pltpu.roll(piece, shift, 1) if shift else piece
                line = piece if line is None else jnp.where(slot == k, piece, line)
            msg_ref[pl.ds(3 * LINES * j + g, LINES, stride=3), :] = line
        msg_ref[pl.ds(3 * LINES * j + 2, LINES, stride=3), :] = everyone


def pick(vector, k):
    return jnp.sum(jnp.where(lane_of((1, NY)) == k, vector, 0.0), axis=1, keepdims=True)


def owner_kernel(groups, cells, me_ref, rate_ref, gain_ref, sigma_ref, got_ref, edge_q_ref, p_ref, q_ref, w_ref, back_ref, mass_ref):
    rate, gain, sigma = rate_ref[0], gain_ref[0], sigma_ref[0]
    devices = 2 * groups
    total = jnp.sum(got_ref[pl.ds(2, devices, stride=3), :], axis=0, keepdims=True)
    shifts = []
    lane1 = lane_of((1, NY))
    mass = jnp.zeros((1, NY), jnp.float32)
    for c in range(COMPS):
        mean_square = pick(total, COMPS + c) / cells
        energy = (pick(total, c) / cells) / (mean_square + EPS)
        shifts.append(energy + sigma)
        mass = jnp.where(lane1 == c, mean_square, mass)
    mass_ref[...] = jnp.broadcast_to(mass, (8, NY))

    lane = lane_of((NZ, NY))
    ends = (lane == 0) | (lane == NY - 1)
    own = []
    for c in range(COMPS):
        half = 0.5 * edge_q_ref[c * NZ : (c + 1) * NZ, :]
        shift = jnp.broadcast_to(shifts[c], (NZ, NY))

        def step(x, acc):
            edge = jnp.where(ends, pltpu.roll(half, NY - (2 * x + 1), 1), 0.0)
            w = (p_ref[rows(x, c), :] + edge) + shift * q_ref[rows(x, c), :]
            w_ref[rows(x, c), :] = w
            return acc + w * w

        acc = lax.fori_loop(0, NX, step, jnp.zeros((NZ, NY), jnp.float32), unroll=8)
        own.append(jnp.sum(jnp.sum(acc, axis=0, keepdims=True), axis=1, keepdims=True))

    comp = (me_ref[0] % LINES) // NZ
    shift = jnp.where(comp == 0, shifts[0], shifts[1])
    shape = (groups, groups)
    here, other = row_of(shape), lane_of(shape)
    block_rate = rate * float(NX)
    wrap = 1.0 - jnp.exp(jnp.full(shape, -rate * float(NX * groups), jnp.float32))
    ahead = lax.rem(here - other + (groups - 1), groups).astype(jnp.float32)
    behind = lax.rem(other - here + (groups - 1), groups).astype(jnp.float32)
    weight_f = jnp.exp(-block_rate * ahead) / wrap
    weight_b = jnp.exp(-block_rate * behind) / wrap
    wide = lane_of((groups, NY))
    upper = wide >= 2 * WIDE
    powers = jnp.exp(-2.0 * rate * (lane1 + 1).astype(jnp.float32))
    rho = jnp.sum(jnp.where(lane1 < NX, powers, 0.0), axis=1, keepdims=True)
    omega = float(NX) * jnp.exp(jnp.full((1, 1), -rate * float(NX + 1), jnp.float32))
    gain4 = TAU * gain
    part = jnp.zeros((groups, NY), jnp.float32)
    combined = []
    for y in range(2):
        tips = got_ref[pl.ds(3 * y, groups, stride=6), :]
        moments = got_ref[pl.ds(3 * y + 1, groups, stride=6), :]
        carry = jnp.where((wide // WIDE) % 2 == 0, dot(weight_f, tips), dot(weight_b, tips))
        carry = gain4 * (carry - shift * pltpu.roll(carry, 2 * WIDE, 1))
        moments = moments + shift * pltpu.roll(moments, 2 * WIDE, 1)
        mixed = jnp.where((wide // WIDE) % 2 == 0, pltpu.roll(carry, NY - WIDE, 1), pltpu.roll(carry, WIDE, 1))
        term = carry * (rho * carry + omega * mixed - 2.0 * moments)
        part = part + jnp.where(upper, term, 0.0)
        combined.append(carry)
    joined = jnp.sum(jnp.sum(part, axis=0, keepdims=True), axis=1, keepdims=True)
    scalars = jnp.zeros((1, NY), jnp.float32)
    for c in range(COMPS):
        value = own[c] + jnp.where(comp == c, joined, 0.0)
        scalars = jnp.where(lane1 == c, value, scalars)
    for y in range(2):
        back_ref[pl.ds(y, groups, stride=2), :] = jnp.where(upper, combined[y], scalars)


def finish_kernel(cells, rate_ref, got_ref, mass_ref, w_ref, out_ref, tab_scr):
    rate = rate_ref[0]
    index = row_of((NX, NY)).astype(jnp.float32)
    tab_scr[0] = jnp.exp(-rate * (index + 1.0))
    tab_scr[1] = jnp.exp(-rate * (float(NX) - index))
    total = jnp.sum(got_ref[...], axis=0, keepdims=True)
    slot = lane_of((NZ, NY)) // WIDE
    for c in range(COMPS):
        mean_square = pick(mass_ref[0:1, :], c)
        ratio = jnp.sqrt(mean_square / (pick(total, c) / cells + EPS))
        ratio = jnp.broadcast_to(ratio, (NZ, NY))
        forward = jnp.zeros((NZ, NY), jnp.float32)
        backward = jnp.zeros((NZ, NY), jnp.float32)
        for j in range(BLOCKS):
            piece = got_ref[j * LINES + c * NZ : j * LINES + (c + 1) * NZ, :]
            forward = jnp.where(slot == j, pltpu.roll(piece, (WIDE * (j - 2)) % NY, 1) if j != 2 else piece, forward)
            backward = jnp.where(slot == j, pltpu.roll(piece, (WIDE * (j - 3)) % NY, 1) if j != 3 else piece, backward)
        forward = ratio * forward
        backward = ratio * backward

        def step(x, _):
            rise = tab_scr[0, pl.ds(x, 1), :]
            fall = tab_scr[1, pl.ds(x, 1), :]
            value = ratio * w_ref[rows(x, c), :] - (rise * forward + fall * backward)
            out_ref[pl.ds(c * NZ * NX + x, NZ, stride=NX), :] = value
            return 0

        lax.fori_loop(0, NX, step, 0, unroll=8)


def f32(*shape):
    return jax.ShapeDtypeStruct(shape, jnp.float32)


def shards(orbitals, potential, shift_ratio):
    groups = lax.axis_size(GX)
    devices = lax.axis_size(ALL)
    cells = float(NZ * NX * NY * devices)
    line_cells = NX * groups
    sigma = shift_ratio / float(line_cells * line_cells)
    rate = jnp.log1p(sigma + jnp.sqrt(sigma * (sigma + 2.0)))
    gain = jnp.sqrt(sigma / (sigma + 2.0))
    me = lax.axis_index(ALL).astype(jnp.int32).reshape(1)
    o = orbitals.reshape(LINES * NX, NY)
    v = potential.reshape(NZ * NX, NY)
    cells_all = LINES * NX

    edge, first, last = pl.pallas_call(
        extract_kernel,
        out_shape=(f32(LINES, NY),) * 3,
        in_specs=[VMEM],
        out_specs=(VMEM,) * 3,
        name="extract",
    )(o)
    halo = lax.ppermute(edge, "gy", [(0, 1), (1, 0)])
    before = lax.ppermute(last, GX, [(i, (i + 1) % groups) for i in range(groups)])

    big = pltpu.VMEM((cells_all, NY), jnp.float32)
    p, q, tips, sums = pl.pallas_call(
        sweep_kernel,
        out_shape=(f32(cells_all, NY), f32(cells_all, NY), f32(8, LINES, NY), f32(2 * COMPS, NY)),
        in_specs=[SMEM, SMEM, SMEM, VMEM, VMEM],
        out_specs=(VMEM,) * 4,
        scratch_shapes=[big, big, big, pltpu.VMEM((2, NX, NY), jnp.float32)],
        name="sweep",
    )(rate, gain, sigma, o, v)

    msg, edge_q = pl.pallas_call(
        pack_kernel,
        out_shape=(f32(3 * devices, NY), f32(LINES, NY)),
        in_specs=[SMEM, SMEM] + [VMEM] * 6,
        out_specs=(VMEM,) * 2,
        name="pack",
    )(rate, gain, tips, sums, edge, halo, first, before)
    got = lax.all_to_all(msg.reshape(devices, 1, 3 * NY), ALL, 0, 0, tiled=True).reshape(3 * devices, NY)

    w, back, mass = pl.pallas_call(
        lambda *refs: owner_kernel(groups, cells, *refs),
        out_shape=(f32(cells_all, NY), f32(devices, NY), f32(8, NY)),
        in_specs=[SMEM] * 4 + [VMEM] * 4,
        out_specs=(VMEM,) * 3,
        name="owner",
    )(me, rate, gain, sigma, got, edge_q, p, q)
    returned = lax.all_to_all(back.reshape(devices, 1, NY), ALL, 0, 0, tiled=True).reshape(devices, NY)

    out = pl.pallas_call(
        lambda *refs: finish_kernel(cells, *refs),
        out_shape=f32(cells_all, NY),
        in_specs=[SMEM] + [VMEM] * 3,
        out_specs=VMEM,
        scratch_shapes=[pltpu.VMEM((2, NX, NY), jnp.float32)],
        name="finish",
    )(rate, returned, mass, w)
    return out.reshape(orbitals.shape)


def solution(mesh):
    split = Mesh(mesh.devices.reshape(2, 4, 8, 2, mesh.shape["gy"]), ALL)
    return jax.shard_map(
        shards,
        mesh=split,
        in_specs=(P(None, None, GX, "gy"), P(None, GX, "gy"), P()),
        out_specs=P(None, None, GX, "gy"),
        check_vma=False,
    )
```

time: 279 us -> 87.4 us (0.31)
  waiting for transfers between devices: 125 us -> 17.1 us
  blocking collectives: 80.8 us -> 21.2 us
  Pallas kernels: 0 us -> 29.3 us
  local copies, waits for them, and re-layouts: 22.3 us -> 1.36 us
  matrix products: 15.2 us -> 0 us
  other arithmetic: 15 us -> 0 us
  between operations: 14.4 us -> 0.87 us
  starting transfers between devices: 5.43 us -> 17.4 us
    all_gather x1 -> x0, waiting for transfers between devices: 125 us -> none  [gathered_tips(): every = lax.all_gather(tips, GX, axis=0, tiled=True)]
    psum x10 -> x0, blocking collectives: 80.8 us -> none  [by_axis(): return functools.reduce(lax.psum, axes, x)]
    pallas_call x0 -> x5, Pallas kernels: none -> 29.3 us  [the longest x1 11.6 us: shards(): pl.pallas_call(sweep_kernel, out_shape=(f32(cells_all, NY), f32(cells_all...]
    all_to_all x0 -> x1, blocking collectives: none -> 21.2 us  [shards(): lax.all_to_all(back.reshape(devices, 1, NY), ALL, 0, 0, tiled=True)]
    all_to_all x0 -> x1, waiting for transfers between devices: none -> 17.1 us  [shards(): lax.all_to_all(msg.reshape(devices, 1, 3 * NY), ALL, 0, 0, tiled=True)]
    dot_general x4 -> x0, matrix products: 15.2 us -> none  [the longest x1 4.57 us: gathered_tips(): jnp.einsum('k,kazy->azy', ahead[0], every[:, 0], precision=lax.Precision....]
    all_to_all x0 -> x1, starting transfers between devices: none -> 13.1 us  [shards(): lax.all_to_all(msg.reshape(devices, 1, 3 * NY), ALL, 0, 0, tiled=True)]
    reduce_sum x2 -> x0, other arithmetic: 9.27 us -> none  [the longest x1 6.79 us: shards(): sum_square = jnp.sum(orbitals * orbitals, axis=(1, 2, 3))]
  transfers between devices with their start and end apart: 5 -> 3, of which waited for: 1 -> 1; matrix products, arithmetic and copies ran while one was open for 4% -> 0% of each run, Pallas kernels for 0% -> 13%
where the time goes in v1:
time: 87.4 us; the launch traced here: 87.2 us
  Pallas kernels  29.3 us (34%)
  blocking collectives  21.2 us (24%)
  starting transfers between devices  17.4 us (20%)
  waiting for transfers between devices  17.1 us (20%)
  local copies, waits for them, and re-layouts  1.36 us (2%)
    all_to_all x1, blocking collectives, shards(): lax.all_to_all(back.reshape(devices, 1, NY), ALL, 0, 0, tiled=True)  21.2 us
    all_to_all x1, waiting for transfers between devices, shards(): lax.all_to_all(msg.reshape(devices, 1, 3 * NY), ALL, 0, 0, tiled=True)  17.1 us
    all_to_all x1, starting transfers between devices, shards(): lax.all_to_all(msg.reshape(devices, 1, 3 * NY), ALL, 0, 0, tiled=True)  13.1 us
    pallas_call x1, Pallas kernels, shards(): pl.pallas_call(sweep_kernel, out_shape=(f32(cells_all, NY), f32(cells_all...  11.6 us
    pallas_call x1, Pallas kernels, shards(): pl.pallas_call(lambda *refs: owner_kernel(groups, cells, *refs), out_shap...  5.63 us
    pallas_call x1, Pallas kernels, shards(): pl.pallas_call(lambda *refs: finish_kernel(cells, *refs), out_shape=f32(c...  5.29 us
    pallas_call x1, Pallas kernels, shards(): pl.pallas_call(extract_kernel, out_shape=(f32(LINES, NY),) * 3, in_specs=...  4.56 us
    ppermute x1, starting transfers between devices, shards(): lax.ppermute(last, GX, [(i, (i + 1) % groups) for i in range(groups)])  3.02 us
  transfers between devices with their start and end apart: 3, of which 1 were waited for; matrix products, arithmetic and copies ran while one was open for 0% of the time, Pallas kernels for 13%

profile of v1, /device:TPU:1, one launch (start us, length us, event | category | flops | bytes accessed | tf_op | source)
XLA Modules:
  0.0 87.2 jit_solution(2734010957860654303)
XLA Ops:
  0.0 4.6 %extract.1 = (f32[64,128]{1,0:T(8,128)}, f32[64,128]{1,0:T(8,128)}, f32[64,128]{1,0:T(8,128)}) custom-call(f32[4096,128]{1,0:T(8,128)} %bitcast.10), custom_call_target="tpu_custom_call" | custom-call | tf_op jit(solution)/shard_map/extract/pallas_call | solution.py:306
  4.6 3.0 %collective-permute-start.1 = (f32[64,128]{1,0:T(8,128)}, f32[64,128]{1,0:T(8,128)S(1)}, u32[]{:S(2)}, u32[]{:S(2)}) collective-permute-start(f32[64,128]{1,0:T(8,128)} %get-tuple-element.21), channel_id=1, source_target_pairs={{0,2},{2,4},{4,6},{6,8},{8,10},{10,12},{12,14},{14,16},{16,18},{18... | collective-permute-start | bytes 98312 | tf_op jit(solution)/shard_map/ppermute | solution.py:314
  7.6 1.3 %collective-permute-start = (f32[64,128]{1,0:T(8,128)}, f32[64,128]{1,0:T(8,128)S(1)}, u32[]{:S(2)}, u32[]{:S(2)}) collective-permute-start(f32[64,128]{1,0:T(8,128)} %get-tuple-element.19.edge_ref), channel_id=1, source_target_pairs={{0,1},{1,0},{2,3},{3,2},{4,5},{5,4},{6,7},{7,6},{8,9},{9,8},{10,11... | collective-permute-start | bytes 98312 | tf_op jit(solution)/shard_map/ppermute | solution.py:313
  9.7 11.6 %sweep.1 = (f32[4096,128]{1,0:T(8,128)}, f32[4096,128]{1,0:T(8,128)}, f32[8,64,128]{2,1,0:T(8,128)}, f32[4,128]{1,0:T(4,128)}) custom-call(f32[1]{0:T(128)S(6)} %log1p.3.rate_ref.refs_1_.refs_0_, f32[1]{0:T(128)S(6)} %sqrt.7.gain_ref.refs_2_, f32[1]{0:T(128)S(6)} %div.6.sigma_ref.refs_3_, f32[4096,128]{1,0:T(8,128)} %bitcast.11, f32[2048,128]{1,0:T(8,128)} %bitcast.13), custom_call_target="tpu_custom_call" | custom-call | tf_op jit(solution)/shard_map/sweep/pallas_call | solution.py:317
  21.3 0.0 collective-permute-done.1.before_ref
  21.3 0.0 copy-start.1
  21.3 0.0 collective-permute-done.halo_ref
  21.3 0.0 copy-start.2
  21.3 0.6 copy-done.1
  21.9 0.0 copy-done.2
  21.9 2.3 %pack.1 = (f32[768,128]{1,0:T(8,128)}, f32[64,128]{1,0:T(8,128)}) custom-call(f32[1]{0:T(128)S(6)} %log1p.3.rate_ref.refs_1_.refs_0_, f32[1]{0:T(128)S(6)} %sqrt.7.gain_ref.refs_2_, f32[8,64,128]{2,1,0:T(8,128)} %get-tuple-element.17.tips_ref, f32[4,128]{1,0:T(4,128)} %get-tuple-element.18.sums_ref, f32[64,128]{1,0:T(8,128)} %get-tuple-element.19.edge_ref, ...), custom_call_target="tpu_custom_call" | custom-call | tf_op jit(solution)/shard_map/pack/pallas_call | solution.py:326
  24.2 13.1 %all-to-all-start = ((f32[256,1,384]{2,1,0:T(1,128)}), f32[256,1,384]{2,1,0:T(1,128)S(1)}, u32[]{:S(2)}, u32[]{:S(2)}) async-start(f32[256,1,384]{2,1,0:T(1,128)} %bitcast.15), calls=%async_computation | async-start | bytes 786432 | tf_op jit(solution)/shard_map/all_to_all | solution.py:333
  37.3 17.1 %all-to-all-done = f32[256,1,384]{2,1,0:T(1,128)S(1)} async-done(((f32[256,1,384]{2,1,0:T(1,128)}), f32[256,1,384]{2,1,0:T(1,128)S(1)}, u32[]{:S(2)}, u32[]{:S(2)}) %all-to-all-start) | async-done | bytes 393248 | tf_op jit(solution)/shard_map/all_to_all | solution.py:333
  54.4 0.0 copy-start
  54.4 0.7 copy-done
  55.1 5.6 %owner.1 = (f32[4096,128]{1,0:T(8,128)}, f32[256,128]{1,0:T(8,128)}, f32[8,128]{1,0:T(8,128)}) custom-call(s32[1]{0:T(128)} %bitcast.refs_0_, f32[1]{0:T(128)S(6)} %log1p.3.rate_ref.refs_1_.refs_0_, f32[1]{0:T(128)S(6)} %sqrt.7.gain_ref.refs_2_, f32[1]{0:T(128)S(6)} %div.6.sigma_ref.refs_3_, f32[768,128]{1,0:T(8,128)} %bitcast.12, ...), custom_call_target="tpu_custom_call" | custom-call | tf_op jit(solution)/shard_map/owner/pallas_call | solution.py:335
  60.7 21.2 %all_to_all.10 = f32[256,1,128]{2,1,0:T(1,128)} all-to-all(f32[256,1,128]{2,1,0:T(1,128)} %bitcast.16), channel_id=1, replica_groups=mesh['gx_0'=2,'gx_1'=4,'gx_2'=8,'gx_3'=2,'gy'=2] {'gx_0','gx_1','gx_2','..., dimensions={0} | all-to-all | bytes 262144 | tf_op jit(solution)/shard_map/all_to_all | solution.py:342
  81.9 5.3 %finish.1 = f32[4096,128]{1,0:T(8,128)} custom-call(f32[1]{0:T(128)S(6)} %log1p.3.rate_ref.refs_1_.refs_0_, f32[256,128]{1,0:T(8,128)} %bitcast.14, f32[8,128]{1,0:T(8,128)} %get-tuple-element.27.refs_2_, f32[4096,128]{1,0:T(8,128)} %get-tuple-element.28.refs_3_), custom_call_target="tpu_custom_call" | custom-call | tf_op jit(solution)/shard_map/finish/pallas_call | solution.py:344
Async XLA Ops:
  4.6 16.7 %collective-permute-start.1 = (f32[64,128]{1,0:T(8,128)}, f32[64,128]{1,0:T(8,128)S(1)}, u32[]{:S(2)}, u32[]{:S(2)}) collective-permute-start(f32[64,128]{1,0:T(8,128)} %get-tuple-element.21), channel_id=1, source_target_pairs={{0,2},{2,4},{4,6},{6,8},{8,10},{10,12},{12,14},{14,16},{16,18},{18... | collective-permute-start | bytes 98312 | tf_op jit(solution)/shard_map/ppermute | solution.py:314
  7.6 13.7 %collective-permute-start = (f32[64,128]{1,0:T(8,128)}, f32[64,128]{1,0:T(8,128)S(1)}, u32[]{:S(2)}, u32[]{:S(2)}) collective-permute-start(f32[64,128]{1,0:T(8,128)} %get-tuple-element.19.edge_ref), channel_id=1, source_target_pairs={{0,1},{1,0},{2,3},{3,2},{4,5},{5,4},{6,7},{7,6},{8,9},{9,8},{10,11... | collective-permute-start | bytes 98312 | tf_op jit(solution)/shard_map/ppermute | solution.py:313
  21.3 0.6 copy-start.1
  21.3 0.6 copy-start.2
  24.2 30.2 %all-to-all-start = ((f32[256,1,384]{2,1,0:T(1,128)}), f32[256,1,384]{2,1,0:T(1,128)S(1)}, u32[]{:S(2)}, u32[]{:S(2)}) async-start(f32[256,1,384]{2,1,0:T(1,128)} %bitcast.15), calls=%async_computation | async-start | bytes 786432 | tf_op jit(solution)/shard_map/all_to_all | solution.py:333
  54.4 0.7 copy-start

commit v2 on v1

v2 whole, which is shorter than its diff:
```python
import jax
import jax.numpy as jnp
from jax import lax
from jax.experimental import pallas as pl
from jax.experimental.pallas import tpu as pltpu
from jax.sharding import Mesh
from jax.sharding import PartitionSpec as P

GX = ("gx_0", "gx_1", "gx_2", "gx_3")
ALL = ("gx_0", "gx_1", "gx_2", "gx_3", "gy")

TAU = 4.0
EPS = 1e-06
COUPLING_FIRST = 0.06
COUPLING_SECOND = 0.05
COUPLING_CROSS = 0.04
HIGHEST = lax.Precision.HIGHEST

COMPS = 2
NZ = 32
NX = 64
NY = 128
LINES = COMPS * NZ
BLOCKS = 4
WIDE = NY // BLOCKS
CHUNKS = 8

PARAMS = pltpu.CompilerParams(vmem_limit_bytes=16 << 20)
VMEM = pl.BlockSpec(memory_space=pltpu.VMEM)
HBM = pl.BlockSpec(memory_space=pltpu.HBM)
SMEM = pl.BlockSpec(memory_space=pltpu.SMEM)


def lane_of(shape):
    return lax.broadcasted_iota(jnp.int32, shape, 1)


def row_of(shape):
    return lax.broadcasted_iota(jnp.int32, shape, 0)


def rows(x, comp):
    return pl.ds(pl.multiple_of(x * LINES + comp * NZ, NZ), NZ)


def part(comp):
    return slice(comp * NZ, (comp + 1) * NZ)


def start_lines(source, target, sems):
    size = source.shape[0]

    def copy(x):
        place = pl.ds(pl.multiple_of(x * size, size), size)
        return pltpu.make_async_copy(source.at[:, x, :], target.at[place, :], sems.at[x])

    def start(x, _):
        copy(x).start()
        return 0

    lax.fori_loop(0, NX, start, 0, unroll=8)
    return copy


def load_kernel(o_hbm, o_ref, edge_ref, first_ref, last_ref, sems):
    copy = start_lines(o_hbm, o_ref, sems)
    lane = lane_of((NZ, NY)) // 2

    def step(x, packed):
        copy(x).wait()
        return [
            jnp.where(lane == x, pltpu.roll(o_ref[rows(x, c), :], 2 * x + 1, 1), packed[c])
            for c in range(COMPS)
        ]

    zero = jnp.zeros((NZ, NY), jnp.float32)
    packed = lax.fori_loop(0, NX, step, [zero, zero], unroll=8)
    for c in range(COMPS):
        edge_ref[part(c), :] = packed[c]
    first_ref[...] = o_ref[0:LINES, :]
    last_ref[...] = o_ref[(NX - 1) * LINES : NX * LINES, :]


def tables(rate, count):
    place = (row_of((count * NX, NY)) // count).astype(jnp.float32)
    index = row_of((NX, NY)).astype(jnp.float32)
    rise = jnp.exp(-rate * (index + 1.0))
    fall = jnp.exp(-rate * (float(NX) - index))
    shape = (count * NX, NX)
    gap = (row_of(shape) // count - lane_of(shape)).astype(jnp.float32)
    near = jnp.exp(-rate * jnp.abs(gap))
    return (
        jnp.exp(-rate * (float(NX - 1) - place)),
        jnp.exp(-rate * place),
        dot(near, rise),
        dot(near, fall),
    )


def gather_kernel(rate_ref, gain_ref, sigma_ref, o_ref, v_hbm, a_ref, tips_ref, sums_ref, v_scr, tab_scr, sems):
    copy = start_lines(v_hbm, v_scr, sems)
    rate = rate_ref[0]
    gain4 = TAU * gain_ref[0]
    keep = 1.0 - TAU * sigma_ref[0]
    for k, table in enumerate(tables(rate, 1)):
        tab_scr[k] = table
    zero = jnp.zeros((NZ, NY), jnp.float32)
    decay = jnp.exp(jnp.full((NZ, NY), -rate, jnp.float32))

    def step(x, carry):
        cross, square, sums = carry
        copy(x).wait()
        o = [o_ref[rows(x, c), :] for c in range(COMPS)]
        back = jnp.maximum(x - 1, 0)
        real = jnp.where(x > 0, 1.0, 0.0)
        weights = [tab_scr[k, pl.ds(x, 1), :] for k in range(4)]
        s = [o[0] * o[0], o[1] * o[1]]
        both = COUPLING_CROSS * (s[0] + s[1])
        base = (v_scr[pl.ds(pl.multiple_of(x * NZ, NZ), NZ), :] + 2.0) + both
        own = (COUPLING_FIRST - COUPLING_CROSS, COUPLING_SECOND - COUPLING_CROSS)
        new_cross, new_square, new_sums = [], [], []
        for c in range(COMPS):
            around = pltpu.roll(o[c], 1, 0) + pltpu.roll(o[c], NZ - 1, 0)
            around = around + (pltpu.roll(o[c], 1, 1) + pltpu.roll(o[c], NY - 1, 1))
            a = (base + own[c] * s[c]) * o[c] - 0.5 * around
            a_ref[rows(x, c), :] = a
            prev = real * o_ref[rows(back, c), :]
            new_cross.append(cross[c] + o[c] * ((a + o[c]) - prev))
            new_square.append(square[c] + s[c])
            new_sums.append(
                [decay * sums[c][0] + o[c], decay * sums[c][1] + a]
                + [sums[c][1 + k] + weights[k] * o[c] for k in range(1, 4)]
                + [sums[c][4 + k] + weights[k] * a for k in range(1, 4)]
            )
        return new_cross, new_square, new_sums

    cross, square, sums = lax.fori_loop(
        0, NX, step, ([zero] * 2, [zero] * 2, [[zero] * 8] * 2), unroll=2
    )
    once = jnp.exp(jnp.full((NZ, NY), -rate, jnp.float32))
    for c in range(COMPS):
        f_o, f_a, b_o, r_o, s_o, b_a, r_a, s_a = sums[c]
        tips_ref[0, part(c), :] = f_o
        tips_ref[1, part(c), :] = b_o
        tips_ref[2, part(c), :] = f_a
        tips_ref[3, part(c), :] = b_a
        tips_ref[4, part(c), :] = gain4 * r_o
        tips_ref[5, part(c), :] = gain4 * s_o
        tips_ref[6, part(c), :] = keep * (once * b_o) - gain4 * r_a
        tips_ref[7, part(c), :] = keep * (once * f_o) - gain4 * s_a
        sums_ref[c : c + 1, :] = jnp.sum(cross[c], axis=0, keepdims=True)
        sums_ref[COMPS + c : COMPS + c + 1, :] = jnp.sum(square[c], axis=0, keepdims=True)


def local_shift(sums_ref, c, sigma):
    cross = jnp.sum(sums_ref[c : c + 1, :], axis=1, keepdims=True)
    square = jnp.sum(sums_ref[COMPS + c : COMPS + c + 1, :], axis=1, keepdims=True)
    return cross / (square + EPS) + sigma


def sweep_kernel(rate_ref, gain_ref, sigma_ref, o_hbm, a_ref, edge_ref, halo_ref, sums_ref, p_ref, q_ref, local_ref, o_ref, fo_scr, fa_scr, sems):
    copy = start_lines(o_hbm, o_ref, sems)
    gain4 = TAU * gain_ref[0]
    keep = 1.0 - TAU * sigma_ref[0]
    decay = jnp.exp(jnp.full((NZ, NY), -rate_ref[0], jnp.float32))
    lane = lane_of((NZ, NY))
    zero = jnp.zeros((NZ, NY), jnp.float32)
    lane1 = lane_of((1, NY))
    for c in range(COMPS):
        delta = -0.5 * (halo_ref[part(c), :] - edge_ref[part(c), :])
        even = lane % 2 == 0
        delta = jnp.where(even, pltpu.roll(delta, NY - 1, 1), pltpu.roll(delta, 1, 1))
        ends = (lane == 0) | (lane == NY - 1)

        def ahead(x, carry):
            fo, fa = carry
            if c == 0:
                copy(x).wait()
            o = o_ref[rows(x, c), :]
            a = a_ref[rows(x, c), :] + jnp.where(ends, pltpu.roll(delta, NY - (2 * x + 1), 1), 0.0)
            fo = decay * fo + o
            fa = decay * fa + a
            fo_scr[pl.ds(pl.multiple_of(x * NZ, NZ), NZ), :] = fo
            fa_scr[pl.ds(pl.multiple_of(x * NZ, NZ), NZ), :] = fa
            p_ref[rows(x, c), :] = a
            return fo, fa

        lax.fori_loop(0, NX, ahead, (zero, zero), unroll=4)
        shift = jnp.broadcast_to(local_shift(sums_ref, c, sigma_ref[0]), (NZ, NY))

        def behind(k, carry):
            x = NX - 1 - k
            bo, ba, ww, wq, qq = carry
            o, a = o_ref[rows(x, c), :], p_ref[rows(x, c), :]
            do, da = decay * bo, decay * ba
            q = gain4 * (fo_scr[pl.ds(pl.multiple_of(x * NZ, NZ), NZ), :] + do)
            p = keep * o - gain4 * (fa_scr[pl.ds(pl.multiple_of(x * NZ, NZ), NZ), :] + da)
            q_ref[rows(x, c), :] = q
            p_ref[rows(x, c), :] = p
            w = p + shift * q
            return do + o, da + a, ww + w * w, wq + w * q, qq + q * q

        _, _, ww, wq, qq = lax.fori_loop(0, NX, behind, (zero,) * 5, unroll=4)
        for k, value in enumerate((ww, wq, qq)):
            local_ref[3 * c + k : 3 * c + k + 1, :] = jnp.sum(value, axis=0, keepdims=True)


def dot(a, b):
    return jnp.dot(a, b, precision=HIGHEST, preferred_element_type=jnp.float32)


def pack_kernel(rate_ref, gain_ref, tips_ref, sums_ref, edge_ref, halo_ref, first_ref, before_ref, msg_ref):
    gain4 = TAU * gain_ref[0]
    halo = halo_ref[...]
    delta = -0.5 * (halo - edge_ref[...])
    shape = (NY, NY)
    odd = row_of(shape) % 2
    hit = ((lane_of(shape) == 0) & (odd == 0)) | ((lane_of(shape) == NY - 1) & (odd == 1))
    fixes = [dot(delta, jnp.where(hit, table, 0.0)) for table in tables(rate_ref[0], 2)]
    tips = [tips_ref[k] for k in range(8)]
    tips[2] = tips[2] + fixes[0]
    tips[3] = tips[3] + fixes[1]
    tips[6] = tips[6] - gain4 * fixes[2]
    tips[7] = tips[7] - gain4 * fixes[3]

    lane = lane_of((LINES, NY))
    even = lane % 2 == 0
    swapped = jnp.where(even, pltpu.roll(delta, NY - 1, 1), pltpu.roll(delta, 1, 1))
    extra = edge_ref[...] * swapped - first_ref[...] * before_ref[...]
    row_lane = lane_of((1, NY))
    scalars = jnp.zeros((1, NY), jnp.float32)
    for c in range(COMPS):
        cross = sums_ref[c : c + 1, :] + jnp.sum(extra[c * NZ : (c + 1) * NZ, :], axis=0, keepdims=True)
        scalars = jnp.where(row_lane == c, jnp.sum(cross, axis=1, keepdims=True), scalars)
        square = jnp.sum(sums_ref[COMPS + c : COMPS + c + 1, :], axis=1, keepdims=True)
        scalars = jnp.where(row_lane == COMPS + c, square, scalars)
    everyone = jnp.broadcast_to(scalars, (LINES, NY))

    slot = lane // WIDE
    for j in range(BLOCKS):
        for g in range(2):
            line = None
            for k in range(4):
                shift = (WIDE * (k - j)) % NY
                piece = tips[4 * g + k]
                piece = pltpu.roll(piece, shift, 1) if shift else piece
                line = piece if line is None else jnp.where(slot == k, piece, line)
            msg_ref[pl.ds(3 * LINES * j + g, LINES, stride=3), :] = line
        msg_ref[pl.ds(3 * LINES * j + 2, LINES, stride=3), :] = everyone


def pick(vector, k):
    return jnp.sum(jnp.where(lane_of((1, NY)) == k, vector, 0.0), axis=1, keepdims=True)


def owner_kernel(groups, cells, me_ref, rate_ref, gain_ref, sigma_ref, got_ref, sums_ref, local_ref, back_ref, mass_ref):
    rate, gain, sigma = rate_ref[0], gain_ref[0], sigma_ref[0]
    devices = 2 * groups
    total = jnp.sum(got_ref[pl.ds(2, devices, stride=3), :], axis=0, keepdims=True)
    shifts, own = [], []
    lane1 = lane_of((1, NY))
    mass = jnp.zeros((1, NY), jnp.float32)
    for c in range(COMPS):
        mean_square = pick(total, COMPS + c) / cells
        energy = (pick(total, c) / cells) / (mean_square + EPS)
        shift = energy + sigma
        shifts.append(shift)
        mass = jnp.where(lane1 == c, mean_square, mass)
        mass = jnp.where(lane1 == COMPS + c, shift, mass)
        ww, wq, qq = [
            jnp.sum(local_ref[3 * c + k : 3 * c + k + 1, :], axis=1, keepdims=True) for k in range(3)
        ]
        more = shift - local_shift(sums_ref, c, sigma)
        own.append(ww + more * (2.0 * wq + more * qq))
    mass_ref[...] = jnp.broadcast_to(mass, (8, NY))

    comp = (me_ref[0] % LINES) // NZ
    shift = jnp.where(comp == 0, shifts[0], shifts[1])
    shape = (groups, groups)
    here, other = row_of(shape), lane_of(shape)
    block_rate = rate * float(NX)
    wrap = 1.0 - jnp.exp(jnp.full(shape, -rate * float(NX * groups), jnp.float32))
    ahead = lax.rem(here - other + (groups - 1), groups).astype(jnp.float32)
    behind = lax.rem(other - here + (groups - 1), groups).astype(jnp.float32)
    weight_f = jnp.exp(-block_rate * ahead) / wrap
    weight_b = jnp.exp(-block_rate * behind) / wrap
    wide = lane_of((groups, NY))
    upper = wide >= 2 * WIDE
    powers = jnp.exp(-2.0 * rate * (lane1 + 1).astype(jnp.float32))
    rho = jnp.sum(jnp.where(lane1 < NX, powers, 0.0), axis=1, keepdims=True)
    omega = float(NX) * jnp.exp(jnp.full((1, 1), -rate * float(NX + 1), jnp.float32))
    gain4 = TAU * gain
    joined = jnp.zeros((groups, NY), jnp.float32)
    combined = []
    for y in range(2):
        tips = got_ref[pl.ds(3 * y, groups, stride=6), :]
        moments = got_ref[pl.ds(3 * y + 1, groups, stride=6), :]
        carry = jnp.where((wide // WIDE) % 2 == 0, dot(weight_f, tips), dot(weight_b, tips))
        carry = gain4 * (carry - shift * pltpu.roll(carry, 2 * WIDE, 1))
        moments = moments + shift * pltpu.roll(moments, 2 * WIDE, 1)
        mixed = jnp.where((wide // WIDE) % 2 == 0, pltpu.roll(carry, NY - WIDE, 1), pltpu.roll(carry, WIDE, 1))
        term = carry * (rho * carry + omega * mixed - 2.0 * moments)
        joined = joined + jnp.where(upper, term, 0.0)
        combined.append(carry)
    joined = jnp.sum(jnp.sum(joined, axis=0, keepdims=True), axis=1, keepdims=True)
    scalars = jnp.zeros((1, NY), jnp.float32)
    for c in range(COMPS):
        value = own[c] + jnp.where(comp == c, joined, 0.0)
        scalars = jnp.where(lane1 == c, value, scalars)
    for y in range(2):
        back_ref[pl.ds(y, groups, stride=2), :] = jnp.where(upper, combined[y], scalars)


def finish_kernel(cells, rate_ref, got_ref, mass_ref, p_hbm, q_hbm, out_hbm, p_ref, q_ref, out_scr, tab_scr, sems, in_sems):
    def copy(x):
        source = out_scr.at[pl.ds(pl.multiple_of(x * LINES, LINES), LINES), :]
        return pltpu.make_async_copy(source, out_hbm.at[:, x, :], sems.at[x])

    size = NX * LINES // CHUNKS

    def fetch(k):
        block = pl.ds(pl.multiple_of(k * size, size), size)
        return (
            pltpu.make_async_copy(p_hbm.at[block, :], p_ref.at[block, :], in_sems.at[0, k]),
            pltpu.make_async_copy(q_hbm.at[block, :], q_ref.at[block, :], in_sems.at[1, k]),
        )

    for k in range(CHUNKS):
        for one in fetch(k):
            one.start()
    rate = rate_ref[0]
    index = row_of((NX, NY)).astype(jnp.float32)
    tab_scr[0] = jnp.exp(-rate * (index + 1.0))
    tab_scr[1] = jnp.exp(-rate * (float(NX) - index))
    total = jnp.sum(got_ref[...], axis=0, keepdims=True)
    slot = lane_of((NZ, NY)) // WIDE
    terms = []
    for c in range(COMPS):
        mean_square = pick(mass_ref[0:1, :], c)
        ratio = jnp.sqrt(mean_square / (pick(total, c) / cells + EPS))
        lifted = jnp.broadcast_to(ratio * pick(mass_ref[0:1, :], COMPS + c), (NZ, NY))
        ratio = jnp.broadcast_to(ratio, (NZ, NY))
        forward = jnp.zeros((NZ, NY), jnp.float32)
        backward = jnp.zeros((NZ, NY), jnp.float32)
        for j in range(BLOCKS):
            piece = got_ref[j * LINES + c * NZ : j * LINES + (c + 1) * NZ, :]
            forward = jnp.where(slot == j, pltpu.roll(piece, (WIDE * (j - 2)) % NY, 1) if j != 2 else piece, forward)
            backward = jnp.where(slot == j, pltpu.roll(piece, (WIDE * (j - 3)) % NY, 1) if j != 3 else piece, backward)
        terms.append((ratio, lifted, ratio * forward, ratio * backward))

    def step(x, _):
        rise = tab_scr[0, pl.ds(x, 1), :]
        fall = tab_scr[1, pl.ds(x, 1), :]
        for c in range(COMPS):
            ratio, lifted, forward, backward = terms[c]
            value = ratio * p_ref[rows(x, c), :] + lifted * q_ref[rows(x, c), :]
            out_scr[rows(x, c), :] = value - (rise * forward + fall * backward)
        copy(x).start()
        return 0

    def drain(x, _):
        copy(x).wait()
        return 0

    def chunk(k, _):
        for one in fetch(k):
            one.wait()
        return lax.fori_loop(0, NX // CHUNKS, lambda i, z: step(k * (NX // CHUNKS) + i, z), 0, unroll=True)

    lax.fori_loop(0, CHUNKS, chunk, 0)
    lax.fori_loop(0, NX, drain, 0, unroll=8)


def far(x):
    return pltpu.with_memory_space_constraint(x, pltpu.HBM)


def near(x):
    return pltpu.with_memory_space_constraint(x, pltpu.VMEM)


def f32(*shape):
    return jax.ShapeDtypeStruct(shape, jnp.float32)


def shards(orbitals, potential, shift_ratio):
    groups = lax.axis_size(GX)
    devices = lax.axis_size(ALL)
    cells = float(NZ * NX * NY * devices)
    line_cells = NX * groups
    sigma = shift_ratio / float(line_cells * line_cells)
    rate = jnp.log1p(sigma + jnp.sqrt(sigma * (sigma + 2.0)))
    gain = jnp.sqrt(sigma / (sigma + 2.0))
    me = lax.axis_index(ALL).astype(jnp.int32).reshape(1)
    o = far(orbitals.reshape(LINES, NX, NY))
    cells_all = LINES * NX
    big = pltpu.VMEM((cells_all, NY), jnp.float32)
    row = pltpu.VMEM((LINES, NY), jnp.float32)
    small = pltpu.VMEM((8, NY), jnp.float32)
    queue = pltpu.SemaphoreType.DMA((NX,))

    o_near, edge, first, last = pl.pallas_call(
        load_kernel,
        out_shape=(big, row, row, row),
        in_specs=[HBM],
        out_specs=(VMEM,) * 4,
        scratch_shapes=[queue],
        name="load",
        compiler_params=PARAMS,
    )(o)
    halo = near(lax.ppermute(edge, "gy", [(0, 1), (1, 0)]))
    before = near(lax.ppermute(last, GX, [(i, (i + 1) % groups) for i in range(groups)]))
    o_near, edge, first = near(o_near), near(edge), near(first)

    a, tips, sums = pl.pallas_call(
        gather_kernel,
        out_shape=(big, pltpu.VMEM((8, LINES, NY), jnp.float32), small),
        in_specs=[SMEM, SMEM, SMEM, VMEM, HBM],
        out_specs=(VMEM,) * 3,
        scratch_shapes=[
            pltpu.VMEM((NX * NZ, NY), jnp.float32),
            pltpu.VMEM((4, NX, NY), jnp.float32),
            queue,
        ],
        name="gather",
        compiler_params=PARAMS,
    )(rate, gain, sigma, o_near, far(potential))
    a, tips, sums = near(a), near(tips), near(sums)

    msg = pl.pallas_call(
        pack_kernel,
        out_shape=pltpu.VMEM((3 * devices, NY), jnp.float32),
        in_specs=[SMEM, SMEM] + [VMEM] * 6,
        out_specs=VMEM,
        name="pack",
        compiler_params=PARAMS,
    )(rate, gain, tips, sums, edge, halo, first, before)
    got = lax.all_to_all(msg.reshape(devices, 1, 3 * NY), ALL, 0, 0, tiled=True).reshape(3 * devices, NY)

    p, q, local = pl.pallas_call(
        sweep_kernel,
        out_shape=(big, big, small),
        in_specs=[SMEM] * 3 + [HBM] + [VMEM] * 4,
        out_specs=(VMEM,) * 3,
        scratch_shapes=[big] + [pltpu.VMEM((NX * NZ, NY), jnp.float32)] * 2 + [queue],
        name="sweep",
        compiler_params=PARAMS,
    )(rate, gain, sigma, o, a, edge, halo, sums)
    local = near(local)

    back, mass = pl.pallas_call(
        lambda *refs: owner_kernel(groups, cells, *refs),
        out_shape=(pltpu.VMEM((devices, NY), jnp.float32), small),
        in_specs=[SMEM] * 4 + [VMEM] * 3,
        out_specs=(VMEM,) * 2,
        name="owner",
        compiler_params=PARAMS,
    )(me, rate, gain, sigma, near(got), sums, local)
    returned = lax.all_to_all(back.reshape(devices, 1, NY), ALL, 0, 0, tiled=True).reshape(devices, NY)

    out = pl.pallas_call(
        lambda *refs: finish_kernel(cells, *refs),
        out_shape=f32(LINES, NX, NY),
        in_specs=[SMEM, VMEM, VMEM, HBM, HBM],
        out_specs=HBM,
        scratch_shapes=[
            big,
            big,
            big,
            pltpu.VMEM((2, NX, NY), jnp.float32),
            queue,
            pltpu.SemaphoreType.DMA((2, CHUNKS)),
        ],
        name="finish",
        compiler_params=PARAMS,
    )(rate, near(returned), near(mass), far(p), far(q))
    return out.reshape(orbitals.shape)


def solution(mesh):
    split = Mesh(mesh.devices.reshape(2, 4, 8, 2, mesh.shape["gy"]), ALL)
    return jax.shard_map(
        shards,
        mesh=split,
        in_specs=(P(None, None, GX, "gy"), P(None, GX, "gy"), P()),
        out_specs=P(None, None, GX, "gy"),
        check_vma=False,
    )
```

time: 87.4 us -> 77.5 us (0.89)
  waiting for transfers between devices: 17.1 us -> 5.3 us
  local copies, waits for them, and re-layouts: 1.36 us -> 2.65 us
    all_to_all x1, waiting for transfers between devices: 17.1 us -> 5.29 us  [shards(): lax.all_to_all(msg.reshape(devices, 1, 3 * NY), ALL, 0, 0, tiled=True)]
    pallas_call x4 -> x5, Pallas kernels: 23.7 us -> 28.9 us  [the longest x1 9.09 us: shards(): pl.pallas_call(sweep_kernel, out_shape=(big, big, small), in_specs=[SMEM]...]
    pallas_call x1, Pallas kernels: 5.63 us -> 0.66 us  [shards(): pl.pallas_call(lambda *refs: owner_kernel(groups, cells, *refs), out_shap...]
    unnamed x6 -> x4, local copies, waits for them, and re-layouts: 1.36 us -> 2.65 us
    ppermute x1, starting transfers between devices: 1.3 us -> 2.2 us  [shards(): halo = near(lax.ppermute(edge, 'gy', [(0, 1), (1, 0)]))]
  transfers between devices with their start and end apart: 3 -> 3, of which waited for: 1 -> 1; matrix products, arithmetic and copies ran while one was open for 0% -> 0% of each run, Pallas kernels for 13% -> 23%
where the time goes in v2:
time: 77.5 us; the launch traced here: 77.1 us
  Pallas kernels  29.6 us (38%)
  blocking collectives  20.9 us (27%)
  starting transfers between devices  17.8 us (23%)
  waiting for transfers between devices  5.3 us (7%)
  local copies, waits for them, and re-layouts  2.65 us (3%)
  between operations  0.9 us (1%)
    all_to_all x1, blocking collectives, shards(): lax.all_to_all(back.reshape(devices, 1, NY), ALL, 0, 0, tiled=True)  20.9 us
    all_to_all x1, starting transfers between devices, shards(): lax.all_to_all(msg.reshape(devices, 1, 3 * NY), ALL, 0, 0, tiled=True)  13.1 us
    pallas_call x1, Pallas kernels, shards(): pl.pallas_call(sweep_kernel, out_shape=(big, big, small), in_specs=[SMEM]...  9.09 us
    pallas_call x1, Pallas kernels, shards(): pl.pallas_call(gather_kernel, out_shape=(big, pltpu.VMEM((8, LINES, NY),...  8.31 us
    pallas_call x1, Pallas kernels, shards(): pl.pallas_call(load_kernel, out_shape=(big, row, row, row), in_specs=[HBM...  6.25 us
    all_to_all x1, waiting for transfers between devices, shards(): lax.all_to_all(msg.reshape(devices, 1, 3 * NY), ALL, 0, 0, tiled=True)  5.29 us
    pallas_call x1, Pallas kernels, shards(): pl.pallas_call(lambda *refs: finish_kernel(cells, *refs), out_shape=f32(L...  3.92 us
    unnamed x4, local copies, waits for them, and re-layouts  2.65 us
  transfers between devices with their start and end apart: 3, of which 1 were waited for; matrix products, arithmetic and copies ran while one was open for 0% of the time, Pallas kernels for 23%

profile of v2, /device:TPU:1, one launch (start us, length us, event | category | flops | bytes accessed | tf_op | source)
XLA Modules:
  0.0 77.1 jit_solution(4484585653357827998)
XLA Ops:
  0.0 6.2 %load.1 = (f32[4096,128]{1,0:T(8,128)S(1)}, f32[64,128]{1,0:T(8,128)S(1)}, f32[64,128]{1,0:T(8,128)S(1)}, f32[64,128]{1,0:T(8,128)S(1)}) custom-call(f32[64,64,128]{2,1,0:T(8,128)} %bitcast.12), custom_call_target="tpu_custom_call" | custom-call | tf_op jit(solution)/shard_map/load/pallas_call | solution.py:402
  6.3 2.2 %collective-permute-start = (f32[64,128]{1,0:T(8,128)S(1)}, f32[64,128]{1,0:T(8,128)S(1)}, u32[]{:S(2)}, u32[]{:S(2)}) collective-permute-start(f32[64,128]{1,0:T(8,128)S(1)} %get-tuple-element.20.edge_ref), channel_id=1, source_target_pairs={{0,1},{1,0},{2,3},{3,2},{4,5},{5,4},{6,7},{7,6},{8,9},{9,8},{10,11... | collective-permute-start | bytes 98312 | tf_op jit(solution)/shard_map/ppermute | solution.py:411
  8.5 2.5 %collective-permute-start.1 = (f32[64,128]{1,0:T(8,128)S(1)}, f32[64,128]{1,0:T(8,128)S(1)}, u32[]{:S(2)}, u32[]{:S(2)}) collective-permute-start(f32[64,128]{1,0:T(8,128)S(1)} %get-tuple-element.22), channel_id=1, source_target_pairs={{0,2},{2,4},{4,6},{6,8},{8,10},{10,12},{12,14},{14,16},{16,18},{18... | collective-permute-start | bytes 98312 | tf_op jit(solution)/shard_map/ppermute | solution.py:412
  11.8 8.3 %gather.1 = (f32[4096,128]{1,0:T(8,128)S(1)}, f32[8,64,128]{2,1,0:T(8,128)S(1)}, f32[8,128]{1,0:T(8,128)S(1)}) custom-call(f32[1]{0:T(128)S(6)} %log1p.3.rate_ref.refs_1_.refs_0_, f32[1]{0:T(128)S(6)} %sqrt.7.gain_ref.refs_2_, f32[1]{0:T(128)S(6)} %div.6.sigma_ref.refs_3_, f32[4096,128]{1,0:T(8,128)S(1)} %get-tuple-element.17.o_ref, f32[32,64,128]{2,1,0:T(8,128)} %v_hbm.1), custom_call_target="tpu_custom_call" | custom-call | tf_op jit(solution)/shard_map/gather/pallas_call | solution.py:415
  20.1 0.0 collective-permute-done.halo_ref
  20.1 0.0 collective-permute-done.1.before_ref
  20.1 1.4 %pack.1 = f32[768,128]{1,0:T(8,128)} custom-call(f32[1]{0:T(128)S(6)} %log1p.3.rate_ref.refs_1_.refs_0_, f32[1]{0:T(128)S(6)} %sqrt.7.gain_ref.refs_2_, f32[8,64,128]{2,1,0:T(8,128)S(1)} %get-tuple-element.18.tips_ref, f32[8,128]{1,0:T(8,128)S(1)} %get-tuple-element.19.sums_ref.refs_5_, f32[64,128]{1,0:T(8,128)S(1)} %get-tuple-element.20.edge_ref, ...), custom_call_target="tpu_custom_call" | custom-call | tf_op jit(solution)/shard_map/pack/pallas_call | solution.py:430
  21.5 13.1 %all-to-all-start = ((f32[256,1,384]{2,1,0:T(1,128)}), f32[256,1,384]{2,1,0:T(1,128)S(1)}, u32[]{:S(2)}, u32[]{:S(2)}) async-start(f32[256,1,384]{2,1,0:T(1,128)} %bitcast.2), calls=%async_computation | async-start | bytes 786432 | tf_op jit(solution)/shard_map/all_to_all | solution.py:438
  34.6 9.1 %sweep.1 = (f32[4096,128]{1,0:T(8,128)S(1)}, f32[4096,128]{1,0:T(8,128)S(1)}, f32[8,128]{1,0:T(8,128)S(1)}) custom-call(f32[1]{0:T(128)S(6)} %log1p.3.rate_ref.refs_1_.refs_0_, f32[1]{0:T(128)S(6)} %sqrt.7.gain_ref.refs_2_, f32[1]{0:T(128)S(6)} %div.6.sigma_ref.refs_3_, f32[64,64,128]{2,1,0:T(8,128)} %bitcast.13, f32[4096,128]{1,0:T(8,128)S(1)} %get-tuple-element.23.a_ref, ...), custom_call_target="tpu_custom_call" | custom-call | tf_op jit(solution)/shard_map/sweep/pallas_call | solution.py:440
  43.7 0.0 copy-start
  43.7 1.3 %copy-done = f32[4096,128]{1,0:T(8,128)} copy-done((f32[4096,128]{1,0:T(8,128)}, f32[4096,128]{1,0:T(8,128)S(1)}, u32[]{:S(2)}) %copy-start) | copy-done | bytes 2097176
  45.0 0.0 copy-start.1
  45.0 1.3 %copy-done.1 = f32[4096,128]{1,0:T(8,128)} copy-done((f32[4096,128]{1,0:T(8,128)}, f32[4096,128]{1,0:T(8,128)S(1)}, u32[]{:S(2)}) %copy-start.1) | copy-done | bytes 2097176
  46.3 5.3 %all-to-all-done = f32[256,1,384]{2,1,0:T(1,128)S(1)} async-done(((f32[256,1,384]{2,1,0:T(1,128)}), f32[256,1,384]{2,1,0:T(1,128)S(1)}, u32[]{:S(2)}, u32[]{:S(2)}) %all-to-all-start) | async-done | bytes 393248 | tf_op jit(solution)/shard_map/all_to_all | solution.py:438
  51.6 0.7 owner.1
  52.3 20.9 %all_to_all.10 = f32[256,1,128]{2,1,0:T(1,128)S(1)} all-to-all(f32[256,1,128]{2,1,0:T(1,128)S(1)} %bitcast.11), channel_id=1, replica_groups=mesh['gx_0'=2,'gx_1'=4,'gx_2'=8,'gx_3'=2,'gy'=2] {'gx_0','gx_1','gx_2','..., dimensions={0} | all-to-all | bytes 262144 | tf_op jit(solution)/shard_map/all_to_all | solution.py:459
  73.2 3.9 %finish.1 = f32[64,64,128]{2,1,0:T(8,128)} custom-call(f32[1]{0:T(128)S(6)} %log1p.3.rate_ref.refs_1_.refs_0_, f32[256,128]{1,0:T(8,128)S(1)} %bitcast.10, f32[8,128]{1,0:T(8,128)S(1)} %get-tuple-element.26.refs_2_, f32[4096,128]{1,0:T(8,128)} %copy-done, f32[4096,128]{1,0:T(8,128)} %copy-done.1), custom_call_target="tpu_custom_call" | custom-call | tf_op jit(solution)/shard_map/finish/pallas_call | solution.py:461
Async XLA Ops:
  6.3 13.8 %collective-permute-start = (f32[64,128]{1,0:T(8,128)S(1)}, f32[64,128]{1,0:T(8,128)S(1)}, u32[]{:S(2)}, u32[]{:S(2)}) collective-permute-start(f32[64,128]{1,0:T(8,128)S(1)} %get-tuple-element.20.edge_ref), channel_id=1, source_target_pairs={{0,1},{1,0},{2,3},{3,2},{4,5},{5,4},{6,7},{7,6},{8,9},{9,8},{10,11... | collective-permute-start | bytes 98312 | tf_op jit(solution)/shard_map/ppermute | solution.py:411
  8.5 11.6 %collective-permute-start.1 = (f32[64,128]{1,0:T(8,128)S(1)}, f32[64,128]{1,0:T(8,128)S(1)}, u32[]{:S(2)}, u32[]{:S(2)}) collective-permute-start(f32[64,128]{1,0:T(8,128)S(1)} %get-tuple-element.22), channel_id=1, source_target_pairs={{0,2},{2,4},{4,6},{6,8},{8,10},{10,12},{12,14},{14,16},{16,18},{18... | collective-permute-start | bytes 98312 | tf_op jit(solution)/shard_map/ppermute | solution.py:412
  21.5 30.1 %all-to-all-start = ((f32[256,1,384]{2,1,0:T(1,128)}), f32[256,1,384]{2,1,0:T(1,128)S(1)}, u32[]{:S(2)}, u32[]{:S(2)}) async-start(f32[256,1,384]{2,1,0:T(1,128)} %bitcast.2), calls=%async_computation | async-start | bytes 786432 | tf_op jit(solution)/shard_map/all_to_all | solution.py:438
  43.7 1.3 %copy-start = (f32[4096,128]{1,0:T(8,128)}, f32[4096,128]{1,0:T(8,128)S(1)}, u32[]{:S(2)}) copy-start(f32[4096,128]{1,0:T(8,128)S(1)} %get-tuple-element.27.refs_3_) | copy-start | bytes 6291460
  45.0 1.3 %copy-start.1 = (f32[4096,128]{1,0:T(8,128)}, f32[4096,128]{1,0:T(8,128)S(1)}, u32[]{:S(2)}) copy-start(f32[4096,128]{1,0:T(8,128)S(1)} %get-tuple-element.28.refs_4_) | copy-start | bytes 6291460

commit v3 on v2

--- a/solution.py
+++ b/solution.py
@@ -23,7 +23,8 @@
 LINES = COMPS * NZ
 BLOCKS = 4
 WIDE = NY // BLOCKS
-CHUNKS = 8
+PITCH = NX + 8
+ROWS = 8
 
 PARAMS = pltpu.CompilerParams(vmem_limit_bytes=16 << 20)
 VMEM = pl.BlockSpec(memory_space=pltpu.VMEM)
@@ -47,38 +48,43 @@
     return slice(comp * NZ, (comp + 1) * NZ)
 
 
-def start_lines(source, target, sems):
-    size = source.shape[0]
-
-    def copy(x):
-        place = pl.ds(pl.multiple_of(x * size, size), size)
-        return pltpu.make_async_copy(source.at[:, x, :], target.at[place, :], sems.at[x])
-
-    def start(x, _):
-        copy(x).start()
+def start_planes(source, target, sems):
+    def copy(k):
+        place = pl.ds(pl.multiple_of(k * PITCH, 8), NX)
+        return pltpu.make_async_copy(source.at[k], target.at[place, :], sems.at[k])
+
+    def start(k, _):
+        copy(k).start()
         return 0
 
-    lax.fori_loop(0, NX, start, 0, unroll=8)
-    return copy
+    lax.fori_loop(0, source.shape[0], start, 0, unroll=8)
+
+    def wait(first, last):
+        def one(k, _):
+            copy(k).wait()
+            return 0
+
+        lax.fori_loop(first, last, one, 0, unroll=8)
+
+    return wait
+
+
+def line_rows(x, comp=0):
+    return pl.ds(comp * NZ * PITCH + x, NZ, stride=PITCH)
 
 
 def load_kernel(o_hbm, o_ref, edge_ref, first_ref, last_ref, sems):
-    copy = start_lines(o_hbm, o_ref, sems)
+    wait = start_planes(o_hbm, o_ref, sems)
     lane = lane_of((NZ, NY)) // 2
-
-    def step(x, packed):
-        copy(x).wait()
-        return [
-            jnp.where(lane == x, pltpu.roll(o_ref[rows(x, c), :], 2 * x + 1, 1), packed[c])
-            for c in range(COMPS)
-        ]
-
-    zero = jnp.zeros((NZ, NY), jnp.float32)
-    packed = lax.fori_loop(0, NX, step, [zero, zero], unroll=8)
-    for c in range(COMPS):
-        edge_ref[part(c), :] = packed[c]
-    first_ref[...] = o_ref[0:LINES, :]
-    last_ref[...] = o_ref[(NX - 1) * LINES : NX * LINES, :]
+    for c in range(COMPS):
+        wait(c * NZ, (c + 1) * NZ)
+
+        def step(x, packed):
+            return jnp.where(lane == x, pltpu.roll(o_ref[line_rows(x, c), :], 2 * x + 1, 1), packed)
+
+        edge_ref[part(c), :] = lax.fori_loop(0, NX, step, jnp.zeros((NZ, NY), jnp.float32), unroll=8)
+        first_ref[part(c), :] = o_ref[line_rows(0, c), :]
+        last_ref[part(c), :] = o_ref[line_rows(NX - 1, c), :]
 
 
 def tables(rate, count):
@@ -98,7 +104,7 @@
 
 
 def gather_kernel(rate_ref, gain_ref, sigma_ref, o_ref, v_hbm, a_ref, tips_ref, sums_ref, v_scr, tab_scr, sems):
-    copy = start_lines(v_hbm, v_scr, sems)
+    wait = start_planes(v_hbm, v_scr, sems)
     rate = rate_ref[0]
     gain4 = TAU * gain_ref[0]
     keep = 1.0 - TAU * sigma_ref[0]
@@ -108,15 +114,12 @@
     decay = jnp.exp(jnp.full((NZ, NY), -rate, jnp.float32))
 
     def step(x, carry):
-        cross, square, sums = carry
-        copy(x).wait()
-        o = [o_ref[rows(x, c), :] for c in range(COMPS)]
-        back = jnp.maximum(x - 1, 0)
-        real = jnp.where(x > 0, 1.0, 0.0)
+        before, cross, square, sums = carry
+        o = [o_ref[line_rows(x, c), :] for c in range(COMPS)]
         weights = [tab_scr[k, pl.ds(x, 1), :] for k in range(4)]
         s = [o[0] * o[0], o[1] * o[1]]
         both = COUPLING_CROSS * (s[0] + s[1])
-        base = (v_scr[pl.ds(pl.multiple_of(x * NZ, NZ), NZ), :] + 2.0) + both
+        base = (v_scr[line_rows(x), :] + 2.0) + both
         own = (COUPLING_FIRST - COUPLING_CROSS, COUPLING_SECOND - COUPLING_CROSS)
         new_cross, new_square, new_sums = [], [], []
         for c in range(COMPS):
@@ -124,18 +127,18 @@
             around = around + (pltpu.roll(o[c], 1, 1) + pltpu.roll(o[c], NY - 1, 1))
             a = (base + own[c] * s[c]) * o[c] - 0.5 * around
             a_ref[rows(x, c), :] = a
-            prev = real * o_ref[rows(back, c), :]
-            new_cross.append(cross[c] + o[c] * ((a + o[c]) - prev))
+            new_cross.append(cross[c] + o[c] * ((a + o[c]) - before[c]))
             new_square.append(square[c] + s[c])
             new_sums.append(
                 [decay * sums[c][0] + o[c], decay * sums[c][1] + a]
                 + [sums[c][1 + k] + weights[k] * o[c] for k in range(1, 4)]
                 + [sums[c][4 + k] + weights[k] * a for k in range(1, 4)]
             )
-        return new_cross, new_square, new_sums
-
-    cross, square, sums = lax.fori_loop(
-        0, NX, step, ([zero] * 2, [zero] * 2, [[zero] * 8] * 2), unroll=2
+        return o, new_cross, new_square, new_sums
+
+    wait(0, NZ)
+    _, cross, square, sums = lax.fori_loop(
+        0, NX, step, ([zero] * 2, [zero] * 2, [zero] * 2, [[zero] * 8] * 2), unroll=2
     )
     once = jnp.exp(jnp.full((NZ, NY), -rate, jnp.float32))
     for c in range(COMPS):
@@ -158,8 +161,8 @@
     return cross / (square + EPS) + sigma
 
 
-def sweep_kernel(rate_ref, gain_ref, sigma_ref, o_hbm, a_ref, edge_ref, halo_ref, sums_ref, p_ref, q_ref, local_ref, o_ref, fo_scr, fa_scr, sems):
-    copy = start_lines(o_hbm, o_ref, sems)
+def sweep_kernel(rate_ref, gain_ref, sigma_ref, o_hbm, a_ref, edge_ref, halo_ref, sums_ref, p_ref, q_ref, local_ref, o_ref, fo_scr, fa_scr, a_scr, sems):
+    wait = start_planes(o_hbm, o_ref, sems)
     gain4 = TAU * gain_ref[0]
     keep = 1.0 - TAU * sigma_ref[0]
     decay = jnp.exp(jnp.full((NZ, NY), -rate_ref[0], jnp.float32))
@@ -174,29 +177,30 @@
 
         def ahead(x, carry):
             fo, fa = carry
-            if c == 0:
-                copy(x).wait()
-            o = o_ref[rows(x, c), :]
+            o = o_ref[line_rows(x, c), :]
             a = a_ref[rows(x, c), :] + jnp.where(ends, pltpu.roll(delta, NY - (2 * x + 1), 1), 0.0)
             fo = decay * fo + o
             fa = decay * fa + a
             fo_scr[pl.ds(pl.multiple_of(x * NZ, NZ), NZ), :] = fo
             fa_scr[pl.ds(pl.multiple_of(x * NZ, NZ), NZ), :] = fa
-            p_ref[rows(x, c), :] = a
+            a_scr[pl.ds(pl.multiple_of(x * NZ, NZ), NZ), :] = a
             return fo, fa
 
+        wait(c * NZ, (c + 1) * NZ)
         lax.fori_loop(0, NX, ahead, (zero, zero), unroll=4)
         shift = jnp.broadcast_to(local_shift(sums_ref, c, sigma_ref[0]), (NZ, NY))
 
         def behind(k, carry):
             x = NX - 1 - k
             bo, ba, ww, wq, qq = carry
-            o, a = o_ref[rows(x, c), :], p_ref[rows(x, c), :]
+            o, a = o_ref[line_rows(x, c), :], a_scr[pl.ds(pl.multiple_of(x * NZ, NZ), NZ), :]
             do, da = decay * bo, decay * ba
             q = gain4 * (fo_scr[pl.ds(pl.multiple_of(x * NZ, NZ), NZ), :] + do)
             p = keep * o - gain4 * (fa_scr[pl.ds(pl.multiple_of(x * NZ, NZ), NZ), :] + da)
-            q_ref[rows(x, c), :] = q
-            p_ref[rows(x, c), :] = p
+            for b in range(NZ // ROWS):
+                place = pl.ds(pl.multiple_of(((c * NZ // ROWS + b) * NX + x) * ROWS, ROWS), ROWS)
+                q_ref[place, :] = q[b * ROWS : (b + 1) * ROWS, :]
+                p_ref[place, :] = p[b * ROWS : (b + 1) * ROWS, :]
             w = p + shift * q
             return do + o, da + a, ww + w * w, wq + w * q, qq + q * q
 
@@ -312,20 +316,20 @@
 
 
 def finish_kernel(cells, rate_ref, got_ref, mass_ref, p_hbm, q_hbm, out_hbm, p_ref, q_ref, out_scr, tab_scr, sems, in_sems):
-    def copy(x):
-        source = out_scr.at[pl.ds(pl.multiple_of(x * LINES, LINES), LINES), :]
-        return pltpu.make_async_copy(source, out_hbm.at[:, x, :], sems.at[x])
-
-    size = NX * LINES // CHUNKS
+    blocks = LINES // ROWS
+    size = NX * ROWS
 
     def fetch(k):
-        block = pl.ds(pl.multiple_of(k * size, size), size)
+        block = pl.ds(k * size, size)
         return (
             pltpu.make_async_copy(p_hbm.at[block, :], p_ref.at[block, :], in_sems.at[0, k]),
             pltpu.make_async_copy(q_hbm.at[block, :], q_ref.at[block, :], in_sems.at[1, k]),
         )
 
-    for k in range(CHUNKS):
+    def copy(k):
+        return pltpu.make_async_copy(out_scr.at[pl.ds(k * PITCH, NX), :], out_hbm.at[k], sems.at[k])
+
+    for k in range(blocks):
         for one in fetch(k):
             one.start()
     rate = rate_ref[0]
@@ -346,29 +350,29 @@
             piece = got_ref[j * LINES + c * NZ : j * LINES + (c + 1) * NZ, :]
             forward = jnp.where(slot == j, pltpu.roll(piece, (WIDE * (j - 2)) % NY, 1) if j != 2 else piece, forward)
             backward = jnp.where(slot == j, pltpu.roll(piece, (WIDE * (j - 3)) % NY, 1) if j != 3 else piece, backward)
-        terms.append((ratio, lifted, ratio * forward, ratio * backward))
-
-    def step(x, _):
-        rise = tab_scr[0, pl.ds(x, 1), :]
-        fall = tab_scr[1, pl.ds(x, 1), :]
-        for c in range(COMPS):
-            ratio, lifted, forward, backward = terms[c]
-            value = ratio * p_ref[rows(x, c), :] + lifted * q_ref[rows(x, c), :]
-            out_scr[rows(x, c), :] = value - (rise * forward + fall * backward)
-        copy(x).start()
-        return 0
-
-    def drain(x, _):
-        copy(x).wait()
-        return 0
-
-    def chunk(k, _):
+        terms.append((ratio[:ROWS], lifted[:ROWS], ratio * forward, ratio * backward))
+
+    for k in range(blocks):
+        comp, block = k // (NZ // ROWS), k % (NZ // ROWS)
+        ratio, lifted = terms[comp][:2]
+        forward, backward = [t[block * ROWS : (block + 1) * ROWS, :] for t in terms[comp][2:]]
         for one in fetch(k):
             one.wait()
-        return lax.fori_loop(0, NX // CHUNKS, lambda i, z: step(k * (NX // CHUNKS) + i, z), 0, unroll=True)
-
-    lax.fori_loop(0, CHUNKS, chunk, 0)
-    lax.fori_loop(0, NX, drain, 0, unroll=8)
+
+        def step(x, _):
+            rise = tab_scr[0, pl.ds(x, 1), :]
+            fall = tab_scr[1, pl.ds(x, 1), :]
+            place = pl.ds(pl.multiple_of(k * size + x * ROWS, ROWS), ROWS)
+            value = ratio * p_ref[place, :] + lifted * q_ref[place, :]
+            target = pl.ds(k * ROWS * PITCH + x, ROWS, stride=PITCH)
+            out_scr[target, :] = value - (rise * forward + fall * backward)
+            return 0
+
+        lax.fori_loop(0, NX, step, 0, unroll=16)
+        for line in range(ROWS):
+            copy(k * ROWS + line).start()
+    for line in range(LINES):
+        copy(line).wait()
 
 
 def far(x):
@@ -395,13 +399,14 @@
     o = far(orbitals.reshape(LINES, NX, NY))
     cells_all = LINES * NX
     big = pltpu.VMEM((cells_all, NY), jnp.float32)
+    spread = pltpu.VMEM((LINES * PITCH, NY), jnp.float32)
     row = pltpu.VMEM((LINES, NY), jnp.float32)
     small = pltpu.VMEM((8, NY), jnp.float32)
-    queue = pltpu.SemaphoreType.DMA((NX,))
+    queue = pltpu.SemaphoreType.DMA((LINES,))
 
     o_near, edge, first, last = pl.pallas_call(
         load_kernel,
-        out_shape=(big, row, row, row),
+        out_shape=(spread, row, row, row),
         in_specs=[HBM],
         out_specs=(VMEM,) * 4,
         scratch_shapes=[queue],
@@ -418,7 +423,7 @@
         in_specs=[SMEM, SMEM, SMEM, VMEM, HBM],
         out_specs=(VMEM,) * 3,
         scratch_shapes=[
-            pltpu.VMEM((NX * NZ, NY), jnp.float32),
+            pltpu.VMEM((NZ * PITCH, NY), jnp.float32),
             pltpu.VMEM((4, NX, NY), jnp.float32),
             queue,
         ],
@@ -442,7 +447,7 @@
         out_shape=(big, big, small),
         in_specs=[SMEM] * 3 + [HBM] + [VMEM] * 4,
         out_specs=(VMEM,) * 3,
-        scratch_shapes=[big] + [pltpu.VMEM((NX * NZ, NY), jnp.float32)] * 2 + [queue],
+        scratch_shapes=[spread] + [pltpu.VMEM((NX * NZ, NY), jnp.float32)] * 3 + [queue],
         name="sweep",
         compiler_params=PARAMS,
     )(rate, gain, sigma, o, a, edge, halo, sums)
@@ -466,10 +471,10 @@
         scratch_shapes=[
             big,
             big,
-            big,
+            spread,
             pltpu.VMEM((2, NX, NY), jnp.float32),
             queue,
-            pltpu.SemaphoreType.DMA((2, CHUNKS)),
+            pltpu.SemaphoreType.DMA((2, LINES // ROWS)),
         ],
         name="finish",
         compiler_params=PARAMS,

time: 77.5 us -> 71.5 us (0.923)
  Pallas kernels: 29.6 us -> 22.3 us
  waiting for transfers between devices: 5.3 us -> 7.95 us
  blocking collectives: 20.9 us -> 19.6 us
    pallas_call x1, Pallas kernels: 6.25 us -> 3.48 us  [shards(): pl.pallas_call(load_kernel, out_shape=(spread, row, row, row), in_specs=[...]
    pallas_call x1, Pallas kernels: 9.09 us -> 6.44 us  [shards(): pl.pallas_call(sweep_kernel, out_shape=(big, big, small), in_specs=[SMEM]...]
    all_to_all x1, waiting for transfers between devices: 5.29 us -> 7.95 us  [shards(): lax.all_to_all(msg.reshape(devices, 1, 3 * NY), ALL, 0, 0, tiled=True)]
    pallas_call x1, Pallas kernels: 8.31 us -> 6.4 us  [shards(): pl.pallas_call(gather_kernel, out_shape=(big, pltpu.VMEM((8, LINES, NY),...]
    all_to_all x1, blocking collectives: 20.9 us -> 19.6 us  [shards(): lax.all_to_all(back.reshape(devices, 1, NY), ALL, 0, 0, tiled=True)]
  transfers between devices with their start and end apart: 3 -> 3, of which waited for: 1 -> 1; matrix products, arithmetic and copies ran while one was open for 0% -> 0% of each run, Pallas kernels for 23% -> 18%
where the time goes in v3:
time: 71.5 us; the launch traced here: 71.1 us
  Pallas kernels  22.3 us (31%)
  blocking collectives  19.6 us (27%)
  starting transfers between devices  17.8 us (25%)
  waiting for transfers between devices  7.95 us (11%)
  local copies, waits for them, and re-layouts  2.65 us (4%)
  between operations  0.9 us (1%)
    all_to_all x1, blocking collectives, shards(): lax.all_to_all(back.reshape(devices, 1, NY), ALL, 0, 0, tiled=True)  19.6 us
    all_to_all x1, starting transfers between devices, shards(): lax.all_to_all(msg.reshape(devices, 1, 3 * NY), ALL, 0, 0, tiled=True)  13.1 us
    all_to_all x1, waiting for transfers between devices, shards(): lax.all_to_all(msg.reshape(devices, 1, 3 * NY), ALL, 0, 0, tiled=True)  7.95 us
    pallas_call x1, Pallas kernels, shards(): pl.pallas_call(sweep_kernel, out_shape=(big, big, small), in_specs=[SMEM]...  6.44 us
    pallas_call x1, Pallas kernels, shards(): pl.pallas_call(gather_kernel, out_shape=(big, pltpu.VMEM((8, LINES, NY),...  6.4 us
    pallas_call x1, Pallas kernels, shards(): pl.pallas_call(lambda *refs: finish_kernel(cells, *refs), out_shape=f32(L...  3.9 us
    pallas_call x1, Pallas kernels, shards(): pl.pallas_call(load_kernel, out_shape=(spread, row, row, row), in_specs=[...  3.48 us
    unnamed x4, local copies, waits for them, and re-layouts  2.65 us
  transfers between devices with their start and end apart: 3, of which 1 were waited for; matrix products, arithmetic and copies ran while one was open for 0% of the time, Pallas kernels for 18%

profile of v3, /device:TPU:1, one launch (start us, length us, event | category | flops | bytes accessed | tf_op | source)
XLA Modules:
  0.0 71.1 jit_solution(7205729594396223412)
XLA Ops:
  0.0 3.5 %load.1 = (f32[4608,128]{1,0:T(8,128)S(1)}, f32[64,128]{1,0:T(8,128)S(1)}, f32[64,128]{1,0:T(8,128)S(1)}, f32[64,128]{1,0:T(8,128)S(1)}) custom-call(f32[64,64,128]{2,1,0:T(8,128)} %bitcast.12), custom_call_target="tpu_custom_call" | custom-call | tf_op jit(solution)/shard_map/load/pallas_call | solution.py:407
  3.5 2.2 %collective-permute-start = (f32[64,128]{1,0:T(8,128)S(1)}, f32[64,128]{1,0:T(8,128)S(1)}, u32[]{:S(2)}, u32[]{:S(2)}) collective-permute-start(f32[64,128]{1,0:T(8,128)S(1)} %get-tuple-element.20.edge_ref), channel_id=1, source_target_pairs={{0,1},{1,0},{2,3},{3,2},{4,5},{5,4},{6,7},{7,6},{8,9},{9,8},{10,11... | collective-permute-start | bytes 98312 | tf_op jit(solution)/shard_map/ppermute | solution.py:416
  5.7 2.5 %collective-permute-start.1 = (f32[64,128]{1,0:T(8,128)S(1)}, f32[64,128]{1,0:T(8,128)S(1)}, u32[]{:S(2)}, u32[]{:S(2)}) collective-permute-start(f32[64,128]{1,0:T(8,128)S(1)} %get-tuple-element.22), channel_id=1, source_target_pairs={{0,2},{2,4},{4,6},{6,8},{8,10},{10,12},{12,14},{14,16},{16,18},{18... | collective-permute-start | bytes 98312 | tf_op jit(solution)/shard_map/ppermute | solution.py:417
  9.0 6.4 %gather.1 = (f32[4096,128]{1,0:T(8,128)S(1)}, f32[8,64,128]{2,1,0:T(8,128)S(1)}, f32[8,128]{1,0:T(8,128)S(1)}) custom-call(f32[1]{0:T(128)S(6)} %log1p.3.rate_ref.refs_1_.refs_0_, f32[1]{0:T(128)S(6)} %sqrt.7.gain_ref.refs_2_, f32[1]{0:T(128)S(6)} %div.6.sigma_ref.refs_3_, f32[4608,128]{1,0:T(8,128)S(1)} %get-tuple-element.17.o_ref, f32[32,64,128]{2,1,0:T(8,128)} %v_hbm.1), custom_call_target="tpu_custom_call" | custom-call | tf_op jit(solution)/shard_map/gather/pallas_call | solution.py:420
  15.4 0.0 collective-permute-done.halo_ref
  15.4 0.0 collective-permute-done.1.before_ref
  15.4 1.4 %pack.1 = f32[768,128]{1,0:T(8,128)} custom-call(f32[1]{0:T(128)S(6)} %log1p.3.rate_ref.refs_1_.refs_0_, f32[1]{0:T(128)S(6)} %sqrt.7.gain_ref.refs_2_, f32[8,64,128]{2,1,0:T(8,128)S(1)} %get-tuple-element.18.tips_ref, f32[8,128]{1,0:T(8,128)S(1)} %get-tuple-element.19.sums_ref.refs_5_, f32[64,128]{1,0:T(8,128)S(1)} %get-tuple-element.20.edge_ref, ...), custom_call_target="tpu_custom_call" | custom-call | tf_op jit(solution)/shard_map/pack/pallas_call | solution.py:435
  16.8 13.1 %all-to-all-start = ((f32[256,1,384]{2,1,0:T(1,128)}), f32[256,1,384]{2,1,0:T(1,128)S(1)}, u32[]{:S(2)}, u32[]{:S(2)}) async-start(f32[256,1,384]{2,1,0:T(1,128)} %bitcast.2), calls=%async_computation | async-start | bytes 786432 | tf_op jit(solution)/shard_map/all_to_all | solution.py:443
  29.9 6.4 %sweep.1 = (f32[4096,128]{1,0:T(8,128)S(1)}, f32[4096,128]{1,0:T(8,128)S(1)}, f32[8,128]{1,0:T(8,128)S(1)}) custom-call(f32[1]{0:T(128)S(6)} %log1p.3.rate_ref.refs_1_.refs_0_, f32[1]{0:T(128)S(6)} %sqrt.7.gain_ref.refs_2_, f32[1]{0:T(128)S(6)} %div.6.sigma_ref.refs_3_, f32[64,64,128]{2,1,0:T(8,128)} %bitcast.13, f32[4096,128]{1,0:T(8,128)S(1)} %get-tuple-element.23.a_ref, ...), custom_call_target="tpu_custom_call" | custom-call | tf_op jit(solution)/shard_map/sweep/pallas_call | solution.py:445
  36.3 0.0 copy-start
  36.3 1.3 %copy-done = f32[4096,128]{1,0:T(8,128)} copy-done((f32[4096,128]{1,0:T(8,128)}, f32[4096,128]{1,0:T(8,128)S(1)}, u32[]{:S(2)}) %copy-start) | copy-done | bytes 2097176
  37.7 0.0 copy-start.1
  37.7 1.3 %copy-done.1 = f32[4096,128]{1,0:T(8,128)} copy-done((f32[4096,128]{1,0:T(8,128)}, f32[4096,128]{1,0:T(8,128)S(1)}, u32[]{:S(2)}) %copy-start.1) | copy-done | bytes 2097176
  39.0 7.9 %all-to-all-done = f32[256,1,384]{2,1,0:T(1,128)S(1)} async-done(((f32[256,1,384]{2,1,0:T(1,128)}), f32[256,1,384]{2,1,0:T(1,128)S(1)}, u32[]{:S(2)}, u32[]{:S(2)}) %all-to-all-start) | async-done | bytes 393248 | tf_op jit(solution)/shard_map/all_to_all | solution.py:443
  46.9 0.7 owner.1
  47.6 19.6 %all_to_all.10 = f32[256,1,128]{2,1,0:T(1,128)S(1)} all-to-all(f32[256,1,128]{2,1,0:T(1,128)S(1)} %bitcast.11), channel_id=1, replica_groups=mesh['gx_0'=2,'gx_1'=4,'gx_2'=8,'gx_3'=2,'gy'=2] {'gx_0','gx_1','gx_2','..., dimensions={0} | all-to-all | bytes 262144 | tf_op jit(solution)/shard_map/all_to_all | solution.py:464
  67.2 3.9 %finish.1 = f32[64,64,128]{2,1,0:T(8,128)} custom-call(f32[1]{0:T(128)S(6)} %log1p.3.rate_ref.refs_1_.refs_0_, f32[256,128]{1,0:T(8,128)S(1)} %bitcast.10, f32[8,128]{1,0:T(8,128)S(1)} %get-tuple-element.26.refs_2_, f32[4096,128]{1,0:T(8,128)} %copy-done, f32[4096,128]{1,0:T(8,128)} %copy-done.1), custom_call_target="tpu_custom_call" | custom-call | tf_op jit(solution)/shard_map/finish/pallas_call | solution.py:466
Async XLA Ops:
  3.5 11.9 %collective-permute-start = (f32[64,128]{1,0:T(8,128)S(1)}, f32[64,128]{1,0:T(8,128)S(1)}, u32[]{:S(2)}, u32[]{:S(2)}) collective-permute-start(f32[64,128]{1,0:T(8,128)S(1)} %get-tuple-element.20.edge_ref), channel_id=1, source_target_pairs={{0,1},{1,0},{2,3},{3,2},{4,5},{5,4},{6,7},{7,6},{8,9},{9,8},{10,11... | collective-permute-start | bytes 98312 | tf_op jit(solution)/shard_map/ppermute | solution.py:416
  5.7 9.7 %collective-permute-start.1 = (f32[64,128]{1,0:T(8,128)S(1)}, f32[64,128]{1,0:T(8,128)S(1)}, u32[]{:S(2)}, u32[]{:S(2)}) collective-permute-start(f32[64,128]{1,0:T(8,128)S(1)} %get-tuple-element.22), channel_id=1, source_target_pairs={{0,2},{2,4},{4,6},{6,8},{8,10},{10,12},{12,14},{14,16},{16,18},{18... | collective-permute-start | bytes 98312 | tf_op jit(solution)/shard_map/ppermute | solution.py:417
  16.8 30.1 %all-to-all-start = ((f32[256,1,384]{2,1,0:T(1,128)}), f32[256,1,384]{2,1,0:T(1,128)S(1)}, u32[]{:S(2)}, u32[]{:S(2)}) async-start(f32[256,1,384]{2,1,0:T(1,128)} %bitcast.2), calls=%async_computation | async-start | bytes 786432 | tf_op jit(solution)/shard_map/all_to_all | solution.py:443
  36.3 1.3 %copy-start = (f32[4096,128]{1,0:T(8,128)}, f32[4096,128]{1,0:T(8,128)S(1)}, u32[]{:S(2)}) copy-start(f32[4096,128]{1,0:T(8,128)S(1)} %get-tuple-element.27.refs_3_) | copy-start | bytes 6291460
  37.7 1.3 %copy-start.1 = (f32[4096,128]{1,0:T(8,128)}, f32[4096,128]{1,0:T(8,128)S(1)}, u32[]{:S(2)}) copy-start(f32[4096,128]{1,0:T(8,128)S(1)} %get-tuple-element.28.refs_4_) | copy-start | bytes 6291460

commit v4 on v3

v4 whole, which is shorter than its diff:
```python
import jax
import jax.numpy as jnp
from jax import lax
from jax.experimental import pallas as pl
from jax.experimental.pallas import tpu as pltpu
from jax.sharding import Mesh
from jax.sharding import PartitionSpec as P

GX = ("gx_0", "gx_1", "gx_2", "gx_3")
INNER = ("gx_2", "gx_3")
OUTER = ("gx_0", "gx_1", "gy")
ALL = ("gx_0", "gx_1", "gx_2", "gx_3", "gy")

TAU = 4.0
EPS = 1e-06
COUPLING_FIRST = 0.06
COUPLING_SECOND = 0.05
COUPLING_CROSS = 0.04
HIGHEST = lax.Precision.HIGHEST

COMPS = 2
NZ = 32
NX = 64
NY = 128
LINES = COMPS * NZ
MEMBERS = 16
SHARE = LINES // MEMBERS
STRIDE = 8 * SHARE + 1
BACK = 2 * SHARE + 1
PITCH = NX + 8
ROWS = 8

PARAMS = pltpu.CompilerParams(vmem_limit_bytes=16 << 20)
VMEM = pl.BlockSpec(memory_space=pltpu.VMEM)
HBM = pl.BlockSpec(memory_space=pltpu.HBM)
SMEM = pl.BlockSpec(memory_space=pltpu.SMEM)


def lane_of(shape):
    return lax.broadcasted_iota(jnp.int32, shape, 1)


def row_of(shape):
    return lax.broadcasted_iota(jnp.int32, shape, 0)


def rows(x, comp):
    return pl.ds(pl.multiple_of(x * LINES + comp * NZ, NZ), NZ)


def part(comp):
    return slice(comp * NZ, (comp + 1) * NZ)


def start_planes(source, target, sems):
    def copy(k):
        place = pl.ds(pl.multiple_of(k * PITCH, 8), NX)
        return pltpu.make_async_copy(source.at[k], target.at[place, :], sems.at[k])

    def start(k, _):
        copy(k).start()
        return 0

    lax.fori_loop(0, source.shape[0], start, 0, unroll=8)

    def wait(first, last):
        def one(k, _):
            copy(k).wait()
            return 0

        lax.fori_loop(first, last, one, 0, unroll=8)

    return wait


def line_rows(x, comp=0):
    return pl.ds(comp * NZ * PITCH + x, NZ, stride=PITCH)


def load_kernel(o_hbm, v_hbm, o_ref, v_ref, edge_ref, first_ref, last_ref, sems, v_sems):
    wait = start_planes(o_hbm, o_ref, sems)
    wait_v = start_planes(v_hbm, v_ref, v_sems)
    lane = lane_of((NZ, NY)) // 2
    for c in range(COMPS):
        wait(c * NZ, (c + 1) * NZ)

        def step(x, packed):
            return jnp.where(lane == x, pltpu.roll(o_ref[line_rows(x, c), :], 2 * x + 1, 1), packed)

        edge_ref[part(c), :] = lax.fori_loop(0, NX, step, jnp.zeros((NZ, NY), jnp.float32), unroll=8)
        first_ref[part(c), :] = o_ref[line_rows(0, c), :]
        last_ref[part(c), :] = o_ref[line_rows(NX - 1, c), :]
    wait_v(0, NZ)


def tables(rate, count):
    place = (row_of((count * NX, NY)) // count).astype(jnp.float32)
    index = row_of((NX, NY)).astype(jnp.float32)
    rise = jnp.exp(-rate * (index + 1.0))
    fall = jnp.exp(-rate * (float(NX) - index))
    shape = (count * NX, NX)
    gap = (row_of(shape) // count - lane_of(shape)).astype(jnp.float32)
    near = jnp.exp(-rate * jnp.abs(gap))
    return (
        jnp.exp(-rate * (float(NX - 1) - place)),
        jnp.exp(-rate * place),
        dot(near, rise),
        dot(near, fall),
    )


def gather_kernel(rate_ref, gain_ref, sigma_ref, o_ref, v_ref, a_ref, tips_ref, sums_ref, tab_scr):
    rate = rate_ref[0]
    gain4 = TAU * gain_ref[0]
    keep = 1.0 - TAU * sigma_ref[0]
    for k, table in enumerate(tables(rate, 1)):
        tab_scr[k] = table
    zero = jnp.zeros((NZ, NY), jnp.float32)
    decay = jnp.exp(jnp.full((NZ, NY), -rate, jnp.float32))

    def step(x, carry):
        before, cross, square, sums = carry
        o = [o_ref[line_rows(x, c), :] for c in range(COMPS)]
        weights = [tab_scr[k, pl.ds(x, 1), :] for k in range(4)]
        s = [o[0] * o[0], o[1] * o[1]]
        both = COUPLING_CROSS * (s[0] + s[1])
        base = (v_ref[line_rows(x), :] + 2.0) + both
        own = (COUPLING_FIRST - COUPLING_CROSS, COUPLING_SECOND - COUPLING_CROSS)
        new_cross, new_square, new_sums = [], [], []
        for c in range(COMPS):
            around = pltpu.roll(o[c], 1, 0) + pltpu.roll(o[c], NZ - 1, 0)
            around = around + (pltpu.roll(o[c], 1, 1) + pltpu.roll(o[c], NY - 1, 1))
            a = (base + own[c] * s[c]) * o[c] - 0.5 * around
            a_ref[rows(x, c), :] = a
            new_cross.append(cross[c] + o[c] * ((a + o[c]) - before[c]))
            new_square.append(square[c] + s[c])
            new_sums.append(
                [decay * sums[c][0] + o[c], decay * sums[c][1] + a]
                + [sums[c][1 + k] + weights[k] * o[c] for k in range(1, 4)]
                + [sums[c][4 + k] + weights[k] * a for k in range(1, 4)]
            )
        return o, new_cross, new_square, new_sums

    _, cross, square, sums = lax.fori_loop(
        0, NX, step, ([zero] * 2, [zero] * 2, [zero] * 2, [[zero] * 8] * 2), unroll=2
    )
    once = jnp.exp(jnp.full((NZ, NY), -rate, jnp.float32))
    for c in range(COMPS):
        f_o, f_a, b_o, r_o, s_o, b_a, r_a, s_a = sums[c]
        tips_ref[0, part(c), :] = f_o
        tips_ref[1, part(c), :] = b_o
        tips_ref[2, part(c), :] = f_a
        tips_ref[3, part(c), :] = b_a
        tips_ref[4, part(c), :] = gain4 * r_o
        tips_ref[5, part(c), :] = gain4 * s_o
        tips_ref[6, part(c), :] = keep * (once * b_o) - gain4 * r_a
        tips_ref[7, part(c), :] = keep * (once * f_o) - gain4 * s_a
        sums_ref[c : c + 1, :] = jnp.sum(cross[c], axis=0, keepdims=True)
        sums_ref[COMPS + c : COMPS + c + 1, :] = jnp.sum(square[c], axis=0, keepdims=True)


def local_shift(sums_ref, c, sigma):
    cross = jnp.sum(sums_ref[c : c + 1, :], axis=1, keepdims=True)
    square = jnp.sum(sums_ref[COMPS + c : COMPS + c + 1, :], axis=1, keepdims=True)
    return cross / (square + EPS) + sigma


def sweep_kernel(rate_ref, gain_ref, sigma_ref, o_hbm, a_ref, edge_ref, halo_ref, sums_ref, p_hbm, q_hbm, local_ref, p_ref, q_ref, o_ref, fo_scr, fa_scr, a_scr, sems, out_sems):
    wait = start_planes(o_hbm, o_ref, sems)

    def send(c):
        block = pl.ds(c * NZ * NX, NZ * NX)
        return (
            pltpu.make_async_copy(p_ref.at[block, :], p_hbm.at[block, :], out_sems.at[0, c]),
            pltpu.make_async_copy(q_ref.at[block, :], q_hbm.at[block, :], out_sems.at[1, c]),
        )

    gain4 = TAU * gain_ref[0]
    keep = 1.0 - TAU * sigma_ref[0]
    decay = jnp.exp(jnp.full((NZ, NY), -rate_ref[0], jnp.float32))
    lane = lane_of((NZ, NY))
    zero = jnp.zeros((NZ, NY), jnp.float32)
    lane1 = lane_of((1, NY))
    for c in range(COMPS):
        delta = -0.5 * (halo_ref[part(c), :] - edge_ref[part(c), :])
        even = lane % 2 == 0
        delta = jnp.where(even, pltpu.roll(delta, NY - 1, 1), pltpu.roll(delta, 1, 1))
        ends = (lane == 0) | (lane == NY - 1)

        def ahead(x, carry):
            fo, fa = carry
            o = o_ref[line_rows(x, c), :]
            a = a_ref[rows(x, c), :] + jnp.where(ends, pltpu.roll(delta, NY - (2 * x + 1), 1), 0.0)
            fo = decay * fo + o
            fa = decay * fa + a
            fo_scr[pl.ds(pl.multiple_of(x * NZ, NZ), NZ), :] = fo
            fa_scr[pl.ds(pl.multiple_of(x * NZ, NZ), NZ), :] = fa
            a_scr[pl.ds(pl.multiple_of(x * NZ, NZ), NZ), :] = a
            return fo, fa

        wait(c * NZ, (c + 1) * NZ)
        lax.fori_loop(0, NX, ahead, (zero, zero), unroll=4)
        shift = jnp.broadcast_to(local_shift(sums_ref, c, sigma_ref[0]), (NZ, NY))

        def behind(k, carry):
            x = NX - 1 - k
            bo, ba, ww, wq, qq = carry
            o, a = o_ref[line_rows(x, c), :], a_scr[pl.ds(pl.multiple_of(x * NZ, NZ), NZ), :]
            do, da = decay * bo, decay * ba
            q = gain4 * (fo_scr[pl.ds(pl.multiple_of(x * NZ, NZ), NZ), :] + do)
            p = keep * o - gain4 * (fa_scr[pl.ds(pl.multiple_of(x * NZ, NZ), NZ), :] + da)
            for b in range(NZ // ROWS):
                place = pl.ds(pl.multiple_of(((c * NZ // ROWS + b) * NX + x) * ROWS, ROWS), ROWS)
                q_ref[place, :] = q[b * ROWS : (b + 1) * ROWS, :]
                p_ref[place, :] = p[b * ROWS : (b + 1) * ROWS, :]
            w = p + shift * q
            return do + o, da + a, ww + w * w, wq + w * q, qq + q * q

        _, _, ww, wq, qq = lax.fori_loop(0, NX, behind, (zero,) * 5, unroll=4)
        for k, value in enumerate((ww, wq, qq)):
            local_ref[3 * c + k : 3 * c + k + 1, :] = jnp.sum(value, axis=0, keepdims=True)
        for one in send(c):
            one.start()
    for c in range(COMPS):
        for one in send(c):
            one.wait()


def dot(a, b):
    return jnp.dot(a, b, precision=HIGHEST, preferred_element_type=jnp.float32)


def pack_kernel(rate_ref, gain_ref, tips_ref, sums_ref, edge_ref, halo_ref, first_ref, before_ref, msg_ref):
    gain4 = TAU * gain_ref[0]
    halo = halo_ref[...]
    delta = -0.5 * (halo - edge_ref[...])
    shape = (NY, NY)
    odd = row_of(shape) % 2
    hit = ((lane_of(shape) == 0) & (odd == 0)) | ((lane_of(shape) == NY - 1) & (odd == 1))
    fixes = [dot(delta, jnp.where(hit, table, 0.0)) for table in tables(rate_ref[0], 2)]
    tips = [tips_ref[k] for k in range(8)]
    tips[2] = tips[2] + fixes[0]
    tips[3] = tips[3] + fixes[1]
    tips[6] = tips[6] - gain4 * fixes[2]
    tips[7] = tips[7] - gain4 * fixes[3]

    lane = lane_of((LINES, NY))
    even = lane % 2 == 0
    swapped = jnp.where(even, pltpu.roll(delta, NY - 1, 1), pltpu.roll(delta, 1, 1))
    extra = edge_ref[...] * swapped - first_ref[...] * before_ref[...]
    row_lane = lane_of((1, NY))
    scalars = jnp.zeros((1, NY), jnp.float32)
    for c in range(COMPS):
        cross = sums_ref[c : c + 1, :] + jnp.sum(extra[c * NZ : (c + 1) * NZ, :], axis=0, keepdims=True)
        scalars = jnp.where(row_lane == c, jnp.sum(cross, axis=1, keepdims=True), scalars)
        square = jnp.sum(sums_ref[COMPS + c : COMPS + c + 1, :], axis=1, keepdims=True)
        scalars = jnp.where(row_lane == COMPS + c, square, scalars)
    for f in range(MEMBERS):
        base = STRIDE * f
        for k in range(8):
            msg_ref[base + SHARE * k : base + SHARE * (k + 1), :] = tips[k][SHARE * f : SHARE * (f + 1), :]
        msg_ref[base + 8 * SHARE : base + 8 * SHARE + 1, :] = scalars


def pick(vector, k):
    return jnp.sum(jnp.where(lane_of((1, NY)) == k, vector, 0.0), axis=1, keepdims=True)


def total_of(block):
    return jnp.sum(jnp.sum(block, axis=0, keepdims=True), axis=1, keepdims=True)


def scalar_row(values):
    lane = lane_of((1, NY))
    row = jnp.zeros((1, NY), jnp.float32)
    for k, value in enumerate(values):
        row = jnp.where(lane == k, value, row)
    return row


def overlap(rate, count):
    shape = (8, NY)
    index = (row_of(shape) * NY + lane_of(shape) + 1).astype(jnp.float32)
    rho = total_of(jnp.where(index <= float(count), jnp.exp(-2.0 * rate * index), 0.0))
    omega = float(count) * jnp.exp(jnp.full((1, 1), -rate * float(count + 1), jnp.float32))
    return rho, omega


def other_half(x):
    return pltpu.roll(x, SHARE, 0)


def reach(rate, f, upper):
    steps = jnp.where(upper, float(f), float(MEMBERS - 1 - f))
    return jnp.exp(-rate * float(NX) * steps)


def group_kernel(member_ref, rate_ref, gain_ref, sigma_ref, got_ref, sums_ref, local_ref, msg_ref, pre_ref):
    rate, sigma = rate_ref[0], sigma_ref[0]
    gain4 = TAU * gain_ref[0]
    shape = (2 * SHARE, NY)
    upper = row_of(shape) < SHARE
    block = jnp.exp(jnp.full(shape, -rate * float(NX), jnp.float32))
    rho, omega = overlap(rate, NX)
    zero = jnp.zeros(shape, jnp.float32)

    def piece(f, k):
        start = STRIDE * f + 2 * SHARE * k
        return got_ref[start : start + 2 * SHARE, :]

    total = got_ref[STRIDE - 1 : STRIDE, :]
    for f in range(1, MEMBERS):
        total = total + got_ref[STRIDE * (f + 1) - 1 : STRIDE * (f + 1), :]
    sums = [pick(total, k) for k in range(2 * COMPS)]
    shifts = [sums[c] / (sums[COMPS + c] + EPS) + sigma for c in range(COMPS)]
    shift = jnp.where(member_ref[0] * SHARE < NZ, shifts[0], shifts[1])

    tips = [[piece(f, k) for f in range(MEMBERS)] for k in range(2)]
    ends, before = [], []
    for k in range(2):
        forward, backward = [zero], [zero]
        for f in range(MEMBERS):
            forward.append(block * forward[-1] + tips[k][f])
            backward.append(block * backward[-1] + tips[k][MEMBERS - 1 - f])
        ends.append(jnp.where(upper, forward[-1], backward[-1]))
        before.append([jnp.where(upper, forward[f], backward[MEMBERS - 1 - f]) for f in range(MEMBERS)])
    moment0, moment1, ww, wq, qq = (zero,) * 5
    for f in range(MEMBERS):
        pre_o, pre_a = gain4 * before[0][f], gain4 * before[1][f]
        pre_ref[4 * SHARE * f : 4 * SHARE * f + 2 * SHARE, :] = pre_o
        pre_ref[4 * SHARE * f + 2 * SHARE : 4 * SHARE * (f + 1), :] = pre_a
        own_q, own_p = piece(f, 2), piece(f, 3)
        weight = reach(rate, f, upper)
        spread_o = rho * pre_o + omega * other_half(pre_o)
        spread_a = rho * pre_a + omega * other_half(pre_a)
        moment0 = moment0 + weight * (own_p - spread_a)
        moment1 = moment1 + weight * (own_q + spread_o)
        y = pre_a - shift * pre_o
        spread_y = spread_a - shift * spread_o
        own_w = own_p + shift * own_q
        ww = ww + y * (spread_y - 2.0 * own_w)
        wq = wq + (pre_o * (own_w - spread_y) - y * own_q)
        qq = qq + pre_o * (2.0 * own_q + spread_o)
    values = list(sums)
    for c in range(COMPS):
        values += [jnp.sum(local_ref[3 * c + k : 3 * c + k + 1, :], axis=1, keepdims=True) for k in range(3)]
        values.append(local_shift(sums_ref, c, sigma))
    values += [total_of(ww), total_of(wq), total_of(qq), shift]
    scalars = scalar_row(values)
    for k in range(MEMBERS):
        for i, value in enumerate((gain4 * ends[0], gain4 * ends[1], moment1, moment0)):
            start = STRIDE * k + 2 * SHARE * i
            msg_ref[start : start + 2 * SHARE, :] = value
        msg_ref[STRIDE * (k + 1) - 1 : STRIDE * (k + 1), :] = scalars


def owner_kernel(groups, cells, member_ref, mine_ref, rate_ref, sigma_ref, got_ref, pre_ref, back_ref, mass_ref):
    rate, sigma = rate_ref[0], sigma_ref[0]
    member, mine = member_ref[0], mine_ref[0]
    shape = (2 * SHARE, NY)
    upper = row_of(shape) < SHARE
    span = NX * MEMBERS
    block = jnp.exp(jnp.full(shape, -rate * float(span), jnp.float32))
    wrap = 1.0 - jnp.exp(jnp.full(shape, -rate * float(span * groups), jnp.float32))
    rho, omega = overlap(rate, span)
    scal = got_ref[pl.ds(STRIDE - 1, 2 * groups, stride=STRIDE), :]
    lane = lane_of((2 * groups, NY))

    def column(k):
        return jnp.sum(jnp.where(lane == k, scal, 0.0), axis=1, keepdims=True)

    def expand(first, value):
        ww, wq, qq, base = [column(first + k) for k in range(4)]
        more = value - base
        return jnp.sum(ww + more * (2.0 * wq + more * qq), axis=0, keepdims=True)

    total = jnp.sum(scal, axis=0, keepdims=True)
    squares, shifts = [], []
    for c in range(COMPS):
        mean_square = pick(total, COMPS + c) / cells
        squares.append(mean_square)
        shifts.append((pick(total, c) / cells) / (mean_square + EPS) + sigma)
    mass_ref[...] = jnp.broadcast_to(scalar_row(squares + shifts), (8, NY))
    first = member * SHARE < NZ
    shift = jnp.where(first, shifts[0], shifts[1])

    def piece(g, y, k):
        start = STRIDE * (2 * g + y) + 2 * SHARE * k
        return got_ref[start : start + 2 * SHARE, :]

    zero = jnp.zeros(shape, jnp.float32)
    acc, chosen = zero, zero
    for y in range(2):
        ends = [piece(g, y, 1) - shift * piece(g, y, 0) for g in range(groups)]
        forward, backward = zero, zero
        for g in range(groups):
            forward = block * forward + ends[g]
            backward = block * backward + ends[groups - 1 - g]
        entering_f, entering_b = [forward / wrap], [backward / wrap]
        for g in range(groups - 1):
            entering_f.append(block * entering_f[-1] + ends[g])
            entering_b.append(block * entering_b[-1] + ends[groups - 1 - g])
        for g in range(groups):
            carry = jnp.where(upper, entering_f[g], entering_b[groups - 1 - g])
            moment = piece(g, y, 3) + shift * piece(g, y, 2)
            acc = acc + carry * (rho * carry + omega * other_half(carry) - 2.0 * moment)
            chosen = jnp.where(mine == 2 * g + y, carry, chosen)
    joined = total_of(acc) + expand(12, shift)
    values = []
    for c in range(COMPS):
        value = expand(4 + 4 * c, shifts[c])
        values.append(value + jnp.where(first == (c == 0), joined, 0.0))
    scalars = scalar_row(values)
    for f in range(MEMBERS):
        pre_o = pre_ref[4 * SHARE * f : 4 * SHARE * f + 2 * SHARE, :]
        pre_a = pre_ref[4 * SHARE * f + 2 * SHARE : 4 * SHARE * (f + 1), :]
        value = (pre_a - shift * pre_o) + reach(rate, f, upper) * chosen
        back_ref[BACK * f : BACK * f + 2 * SHARE, :] = value
        back_ref[BACK * (f + 1) - 1 : BACK * (f + 1), :] = scalars


def blend_kernel(mass_ref, p_hbm, q_hbm, w_ref, p_ref, q_ref, sems):
    size = NX * ROWS

    def fetch(k):
        block = pl.ds(k * size, size)
        return (
            pltpu.make_async_copy(p_hbm.at[block, :], p_ref.at[block, :], sems.at[0, k]),
            pltpu.make_async_copy(q_hbm.at[block, :], q_ref.at[block, :], sems.at[1, k]),
        )

    for k in range(LINES // ROWS):
        for one in fetch(k):
            one.start()
    for k in range(LINES // ROWS):
        comp = k * ROWS // NZ
        shift = jnp.broadcast_to(pick(mass_ref[0:1, :], COMPS + comp), (NX, NY))
        for one in fetch(k):
            one.wait()

        def step(i, _):
            place = pl.ds(pl.multiple_of(k * size + i * NX, NX), NX)
            w_ref[place, :] = p_ref[place, :] + shift * q_ref[place, :]
            return 0

        lax.fori_loop(0, ROWS, step, 0, unroll=2)


def finish_kernel(cells, rate_ref, got_ref, mass_ref, w_ref, out_hbm, out_scr, tab_scr, sems):
    blocks = LINES // ROWS
    size = NX * ROWS

    def copy(k):
        return pltpu.make_async_copy(out_scr.at[pl.ds(k * PITCH, NX), :], out_hbm.at[k], sems.at[k])

    rate = rate_ref[0]
    index = row_of((NX, NY)).astype(jnp.float32)
    tab_scr[0] = jnp.exp(-rate * (index + 1.0))
    tab_scr[1] = jnp.exp(-rate * (float(NX) - index))
    total = got_ref[BACK - 1 : BACK, :]
    for f in range(1, MEMBERS):
        total = total + got_ref[BACK * (f + 1) - 1 : BACK * (f + 1), :]
    scales = []
    for c in range(COMPS):
        mean_square = pick(mass_ref[0:1, :], c)
        ratio = jnp.sqrt(mean_square / (pick(total, c) / cells + EPS))
        scales.append(jnp.broadcast_to(ratio, (ROWS, NY)))

    def carries(k, half):
        members = range(k * ROWS // SHARE, (k + 1) * ROWS // SHARE)
        starts = [BACK * f + half * SHARE for f in members]
        return jnp.concatenate([got_ref[i : i + SHARE, :] for i in starts], axis=0)

    for k in range(blocks):
        comp = k * ROWS // NZ
        ratio = scales[comp]
        forward, backward = ratio * carries(k, 0), ratio * carries(k, 1)
        def step(x, _):
            rise = tab_scr[0, pl.ds(x, 1), :]
            fall = tab_scr[1, pl.ds(x, 1), :]
            place = pl.ds(pl.multiple_of(k * size + x * ROWS, ROWS), ROWS)
            value = ratio * w_ref[place, :]
            target = pl.ds(k * ROWS * PITCH + x, ROWS, stride=PITCH)
            out_scr[target, :] = value - (rise * forward + fall * backward)
            return 0

        lax.fori_loop(0, NX, step, 0, unroll=16)
        for line in range(ROWS):
            copy(k * ROWS + line).start()
    for line in range(LINES):
        copy(line).wait()


def far(x):
    return pltpu.with_memory_space_constraint(x, pltpu.HBM)


def near(x):
    return pltpu.with_memory_space_constraint(x, pltpu.VMEM)


def exchange(x, axes):
    peers = lax.axis_size(axes)
    moved = lax.all_to_all(x.reshape(peers, 1, x.size // peers), axes, 0, 0, tiled=True)
    return moved.reshape(x.shape)


def f32(*shape):
    return jax.ShapeDtypeStruct(shape, jnp.float32)


def shards(orbitals, potential, shift_ratio):
    groups = lax.axis_size(GX)
    devices = lax.axis_size(ALL)
    cells = float(NZ * NX * NY * devices)
    line_cells = NX * groups
    sigma = shift_ratio / float(line_cells * line_cells)
    rate = jnp.log1p(sigma + jnp.sqrt(sigma * (sigma + 2.0)))
    gain = jnp.sqrt(sigma / (sigma + 2.0))
    member = lax.axis_index(INNER).astype(jnp.int32)
    mine = lax.axis_index(OUTER).astype(jnp.int32)
    o = far(orbitals.reshape(LINES, NX, NY))
    cells_all = LINES * NX
    big = pltpu.VMEM((cells_all, NY), jnp.float32)
    distant = pltpu.HBM((cells_all, NY), jnp.float32)
    spread = pltpu.VMEM((LINES * PITCH, NY), jnp.float32)
    row = pltpu.VMEM((LINES, NY), jnp.float32)
    small = pltpu.VMEM((8, NY), jnp.float32)
    queue = pltpu.SemaphoreType.DMA((LINES,))

    o_near, v_near, edge, first, last = pl.pallas_call(
        load_kernel,
        out_shape=(spread, pltpu.VMEM((NZ * PITCH, NY), jnp.float32), row, row, row),
        in_specs=[HBM] * 2,
        out_specs=(VMEM,) * 5,
        scratch_shapes=[queue, pltpu.SemaphoreType.DMA((NZ,))],
        name="load",
        compiler_params=PARAMS,
    )(o, far(potential))
    halo = near(lax.ppermute(edge, "gy", [(0, 1), (1, 0)]))
    before = near(lax.ppermute(last, GX, [(i, (i + 1) % groups) for i in range(groups)]))
    o_near, edge, first = near(o_near), near(edge), near(first)

    a, tips, sums = pl.pallas_call(
        gather_kernel,
        out_shape=(big, pltpu.VMEM((8, LINES, NY), jnp.float32), small),
        in_specs=[SMEM, SMEM, SMEM, VMEM, VMEM],
        out_specs=(VMEM,) * 3,
        scratch_shapes=[pltpu.VMEM((4, NX, NY), jnp.float32)],
        name="gather",
        compiler_params=PARAMS,
    )(rate, gain, sigma, o_near, near(v_near))
    a, tips, sums = near(a), near(tips), near(sums)

    msg = pl.pallas_call(
        pack_kernel,
        out_shape=pltpu.VMEM((MEMBERS * STRIDE, NY), jnp.float32),
        in_specs=[SMEM, SMEM] + [VMEM] * 6,
        out_specs=VMEM,
        name="pack",
        compiler_params=PARAMS,
    )(rate, gain, tips, sums, edge, halo, first, before)
    got = exchange(msg, INNER)

    p, q, local = pl.pallas_call(
        sweep_kernel,
        out_shape=(distant, distant, small),
        in_specs=[SMEM] * 3 + [HBM] + [VMEM] * 4,
        out_specs=(HBM, HBM, VMEM),
        scratch_shapes=[big, big, spread]
        + [pltpu.VMEM((NX * NZ, NY), jnp.float32)] * 3
        + [queue, pltpu.SemaphoreType.DMA((2, COMPS))],
        name="sweep",
        compiler_params=PARAMS,
    )(rate, gain, sigma, o, a, edge, halo, sums)
    p, q, local = far(p), far(q), near(local)

    joint, pre = pl.pallas_call(
        group_kernel,
        out_shape=(
            pltpu.VMEM((MEMBERS * STRIDE, NY), jnp.float32),
            pltpu.VMEM((4 * SHARE * MEMBERS, NY), jnp.float32),
        ),
        in_specs=[SMEM] * 4 + [VMEM] * 3,
        out_specs=(VMEM,) * 2,
        name="group",
        compiler_params=PARAMS,
    )(member.reshape(1), rate, gain, sigma, near(got), sums, local)
    outer = exchange(joint, OUTER)

    back, mass = pl.pallas_call(
        lambda *refs: owner_kernel(groups // MEMBERS, cells, *refs),
        out_shape=(pltpu.VMEM((MEMBERS * BACK, NY), jnp.float32), small),
        in_specs=[SMEM] * 4 + [VMEM] * 2,
        out_specs=(VMEM,) * 2,
        name="owner",
        compiler_params=PARAMS,
    )(member.reshape(1), mine.reshape(1), rate, sigma, near(outer), near(pre))
    returned = exchange(back, INNER)

    mass = near(mass)
    w = pl.pallas_call(
        blend_kernel,
        out_shape=big,
        in_specs=[VMEM, HBM, HBM],
        out_specs=VMEM,
        scratch_shapes=[big, big, pltpu.SemaphoreType.DMA((2, LINES // ROWS))],
        name="blend",
        compiler_params=PARAMS,
    )(mass, p, q)

    out = pl.pallas_call(
        lambda *refs: finish_kernel(cells, *refs),
        out_shape=f32(LINES, NX, NY),
        in_specs=[SMEM, VMEM, VMEM, VMEM],
        out_specs=HBM,
        scratch_shapes=[spread, pltpu.VMEM((2, NX, NY), jnp.float32), queue],
        name="finish",
        compiler_params=PARAMS,
    )(rate, near(returned), mass, near(w))
    return out.reshape(orbitals.shape)


def solution(mesh):
    split = Mesh(mesh.devices.reshape(2, 4, 8, 2, mesh.shape["gy"]), ALL)
    return jax.shard_map(
        shards,
        mesh=split,
        in_specs=(P(None, None, GX, "gy"), P(None, GX, "gy"), P()),
        out_specs=P(None, None, GX, "gy"),
        check_vma=False,
    )
```

time: 71.5 us -> 66.3 us (0.927)
  blocking collectives: 19.6 us -> 0 us
  waiting for transfers between devices: 7.95 us -> 18.1 us
  starting transfers between devices: 17.8 us -> 23 us
  local copies, waits for them, and re-layouts: 2.65 us -> 0 us
  Pallas kernels: 22.3 us -> 23.9 us
    all_to_all x1 -> x0, blocking collectives: 19.6 us -> none  [shards(): lax.all_to_all(back.reshape(devices, 1, NY), ALL, 0, 0, tiled=True)]
    all_to_all x1 -> x3, waiting for transfers between devices: 7.95 us -> 18.1 us  [exchange(): lax.all_to_all(x.reshape(peers, 1, x.size // peers), axes, 0, 0, tiled=True)]
    all_to_all x1 -> x3, starting transfers between devices: 13.1 us -> 18.6 us  [exchange(): lax.all_to_all(x.reshape(peers, 1, x.size // peers), axes, 0, 0, tiled=True)]
    pallas_call x4 -> x6, Pallas kernels: 11.9 us -> 16.9 us  [the longest x1 7.76 us: shards(): pl.pallas_call(sweep_kernel, out_shape=(distant, distant, small), in_spec...]
    unnamed x4 -> x0, local copies, waits for them, and re-layouts: 2.65 us -> none
    pallas_call x1, Pallas kernels: 3.9 us -> 2.06 us  [shards(): pl.pallas_call(lambda *refs: finish_kernel(cells, *refs), out_shape=f32(L...]
    pallas_call x1, Pallas kernels: 6.4 us -> 4.89 us  [shards(): pl.pallas_call(gather_kernel, out_shape=(big, pltpu.VMEM((8, LINES, NY),...]
    ppermute x1, starting transfers between devices: 2.2 us -> 1.3 us  [shards(): halo = near(lax.ppermute(edge, 'gy', [(0, 1), (1, 0)]))]
  transfers between devices with their start and end apart: 3 -> 5, of which waited for: 1 -> 3; matrix products, arithmetic and copies ran while one was open for 0% -> 0% of each run, Pallas kernels for 18% -> 23%
where the time goes in v4:
time: 66.3 us; the launch traced here: 65.8 us
  Pallas kernels  23.9 us (36%)
  starting transfers between devices  23 us (35%)
  waiting for transfers between devices  18.1 us (27%)
  between operations  0.89 us (1%)
    all_to_all x3, starting transfers between devices, exchange(): lax.all_to_all(x.reshape(peers, 1, x.size // peers), axes, 0, 0, tiled=True)  18.6 us
    all_to_all x3, waiting for transfers between devices, exchange(): lax.all_to_all(x.reshape(peers, 1, x.size // peers), axes, 0, 0, tiled=True)  18.1 us
    pallas_call x1, Pallas kernels, shards(): pl.pallas_call(sweep_kernel, out_shape=(distant, distant, small), in_spec...  7.76 us
    pallas_call x1, Pallas kernels, shards(): pl.pallas_call(gather_kernel, out_shape=(big, pltpu.VMEM((8, LINES, NY),...  4.89 us
    pallas_call x1, Pallas kernels, shards(): pl.pallas_call(load_kernel, out_shape=(spread, pltpu.VMEM((NZ * PITCH, NY...  3.77 us
    ppermute x1, starting transfers between devices, shards(): lax.ppermute(last, GX, [(i, (i + 1) % groups) for i in range(groups)])  3.09 us
    pallas_call x1, Pallas kernels, shards(): pl.pallas_call(blend_kernel, out_shape=big, in_specs=[VMEM, HBM, HBM], ou...  2.31 us
    pallas_call x1, Pallas kernels, shards(): pl.pallas_call(lambda *refs: finish_kernel(cells, *refs), out_shape=f32(L...  2.06 us
  transfers between devices with their start and end apart: 5, of which 3 were waited for; matrix products, arithmetic and copies ran while one was open for 0% of the time, Pallas kernels for 23%

profile of v4, /device:TPU:1, one launch (start us, length us, event | category | flops | bytes accessed | tf_op | source)
XLA Modules:
  0.0 65.8 jit_solution(7482415775682351949)
XLA Ops:
  0.0 3.8 %load.1 = (f32[4608,128]{1,0:T(8,128)S(1)}, f32[2304,128]{1,0:T(8,128)S(1)}, f32[64,128]{1,0:T(8,128)S(1)}, f32[64,128]{1,0:T(8,128)S(1)}, f32[64,128]{1,0:T(8,128)S(1)}) custom-call(f32[64,64,128]{2,1,0:T(8,128)} %bitcast.13, f32[32,64,128]{2,1,0:T(8,128)} %v_hbm.1), custom_call_target="tpu_custom_call" | custom-call | tf_op jit(solution)/shard_map/load/pallas_call | solution.py:531
  3.8 3.1 %collective-permute-start.1 = (f32[64,128]{1,0:T(8,128)S(1)}, f32[64,128]{1,0:T(8,128)S(1)}, u32[]{:S(2)}, u32[]{:S(2)}) collective-permute-start(f32[64,128]{1,0:T(8,128)S(1)} %get-tuple-element.26), channel_id=1, source_target_pairs={{0,2},{2,4},{4,6},{6,8},{8,10},{10,12},{12,14},{14,16},{16,18},{18... | collective-permute-start | bytes 98312 | tf_op jit(solution)/shard_map/ppermute | solution.py:541
  6.9 1.3 %collective-permute-start = (f32[64,128]{1,0:T(8,128)S(1)}, f32[64,128]{1,0:T(8,128)S(1)}, u32[]{:S(2)}, u32[]{:S(2)}) collective-permute-start(f32[64,128]{1,0:T(8,128)S(1)} %get-tuple-element.24.edge_ref), channel_id=1, source_target_pairs={{0,1},{1,0},{2,3},{3,2},{4,5},{5,4},{6,7},{7,6},{8,9},{9,8},{10,11... | collective-permute-start | bytes 98312 | tf_op jit(solution)/shard_map/ppermute | solution.py:540
  9.0 4.9 %gather.1 = (f32[4096,128]{1,0:T(8,128)S(1)}, f32[8,64,128]{2,1,0:T(8,128)S(1)}, f32[8,128]{1,0:T(8,128)S(1)}) custom-call(f32[1]{0:T(128)S(6)} %log1p.3.rate_ref.refs_2_.refs_0_, f32[1]{0:T(128)S(6)} %sqrt.7.gain_ref, f32[1]{0:T(128)S(6)} %div.6.sigma_ref.refs_3_, f32[4608,128]{1,0:T(8,128)S(1)} %get-tuple-element.20.o_ref, ...), custom_call_target="tpu_custom_call" | custom-call | tf_op jit(solution)/shard_map/gather/pallas_call | solution.py:544
  13.9 0.0 collective-permute-done.1.before_ref
  13.9 0.0 collective-permute-done.halo_ref
  13.9 1.2 %pack.1 = f32[528,128]{1,0:T(8,128)} custom-call(f32[1]{0:T(128)S(6)} %log1p.3.rate_ref.refs_2_.refs_0_, f32[1]{0:T(128)S(6)} %sqrt.7.gain_ref, f32[8,64,128]{2,1,0:T(8,128)S(1)} %get-tuple-element.22.tips_ref, f32[8,128]{1,0:T(8,128)S(1)} %get-tuple-element.23.sums_ref, f32[64,128]{1,0:T(8,128)S(1)} %get-tuple-element.24.edge_ref, ...), custom_call_target="tpu_custom_call" | custom-call | tf_op jit(solution)/shard_map/pack/pallas_call | solution.py:555
  15.1 7.7 %all-to-all-start = ((f32[16,1,4224]{2,1,0:T(1,128)}), f32[16,1,4224]{2,1,0:T(1,128)S(1)}, u32[]{:S(2)}, u32[]{:S(2)}) async-start(f32[16,1,4224]{2,1,0:T(1,128)} %bitcast.3), calls=%async_computation | async-start | bytes 540672 | tf_op jit(solution)/shard_map/all_to_all | solution.py:504
  22.8 7.8 %sweep.1 = (f32[4096,128]{1,0:T(8,128)}, f32[4096,128]{1,0:T(8,128)}, f32[8,128]{1,0:T(8,128)S(1)}) custom-call(f32[1]{0:T(128)S(6)} %log1p.3.rate_ref.refs_2_.refs_0_, f32[1]{0:T(128)S(6)} %sqrt.7.gain_ref, f32[1]{0:T(128)S(6)} %div.6.sigma_ref.refs_3_, f32[64,64,128]{2,1,0:T(8,128)} %bitcast.14, f32[4096,128]{1,0:T(8,128)S(1)} %get-tuple-element.27.a_ref, ...), custom_call_target="tpu_custom_call" | custom-call | tf_op jit(solution)/shard_map/sweep/pallas_call | solution.py:565
  30.6 4.0 %all-to-all-done = f32[16,1,4224]{2,1,0:T(1,128)S(1)} async-done(((f32[16,1,4224]{2,1,0:T(1,128)}), f32[16,1,4224]{2,1,0:T(1,128)S(1)}, u32[]{:S(2)}, u32[]{:S(2)}) %all-to-all-start) | async-done | bytes 270368 | tf_op jit(solution)/shard_map/all_to_all | solution.py:504
  34.6 1.0 %group.1 = (f32[528,128]{1,0:T(8,128)}, f32[256,128]{1,0:T(8,128)S(1)}) custom-call(s32[1]{0:T(128)} %bitcast.member_ref.refs_0_, f32[1]{0:T(128)S(6)} %log1p.3.rate_ref.refs_2_.refs_0_, f32[1]{0:T(128)S(6)} %sqrt.7.gain_ref, f32[1]{0:T(128)S(6)} %div.6.sigma_ref.refs_3_, f32[528,128]{1,0:T(8,128)S(1)} %bitcast.11, f32[8,128]{1,0:T(8,128)S(1)} %get-tuple-element.23.sums_ref, ...), custom_call_target="tpu_custom_call" | custom-call | tf_op jit(solution)/shard_map/group/pallas_call | solution.py:578
  35.6 6.5 %all-to-all-start.1 = ((f32[16,1,4224]{2,1,0:T(1,128)}), f32[16,1,4224]{2,1,0:T(1,128)S(1)}, u32[]{:S(2)}, u32[]{:S(2)}) async-start(f32[16,1,4224]{2,1,0:T(1,128)} %bitcast.5), calls=%async_computation.1 | async-start | bytes 540672 | tf_op jit(solution)/shard_map/all_to_all | solution.py:504
  42.0 8.4 %all-to-all-done.1 = f32[16,1,4224]{2,1,0:T(1,128)S(1)} async-done(((f32[16,1,4224]{2,1,0:T(1,128)}), f32[16,1,4224]{2,1,0:T(1,128)S(1)}, u32[]{:S(2)}, u32[]{:S(2)}) %all-to-all-start.1) | async-done | bytes 270368 | tf_op jit(solution)/shard_map/all_to_all | solution.py:504
  50.4 0.9 %owner.1 = (f32[144,128]{1,0:T(8,128)}, f32[8,128]{1,0:T(8,128)S(1)}) custom-call(s32[1]{0:T(128)} %bitcast.member_ref.refs_0_, s32[1]{0:T(128)} %bitcast.1.refs_1_, f32[1]{0:T(128)S(6)} %log1p.3.rate_ref.refs_2_.refs_0_, f32[1]{0:T(128)S(6)} %div.6.sigma_ref.refs_3_, f32[528,128]{1,0:T(8,128)S(1)} %bitcast.10, f32[256,128]{1,0:T(8,128)S(1)} %get-tuple-element.30.refs_5_), custom_call_target="tpu_custom_call" | custom-call | tf_op jit(solution)/shard_map/owner/pallas_call | solution.py:591
  51.3 4.4 %all-to-all-start.2 = ((f32[16,1,1152]{2,1,0:T(1,128)}), f32[16,1,1152]{2,1,0:T(1,128)S(1)}, u32[]{:S(2)}, u32[]{:S(2)}) async-start(f32[16,1,1152]{2,1,0:T(1,128)} %bitcast.7), calls=%async_computation.2 | async-start | bytes 147456 | tf_op jit(solution)/shard_map/all_to_all | solution.py:504
  55.7 2.3 %blend.1.refs_3_ = f32[4096,128]{1,0:T(8,128)S(1)} custom-call(f32[8,128]{1,0:T(8,128)S(1)} %get-tuple-element.32.mass_ref.refs_2_, f32[4096,128]{1,0:T(8,128)} %get-tuple-element.33.p_hbm, f32[4096,128]{1,0:T(8,128)} %get-tuple-element.34.q_hbm), custom_call_target="tpu_custom_call" | custom-call | tf_op jit(solution)/shard_map/blend/pallas_call | solution.py:602
  58.1 5.7 %all-to-all-done.2 = f32[16,1,1152]{2,1,0:T(1,128)S(1)} async-done(((f32[16,1,1152]{2,1,0:T(1,128)}), f32[16,1,1152]{2,1,0:T(1,128)S(1)}, u32[]{:S(2)}, u32[]{:S(2)}) %all-to-all-start.2) | async-done | bytes 73760 | tf_op jit(solution)/shard_map/all_to_all | solution.py:504
  63.7 2.1 %finish.1 = f32[64,64,128]{2,1,0:T(8,128)} custom-call(f32[1]{0:T(128)S(6)} %log1p.3.rate_ref.refs_2_.refs_0_, f32[144,128]{1,0:T(8,128)S(1)} %bitcast.12, f32[8,128]{1,0:T(8,128)S(1)} %get-tuple-element.32.mass_ref.refs_2_, f32[4096,128]{1,0:T(8,128)S(1)} %blend.1.refs_3_), custom_call_target="tpu_custom_call" | custom-call | tf_op jit(solution)/shard_map/finish/pallas_call | solution.py:612
Async XLA Ops:
  3.8 10.1 %collective-permute-start.1 = (f32[64,128]{1,0:T(8,128)S(1)}, f32[64,128]{1,0:T(8,128)S(1)}, u32[]{:S(2)}, u32[]{:S(2)}) collective-permute-start(f32[64,128]{1,0:T(8,128)S(1)} %get-tuple-element.26), channel_id=1, source_target_pairs={{0,2},{2,4},{4,6},{6,8},{8,10},{10,12},{12,14},{14,16},{16,18},{18... | collective-permute-start | bytes 98312 | tf_op jit(solution)/shard_map/ppermute | solution.py:541
  6.9 7.0 %collective-permute-start = (f32[64,128]{1,0:T(8,128)S(1)}, f32[64,128]{1,0:T(8,128)S(1)}, u32[]{:S(2)}, u32[]{:S(2)}) collective-permute-start(f32[64,128]{1,0:T(8,128)S(1)} %get-tuple-element.24.edge_ref), channel_id=1, source_target_pairs={{0,1},{1,0},{2,3},{3,2},{4,5},{5,4},{6,7},{7,6},{8,9},{9,8},{10,11... | collective-permute-start | bytes 98312 | tf_op jit(solution)/shard_map/ppermute | solution.py:540
  15.1 19.5 %all-to-all-start = ((f32[16,1,4224]{2,1,0:T(1,128)}), f32[16,1,4224]{2,1,0:T(1,128)S(1)}, u32[]{:S(2)}, u32[]{:S(2)}) async-start(f32[16,1,4224]{2,1,0:T(1,128)} %bitcast.3), calls=%async_computation | async-start | bytes 540672 | tf_op jit(solution)/shard_map/all_to_all | solution.py:504
  35.6 14.9 %all-to-all-start.1 = ((f32[16,1,4224]{2,1,0:T(1,128)}), f32[16,1,4224]{2,1,0:T(1,128)S(1)}, u32[]{:S(2)}, u32[]{:S(2)}) async-start(f32[16,1,4224]{2,1,0:T(1,128)} %bitcast.5), calls=%async_computation.1 | async-start | bytes 540672 | tf_op jit(solution)/shard_map/all_to_all | solution.py:504
  51.3 12.4 %all-to-all-start.2 = ((f32[16,1,1152]{2,1,0:T(1,128)}), f32[16,1,1152]{2,1,0:T(1,128)S(1)}, u32[]{:S(2)}, u32[]{:S(2)}) async-start(f32[16,1,1152]{2,1,0:T(1,128)} %bitcast.7), calls=%async_computation.2 | async-start | bytes 147456 | tf_op jit(solution)/shard_map/all_to_all | solution.py:504

commit v5 on v4

--- a/solution.py
+++ b/solution.py
@@ -29,6 +29,7 @@
 BACK = 2 * SHARE + 1
 PITCH = NX + 8
 ROWS = 8
+UNROLL = 8
 
 PARAMS = pltpu.CompilerParams(vmem_limit_bytes=16 << 20)
 VMEM = pl.BlockSpec(memory_space=pltpu.VMEM)
@@ -79,15 +80,16 @@
 
 def load_kernel(o_hbm, v_hbm, o_ref, v_ref, edge_ref, first_ref, last_ref, sems, v_sems):
     wait = start_planes(o_hbm, o_ref, sems)
-    wait_v = start_planes(v_hbm, v_ref, v_sems)
     lane = lane_of((NZ, NY)) // 2
     for c in range(COMPS):
         wait(c * NZ, (c + 1) * NZ)
+        if c == 0:
+            wait_v = start_planes(v_hbm, v_ref, v_sems)
 
         def step(x, packed):
             return jnp.where(lane == x, pltpu.roll(o_ref[line_rows(x, c), :], 2 * x + 1, 1), packed)
 
-        edge_ref[part(c), :] = lax.fori_loop(0, NX, step, jnp.zeros((NZ, NY), jnp.float32), unroll=8)
+        edge_ref[part(c), :] = lax.fori_loop(0, NX, step, jnp.zeros((NZ, NY), jnp.float32), unroll=16)
         first_ref[part(c), :] = o_ref[line_rows(0, c), :]
         last_ref[part(c), :] = o_ref[line_rows(NX - 1, c), :]
     wait_v(0, NZ)
@@ -118,32 +120,50 @@
     zero = jnp.zeros((NZ, NY), jnp.float32)
     decay = jnp.exp(jnp.full((NZ, NY), -rate, jnp.float32))
 
+    def fold(total, block):
+        for b in range(NZ // ROWS):
+            total = total + block[b * ROWS : (b + 1) * ROWS, :]
+        return total
+
+    def around_of(o):
+        near_z = pltpu.roll(o, 1, 0) + pltpu.roll(o, NZ - 1, 0)
+        return -0.5 * (near_z + (pltpu.roll(o, 1, 1) + pltpu.roll(o, NY - 1, 1)))
+
+    def read(x):
+        o = [o_ref[line_rows(x, c), :] for c in range(COMPS)]
+        return o, [around_of(one) for one in o]
+
     def step(x, carry):
-        before, cross, square, sums = carry
-        o = [o_ref[line_rows(x, c), :] for c in range(COMPS)]
-        weights = [tab_scr[k, pl.ds(x, 1), :] for k in range(4)]
+        before, o, around, cross, square = carry
+        after = read(jnp.minimum(x + 1, NX - 1))
         s = [o[0] * o[0], o[1] * o[1]]
         both = COUPLING_CROSS * (s[0] + s[1])
         base = (v_ref[line_rows(x), :] + 2.0) + both
         own = (COUPLING_FIRST - COUPLING_CROSS, COUPLING_SECOND - COUPLING_CROSS)
-        new_cross, new_square, new_sums = [], [], []
+        new_cross, new_square = [], []
         for c in range(COMPS):
-            around = pltpu.roll(o[c], 1, 0) + pltpu.roll(o[c], NZ - 1, 0)
-            around = around + (pltpu.roll(o[c], 1, 1) + pltpu.roll(o[c], NY - 1, 1))
-            a = (base + own[c] * s[c]) * o[c] - 0.5 * around
+            a = (base + own[c] * s[c]) * o[c] + around[c]
             a_ref[rows(x, c), :] = a
-            new_cross.append(cross[c] + o[c] * ((a + o[c]) - before[c]))
-            new_square.append(square[c] + s[c])
-            new_sums.append(
-                [decay * sums[c][0] + o[c], decay * sums[c][1] + a]
-                + [sums[c][1 + k] + weights[k] * o[c] for k in range(1, 4)]
-                + [sums[c][4 + k] + weights[k] * a for k in range(1, 4)]
+            new_cross.append(fold(cross[c], o[c] * ((a + o[c]) - before[c])))
+            new_square.append(fold(square[c], s[c]))
+        return o, after[0], after[1], new_cross, new_square
+
+    part_sum = [jnp.zeros((ROWS, NY), jnp.float32)] * 2
+    start = read(0)
+    cross, square = lax.fori_loop(0, NX, step, ([zero] * 2, *start, part_sum, part_sum), unroll=UNROLL)[3:]
+
+    sums = []
+    for c in range(COMPS):
+        def add(x, sums):
+            o, a = o_ref[line_rows(x, c), :], a_ref[rows(x, c), :]
+            weights = [tab_scr[k, pl.ds(x, 1), :] for k in range(4)]
+            return (
+                [decay * sums[0] + o, decay * sums[1] + a]
+                + [sums[1 + k] + weights[k] * o for k in range(1, 4)]
+                + [sums[4 + k] + weights[k] * a for k in range(1, 4)]
             )
-        return o, new_cross, new_square, new_sums
-
-    _, cross, square, sums = lax.fori_loop(
-        0, NX, step, ([zero] * 2, [zero] * 2, [zero] * 2, [[zero] * 8] * 2), unroll=2
-    )
+
+        sums.append(lax.fori_loop(0, NX, add, [zero] * 8, unroll=8))
     once = jnp.exp(jnp.full((NZ, NY), -rate, jnp.float32))
     for c in range(COMPS):
         f_o, f_a, b_o, r_o, s_o, b_a, r_a, s_a = sums[c]
@@ -199,7 +219,7 @@
             return fo, fa
 
         wait(c * NZ, (c + 1) * NZ)
-        lax.fori_loop(0, NX, ahead, (zero, zero), unroll=4)
+        lax.fori_loop(0, NX, ahead, (zero, zero), unroll=8)
         shift = jnp.broadcast_to(local_shift(sums_ref, c, sigma_ref[0]), (NZ, NY))
 
         def behind(k, carry):
@@ -216,7 +236,7 @@
             w = p + shift * q
             return do + o, da + a, ww + w * w, wq + w * q, qq + q * q
 
-        _, _, ww, wq, qq = lax.fori_loop(0, NX, behind, (zero,) * 5, unroll=4)
+        _, _, ww, wq, qq = lax.fori_loop(0, NX, behind, (zero,) * 5, unroll=8)
         for k, value in enumerate((ww, wq, qq)):
             local_ref[3 * c + k : 3 * c + k + 1, :] = jnp.sum(value, axis=0, keepdims=True)
         for one in send(c):
@@ -295,7 +315,7 @@
     return jnp.exp(-rate * float(NX) * steps)
 
 
-def group_kernel(member_ref, rate_ref, gain_ref, sigma_ref, got_ref, sums_ref, local_ref, msg_ref, pre_ref):
+def group_kernel(member_ref, mine_ref, rate_ref, gain_ref, sigma_ref, got_ref, sums_ref, local_ref, msg_ref, pre_ref):
     rate, sigma = rate_ref[0], sigma_ref[0]
     gain4 = TAU * gain_ref[0]
     shape = (2 * SHARE, NY)
@@ -581,11 +601,11 @@
             pltpu.VMEM((MEMBERS * STRIDE, NY), jnp.float32),
             pltpu.VMEM((4 * SHARE * MEMBERS, NY), jnp.float32),
         ),
-        in_specs=[SMEM] * 4 + [VMEM] * 3,
+        in_specs=[SMEM] * 5 + [VMEM] * 3,
         out_specs=(VMEM,) * 2,
         name="group",
         compiler_params=PARAMS,
-    )(member.reshape(1), rate, gain, sigma, near(got), sums, local)
+    )(member.reshape(1), mine.reshape(1), rate, gain, sigma, near(got), sums, local)
     outer = exchange(joint, OUTER)
 
     back, mass = pl.pallas_call(

time: 66.3 us -> 63.4 us (0.956)
  blocking collectives: 0 us -> 14.3 us
  waiting for transfers between devices: 18.1 us -> 10.9 us
  starting transfers between devices: 23 us -> 16.8 us
  Pallas kernels: 23.9 us -> 20 us
    all_to_all x0 -> x1, blocking collectives: none -> 14.3 us  [exchange(): lax.all_to_all(x.reshape(peers, 1, x.size // peers), axes, 0, 0, tiled=True)]
    all_to_all x3 -> x2, waiting for transfers between devices: 18.1 us -> 10.9 us  [exchange(): lax.all_to_all(x.reshape(peers, 1, x.size // peers), axes, 0, 0, tiled=True)]
    all_to_all x3 -> x2, starting transfers between devices: 18.6 us -> 12.4 us  [exchange(): lax.all_to_all(x.reshape(peers, 1, x.size // peers), axes, 0, 0, tiled=True)]
    pallas_call x1, Pallas kernels: 4.89 us -> 3.38 us  [shards(): pl.pallas_call(gather_kernel, out_shape=(big, pltpu.VMEM((8, LINES, NY),...]
    pallas_call x1, Pallas kernels: 7.76 us -> 6.64 us  [shards(): pl.pallas_call(sweep_kernel, out_shape=(distant, distant, small), in_spec...]
    pallas_call x1, Pallas kernels: 0.97 us -> 0.25 us  [shards(): pl.pallas_call(group_kernel, out_shape=(pltpu.VMEM((MEMBERS * STRIDE, NY)...]
  transfers between devices with their start and end apart: 5 -> 4, of which waited for: 3 -> 2; matrix products, arithmetic and copies ran while one was open for 0% -> 0% of each run, Pallas kernels for 23% -> 20%
where the time goes in v5:
time: 63.4 us; the launch traced here: 62.8 us
  Pallas kernels  20 us (32%)
  starting transfers between devices  16.8 us (26%)
  blocking collectives  14.3 us (23%)
  waiting for transfers between devices  10.9 us (17%)
  between operations  0.87 us (1%)
    all_to_all x1, blocking collectives, exchange(): lax.all_to_all(x.reshape(peers, 1, x.size // peers), axes, 0, 0, tiled=True)  14.3 us
    all_to_all x2, starting transfers between devices, exchange(): lax.all_to_all(x.reshape(peers, 1, x.size // peers), axes, 0, 0, tiled=True)  12.4 us
    all_to_all x2, waiting for transfers between devices, exchange(): lax.all_to_all(x.reshape(peers, 1, x.size // peers), axes, 0, 0, tiled=True)  10.9 us
    pallas_call x1, Pallas kernels, shards(): pl.pallas_call(sweep_kernel, out_shape=(distant, distant, small), in_spec...  6.64 us
    pallas_call x1, Pallas kernels, shards(): pl.pallas_call(gather_kernel, out_shape=(big, pltpu.VMEM((8, LINES, NY),...  3.38 us
    pallas_call x1, Pallas kernels, shards(): pl.pallas_call(load_kernel, out_shape=(spread, pltpu.VMEM((NZ * PITCH, NY...  3.26 us
    ppermute x1, starting transfers between devices, shards(): lax.ppermute(last, GX, [(i, (i + 1) % groups) for i in range(groups)])  3.09 us
    pallas_call x1, Pallas kernels, shards(): pl.pallas_call(blend_kernel, out_shape=big, in_specs=[VMEM, HBM, HBM], ou...  2.31 us
  transfers between devices with their start and end apart: 4, of which 2 were waited for; matrix products, arithmetic and copies ran while one was open for 0% of the time, Pallas kernels for 20%

profile of v5, /device:TPU:1, one launch (start us, length us, event | category | flops | bytes accessed | tf_op | source)
XLA Modules:
  0.0 62.8 jit_solution(6745358998947594860)
XLA Ops:
  0.0 3.3 %load.1 = (f32[4608,128]{1,0:T(8,128)S(1)}, f32[2304,128]{1,0:T(8,128)S(1)}, f32[64,128]{1,0:T(8,128)S(1)}, f32[64,128]{1,0:T(8,128)S(1)}, f32[64,128]{1,0:T(8,128)S(1)}) custom-call(f32[64,64,128]{2,1,0:T(8,128)} %bitcast.14, f32[32,64,128]{2,1,0:T(8,128)} %v_hbm.1), custom_call_target="tpu_custom_call" | custom-call | tf_op jit(solution)/shard_map/load/pallas_call | solution.py:551
  3.3 3.1 %collective-permute-start.1 = (f32[64,128]{1,0:T(8,128)S(1)}, f32[64,128]{1,0:T(8,128)S(1)}, u32[]{:S(2)}, u32[]{:S(2)}) collective-permute-start(f32[64,128]{1,0:T(8,128)S(1)} %get-tuple-element.26), channel_id=1, source_target_pairs={{0,2},{2,4},{4,6},{6,8},{8,10},{10,12},{12,14},{14,16},{16,18},{18... | collective-permute-start | bytes 98312 | tf_op jit(solution)/shard_map/ppermute | solution.py:561
  6.4 1.3 %collective-permute-start = (f32[64,128]{1,0:T(8,128)S(1)}, f32[64,128]{1,0:T(8,128)S(1)}, u32[]{:S(2)}, u32[]{:S(2)}) collective-permute-start(f32[64,128]{1,0:T(8,128)S(1)} %get-tuple-element.24.edge_ref), channel_id=1, source_target_pairs={{0,1},{1,0},{2,3},{3,2},{4,5},{5,4},{6,7},{7,6},{8,9},{9,8},{10,11... | collective-permute-start | bytes 98312 | tf_op jit(solution)/shard_map/ppermute | solution.py:560
  8.5 3.4 %gather.1 = (f32[4096,128]{1,0:T(8,128)S(1)}, f32[8,64,128]{2,1,0:T(8,128)S(1)}, f32[8,128]{1,0:T(8,128)S(1)}) custom-call(f32[1]{0:T(128)S(6)} %log1p.3.rate_ref.refs_2_.refs_0_, f32[1]{0:T(128)S(6)} %sqrt.7.gain_ref, f32[1]{0:T(128)S(6)} %div.6.sigma_ref.refs_3_, f32[4608,128]{1,0:T(8,128)S(1)} %get-tuple-element.20.o_ref, ...), custom_call_target="tpu_custom_call" | custom-call | tf_op jit(solution)/shard_map/gather/pallas_call | solution.py:564
  11.9 0.0 collective-permute-done.1.before_ref
  11.9 0.0 collective-permute-done.halo_ref
  11.9 1.2 %pack.1 = f32[528,128]{1,0:T(8,128)} custom-call(f32[1]{0:T(128)S(6)} %log1p.3.rate_ref.refs_2_.refs_0_, f32[1]{0:T(128)S(6)} %sqrt.7.gain_ref, f32[8,64,128]{2,1,0:T(8,128)S(1)} %get-tuple-element.22.tips_ref, f32[8,128]{1,0:T(8,128)S(1)} %get-tuple-element.23.sums_ref, f32[64,128]{1,0:T(8,128)S(1)} %get-tuple-element.24.edge_ref, ...), custom_call_target="tpu_custom_call" | custom-call | tf_op jit(solution)/shard_map/pack/pallas_call | solution.py:575
  13.1 8.0 %all-to-all-start = ((f32[16,1,4224]{2,1,0:T(1,128)}), f32[16,1,4224]{2,1,0:T(1,128)S(1)}, u32[]{:S(2)}, u32[]{:S(2)}) async-start(f32[16,1,4224]{2,1,0:T(1,128)} %bitcast.3), calls=%async_computation | async-start | bytes 540672 | tf_op jit(solution)/shard_map/all_to_all | solution.py:524
  21.1 6.6 %sweep.1 = (f32[4096,128]{1,0:T(8,128)}, f32[4096,128]{1,0:T(8,128)}, f32[8,128]{1,0:T(8,128)S(1)}) custom-call(f32[1]{0:T(128)S(6)} %log1p.3.rate_ref.refs_2_.refs_0_, f32[1]{0:T(128)S(6)} %sqrt.7.gain_ref, f32[1]{0:T(128)S(6)} %div.6.sigma_ref.refs_3_, f32[64,64,128]{2,1,0:T(8,128)} %bitcast.15, f32[4096,128]{1,0:T(8,128)S(1)} %get-tuple-element.27.a_ref, ...), custom_call_target="tpu_custom_call" | custom-call | tf_op jit(solution)/shard_map/sweep/pallas_call | solution.py:585
  27.8 5.2 %all-to-all-done = f32[16,1,4224]{2,1,0:T(1,128)S(1)} async-done(((f32[16,1,4224]{2,1,0:T(1,128)}), f32[16,1,4224]{2,1,0:T(1,128)S(1)}, u32[]{:S(2)}, u32[]{:S(2)}) %all-to-all-start) | async-done | bytes 270368 | tf_op jit(solution)/shard_map/all_to_all | solution.py:524
  33.0 0.2 group.1
  33.2 14.3 %all_to_all.15 = f32[16,1,4224]{2,1,0:T(1,128)S(1)} all-to-all(f32[16,1,4224]{2,1,0:T(1,128)S(1)} %bitcast.13), channel_id=1, replica_groups=mesh['gx_0'=2,'gx_1'=4,'gx_2'=8,'gx_3'=2,'gy'=2] {'gx_0','gx_1','gy'}, dimensions={0} | all-to-all | bytes 540672 | tf_op jit(solution)/shard_map/all_to_all | solution.py:524
  47.5 0.9 %owner.1 = (f32[144,128]{1,0:T(8,128)}, f32[8,128]{1,0:T(8,128)S(1)}) custom-call(s32[1]{0:T(128)} %bitcast.member_ref.refs_0_, s32[1]{0:T(128)} %bitcast.1.mine_ref.refs_1_, f32[1]{0:T(128)S(6)} %log1p.3.rate_ref.refs_2_.refs_0_, f32[1]{0:T(128)S(6)} %div.6.sigma_ref.refs_3_, f32[528,128]{1,0:T(8,128)S(1)} %bitcast.11, f32[256,128]{1,0:T(8,128)S(1)} %get-tuple-element.30.refs_5_), custom_call_target="tpu_custom_call" | custom-call | tf_op jit(solution)/shard_map/owner/pallas_call | solution.py:611
  48.4 4.4 %all-to-all-start.2 = ((f32[16,1,1152]{2,1,0:T(1,128)}), f32[16,1,1152]{2,1,0:T(1,128)S(1)}, u32[]{:S(2)}, u32[]{:S(2)}) async-start(f32[16,1,1152]{2,1,0:T(1,128)} %bitcast.7), calls=%async_computation.2 | async-start | bytes 147456 | tf_op jit(solution)/shard_map/all_to_all | solution.py:524
  52.8 2.3 %blend.1.refs_3_ = f32[4096,128]{1,0:T(8,128)S(1)} custom-call(f32[8,128]{1,0:T(8,128)S(1)} %get-tuple-element.32.mass_ref.refs_2_, f32[4096,128]{1,0:T(8,128)} %get-tuple-element.33.p_hbm, f32[4096,128]{1,0:T(8,128)} %get-tuple-element.34.q_hbm), custom_call_target="tpu_custom_call" | custom-call | tf_op jit(solution)/shard_map/blend/pallas_call | solution.py:622
  55.1 5.7 %all-to-all-done.2 = f32[16,1,1152]{2,1,0:T(1,128)S(1)} async-done(((f32[16,1,1152]{2,1,0:T(1,128)}), f32[16,1,1152]{2,1,0:T(1,128)S(1)}, u32[]{:S(2)}, u32[]{:S(2)}) %all-to-all-start.2) | async-done | bytes 73760 | tf_op jit(solution)/shard_map/all_to_all | solution.py:524
  60.8 2.1 %finish.1 = f32[64,64,128]{2,1,0:T(8,128)} custom-call(f32[1]{0:T(128)S(6)} %log1p.3.rate_ref.refs_2_.refs_0_, f32[144,128]{1,0:T(8,128)S(1)} %bitcast.12, f32[8,128]{1,0:T(8,128)S(1)} %get-tuple-element.32.mass_ref.refs_2_, f32[4096,128]{1,0:T(8,128)S(1)} %blend.1.refs_3_), custom_call_target="tpu_custom_call" | custom-call | tf_op jit(solution)/shard_map/finish/pallas_call | solution.py:632
Async XLA Ops:
  3.3 8.6 %collective-permute-start.1 = (f32[64,128]{1,0:T(8,128)S(1)}, f32[64,128]{1,0:T(8,128)S(1)}, u32[]{:S(2)}, u32[]{:S(2)}) collective-permute-start(f32[64,128]{1,0:T(8,128)S(1)} %get-tuple-element.26), channel_id=1, source_target_pairs={{0,2},{2,4},{4,6},{6,8},{8,10},{10,12},{12,14},{14,16},{16,18},{18... | collective-permute-start | bytes 98312 | tf_op jit(solution)/shard_map/ppermute | solution.py:561
  6.4 5.5 %collective-permute-start = (f32[64,128]{1,0:T(8,128)S(1)}, f32[64,128]{1,0:T(8,128)S(1)}, u32[]{:S(2)}, u32[]{:S(2)}) collective-permute-start(f32[64,128]{1,0:T(8,128)S(1)} %get-tuple-element.24.edge_ref), channel_id=1, source_target_pairs={{0,1},{1,0},{2,3},{3,2},{4,5},{5,4},{6,7},{7,6},{8,9},{9,8},{10,11... | collective-permute-start | bytes 98312 | tf_op jit(solution)/shard_map/ppermute | solution.py:560
  13.1 19.9 %all-to-all-start = ((f32[16,1,4224]{2,1,0:T(1,128)}), f32[16,1,4224]{2,1,0:T(1,128)S(1)}, u32[]{:S(2)}, u32[]{:S(2)}) async-start(f32[16,1,4224]{2,1,0:T(1,128)} %bitcast.3), calls=%async_computation | async-start | bytes 540672 | tf_op jit(solution)/shard_map/all_to_all | solution.py:524
  48.4 12.4 %all-to-all-start.2 = ((f32[16,1,1152]{2,1,0:T(1,128)}), f32[16,1,1152]{2,1,0:T(1,128)S(1)}, u32[]{:S(2)}, u32[]{:S(2)}) async-start(f32[16,1,1152]{2,1,0:T(1,128)} %bitcast.7), calls=%async_computation.2 | async-start | bytes 147456 | tf_op jit(solution)/shard_map/all_to_all | solution.py:524

commit v6 on v5

--- a/solution.py
+++ b/solution.py
@@ -115,11 +115,12 @@
     rate = rate_ref[0]
     gain4 = TAU * gain_ref[0]
     keep = 1.0 - TAU * sigma_ref[0]
-    for k, table in enumerate(tables(rate, 1)):
-        tab_scr[k] = table
+    tip_f, tip_b, cell_r, cell_s = tables(rate, 1)
+    tab_scr[0] = 0.5 * (tip_f + tip_b)
+    tab_scr[1] = 0.5 * (tip_f - tip_b)
+    tab_scr[2] = 0.5 * (cell_r + cell_s)
+    tab_scr[3] = 0.5 * (cell_r - cell_s)
     zero = jnp.zeros((NZ, NY), jnp.float32)
-    decay = jnp.exp(jnp.full((NZ, NY), -rate, jnp.float32))
-
     def fold(total, block):
         for b in range(NZ // ROWS):
             total = total + block[b * ROWS : (b + 1) * ROWS, :]
@@ -155,18 +156,25 @@
     sums = []
     for c in range(COMPS):
         def add(x, sums):
-            o, a = o_ref[line_rows(x, c), :], a_ref[rows(x, c), :]
+            y = NX - 1 - x
             weights = [tab_scr[k, pl.ds(x, 1), :] for k in range(4)]
-            return (
-                [decay * sums[0] + o, decay * sums[1] + a]
-                + [sums[1 + k] + weights[k] * o for k in range(1, 4)]
-                + [sums[4 + k] + weights[k] * a for k in range(1, 4)]
+            fields = (
+                (o_ref[line_rows(x, c), :], o_ref[line_rows(y, c), :]),
+                (a_ref[rows(x, c), :], a_ref[rows(y, c), :]),
             )
-
-        sums.append(lax.fori_loop(0, NX, add, [zero] * 8, unroll=8))
+            return [
+                [
+                    old + weight * (one + two if k % 2 == 0 else one - two)
+                    for k, (old, weight) in enumerate(zip(olds, weights))
+                ]
+                for olds, (one, two) in zip(sums, fields)
+            ]
+
+        found = lax.fori_loop(0, NX // 2, add, [[zero] * 4] * 2, unroll=4)
+        sums.append([m for f in found for m in (f[0] + f[1], f[0] - f[1], f[2] + f[3], f[2] - f[3])])
     once = jnp.exp(jnp.full((NZ, NY), -rate, jnp.float32))
     for c in range(COMPS):
-        f_o, f_a, b_o, r_o, s_o, b_a, r_a, s_a = sums[c]
+        f_o, b_o, r_o, s_o, f_a, b_a, r_a, s_a = sums[c]
         tips_ref[0, part(c), :] = f_o
         tips_ref[1, part(c), :] = b_o
         tips_ref[2, part(c), :] = f_a

time: 63.4 us -> 63.1 us (level)
  transfers between devices with their start and end apart: 4 -> 4, of which waited for: 2 -> 2; matrix products, arithmetic and copies ran while one was open for 0% -> 0% of each run, Pallas kernels for 20% -> 19%
where the time goes in v6:
time: 63.1 us; the launch traced here: 62.6 us
  Pallas kernels  19.8 us (31%)
  starting transfers between devices  17 us (27%)
  blocking collectives  14 us (22%)
  waiting for transfers between devices  10.9 us (17%)
  between operations  0.87 us (1%)
    all_to_all x1, blocking collectives, exchange(): lax.all_to_all(x.reshape(peers, 1, x.size // peers), axes, 0, 0, tiled=True)  14 us
    all_to_all x2, starting transfers between devices, exchange(): lax.all_to_all(x.reshape(peers, 1, x.size // peers), axes, 0, 0, tiled=True)  12.7 us
    all_to_all x2, waiting for transfers between devices, exchange(): lax.all_to_all(x.reshape(peers, 1, x.size // peers), axes, 0, 0, tiled=True)  10.9 us
    pallas_call x1, Pallas kernels, shards(): pl.pallas_call(sweep_kernel, out_shape=(distant, distant, small), in_spec...  6.64 us
    pallas_call x1, Pallas kernels, shards(): pl.pallas_call(load_kernel, out_shape=(spread, pltpu.VMEM((NZ * PITCH, NY...  3.26 us
    pallas_call x1, Pallas kernels, shards(): pl.pallas_call(gather_kernel, out_shape=(big, pltpu.VMEM((8, LINES, NY),...  3.13 us
    ppermute x1, starting transfers between devices, shards(): lax.ppermute(last, GX, [(i, (i + 1) % groups) for i in range(groups)])  3.09 us
    pallas_call x1, Pallas kernels, shards(): pl.pallas_call(blend_kernel, out_shape=big, in_specs=[VMEM, HBM, HBM], ou...  2.31 us
  transfers between devices with their start and end apart: 4, of which 2 were waited for; matrix products, arithmetic and copies ran while one was open for 0% of the time, Pallas kernels for 19%

profile of v6, /device:TPU:1, one launch (start us, length us, event | category | flops | bytes accessed | tf_op | source)
XLA Modules:
  0.0 62.6 jit_solution(14864383957996868887)
XLA Ops:
  0.0 3.3 %load.1 = (f32[4608,128]{1,0:T(8,128)S(1)}, f32[2304,128]{1,0:T(8,128)S(1)}, f32[64,128]{1,0:T(8,128)S(1)}, f32[64,128]{1,0:T(8,128)S(1)}, f32[64,128]{1,0:T(8,128)S(1)}) custom-call(f32[64,64,128]{2,1,0:T(8,128)} %bitcast.14, f32[32,64,128]{2,1,0:T(8,128)} %v_hbm.1), custom_call_target="tpu_custom_call" | custom-call | tf_op jit(solution)/shard_map/load/pallas_call | solution.py:559
  3.3 3.1 %collective-permute-start.1 = (f32[64,128]{1,0:T(8,128)S(1)}, f32[64,128]{1,0:T(8,128)S(1)}, u32[]{:S(2)}, u32[]{:S(2)}) collective-permute-start(f32[64,128]{1,0:T(8,128)S(1)} %get-tuple-element.26), channel_id=1, source_target_pairs={{0,2},{2,4},{4,6},{6,8},{8,10},{10,12},{12,14},{14,16},{16,18},{18... | collective-permute-start | bytes 98312 | tf_op jit(solution)/shard_map/ppermute | solution.py:569
  6.4 1.3 %collective-permute-start = (f32[64,128]{1,0:T(8,128)S(1)}, f32[64,128]{1,0:T(8,128)S(1)}, u32[]{:S(2)}, u32[]{:S(2)}) collective-permute-start(f32[64,128]{1,0:T(8,128)S(1)} %get-tuple-element.24.edge_ref), channel_id=1, source_target_pairs={{0,1},{1,0},{2,3},{3,2},{4,5},{5,4},{6,7},{7,6},{8,9},{9,8},{10,11... | collective-permute-start | bytes 98312 | tf_op jit(solution)/shard_map/ppermute | solution.py:568
  8.5 3.1 %gather.1 = (f32[4096,128]{1,0:T(8,128)S(1)}, f32[8,64,128]{2,1,0:T(8,128)S(1)}, f32[8,128]{1,0:T(8,128)S(1)}) custom-call(f32[1]{0:T(128)S(6)} %log1p.3.rate_ref.refs_2_.refs_0_, f32[1]{0:T(128)S(6)} %sqrt.7.gain_ref, f32[1]{0:T(128)S(6)} %div.6.sigma_ref.refs_3_, f32[4608,128]{1,0:T(8,128)S(1)} %get-tuple-element.20.o_ref, ...), custom_call_target="tpu_custom_call" | custom-call | tf_op jit(solution)/shard_map/gather/pallas_call | solution.py:572
  11.6 0.0 collective-permute-done.1.before_ref
  11.6 0.0 collective-permute-done.halo_ref
  11.6 1.2 %pack.1 = f32[528,128]{1,0:T(8,128)} custom-call(f32[1]{0:T(128)S(6)} %log1p.3.rate_ref.refs_2_.refs_0_, f32[1]{0:T(128)S(6)} %sqrt.7.gain_ref, f32[8,64,128]{2,1,0:T(8,128)S(1)} %get-tuple-element.22.tips_ref, f32[8,128]{1,0:T(8,128)S(1)} %get-tuple-element.23.sums_ref, f32[64,128]{1,0:T(8,128)S(1)} %get-tuple-element.24.edge_ref, ...), custom_call_target="tpu_custom_call" | custom-call | tf_op jit(solution)/shard_map/pack/pallas_call | solution.py:583
  12.9 8.2 %all-to-all-start = ((f32[16,1,4224]{2,1,0:T(1,128)}), f32[16,1,4224]{2,1,0:T(1,128)S(1)}, u32[]{:S(2)}, u32[]{:S(2)}) async-start(f32[16,1,4224]{2,1,0:T(1,128)} %bitcast.3), calls=%async_computation | async-start | bytes 540672 | tf_op jit(solution)/shard_map/all_to_all | solution.py:532
  21.1 6.6 %sweep.1 = (f32[4096,128]{1,0:T(8,128)}, f32[4096,128]{1,0:T(8,128)}, f32[8,128]{1,0:T(8,128)S(1)}) custom-call(f32[1]{0:T(128)S(6)} %log1p.3.rate_ref.refs_2_.refs_0_, f32[1]{0:T(128)S(6)} %sqrt.7.gain_ref, f32[1]{0:T(128)S(6)} %div.6.sigma_ref.refs_3_, f32[64,64,128]{2,1,0:T(8,128)} %bitcast.15, f32[4096,128]{1,0:T(8,128)S(1)} %get-tuple-element.27.a_ref, ...), custom_call_target="tpu_custom_call" | custom-call | tf_op jit(solution)/shard_map/sweep/pallas_call | solution.py:593
  27.8 5.2 %all-to-all-done = f32[16,1,4224]{2,1,0:T(1,128)S(1)} async-done(((f32[16,1,4224]{2,1,0:T(1,128)}), f32[16,1,4224]{2,1,0:T(1,128)S(1)}, u32[]{:S(2)}, u32[]{:S(2)}) %all-to-all-start) | async-done | bytes 270368 | tf_op jit(solution)/shard_map/all_to_all | solution.py:532
  33.0 0.2 group.1
  33.2 14.0 %all_to_all.15 = f32[16,1,4224]{2,1,0:T(1,128)S(1)} all-to-all(f32[16,1,4224]{2,1,0:T(1,128)S(1)} %bitcast.13), channel_id=1, replica_groups=mesh['gx_0'=2,'gx_1'=4,'gx_2'=8,'gx_3'=2,'gy'=2] {'gx_0','gx_1','gy'}, dimensions={0} | all-to-all | bytes 540672 | tf_op jit(solution)/shard_map/all_to_all | solution.py:532
  47.3 0.9 %owner.1 = (f32[144,128]{1,0:T(8,128)}, f32[8,128]{1,0:T(8,128)S(1)}) custom-call(s32[1]{0:T(128)} %bitcast.member_ref.refs_0_, s32[1]{0:T(128)} %bitcast.1.mine_ref.refs_1_, f32[1]{0:T(128)S(6)} %log1p.3.rate_ref.refs_2_.refs_0_, f32[1]{0:T(128)S(6)} %div.6.sigma_ref.refs_3_, f32[528,128]{1,0:T(8,128)S(1)} %bitcast.11, f32[256,128]{1,0:T(8,128)S(1)} %get-tuple-element.30.refs_5_), custom_call_target="tpu_custom_call" | custom-call | tf_op jit(solution)/shard_map/owner/pallas_call | solution.py:619
  48.1 4.4 %all-to-all-start.2 = ((f32[16,1,1152]{2,1,0:T(1,128)}), f32[16,1,1152]{2,1,0:T(1,128)S(1)}, u32[]{:S(2)}, u32[]{:S(2)}) async-start(f32[16,1,1152]{2,1,0:T(1,128)} %bitcast.7), calls=%async_computation.2 | async-start | bytes 147456 | tf_op jit(solution)/shard_map/all_to_all | solution.py:532
  52.6 2.3 %blend.1.refs_3_ = f32[4096,128]{1,0:T(8,128)S(1)} custom-call(f32[8,128]{1,0:T(8,128)S(1)} %get-tuple-element.32.mass_ref.refs_2_, f32[4096,128]{1,0:T(8,128)} %get-tuple-element.33.p_hbm, f32[4096,128]{1,0:T(8,128)} %get-tuple-element.34.q_hbm), custom_call_target="tpu_custom_call" | custom-call | tf_op jit(solution)/shard_map/blend/pallas_call | solution.py:630
  54.9 5.7 %all-to-all-done.2 = f32[16,1,1152]{2,1,0:T(1,128)S(1)} async-done(((f32[16,1,1152]{2,1,0:T(1,128)}), f32[16,1,1152]{2,1,0:T(1,128)S(1)}, u32[]{:S(2)}, u32[]{:S(2)}) %all-to-all-start.2) | async-done | bytes 73760 | tf_op jit(solution)/shard_map/all_to_all | solution.py:532
  60.5 2.1 %finish.1 = f32[64,64,128]{2,1,0:T(8,128)} custom-call(f32[1]{0:T(128)S(6)} %log1p.3.rate_ref.refs_2_.refs_0_, f32[144,128]{1,0:T(8,128)S(1)} %bitcast.12, f32[8,128]{1,0:T(8,128)S(1)} %get-tuple-element.32.mass_ref.refs_2_, f32[4096,128]{1,0:T(8,128)S(1)} %blend.1.refs_3_), custom_call_target="tpu_custom_call" | custom-call | tf_op jit(solution)/shard_map/finish/pallas_call | solution.py:640
Async XLA Ops:
  3.3 8.3 %collective-permute-start.1 = (f32[64,128]{1,0:T(8,128)S(1)}, f32[64,128]{1,0:T(8,128)S(1)}, u32[]{:S(2)}, u32[]{:S(2)}) collective-permute-start(f32[64,128]{1,0:T(8,128)S(1)} %get-tuple-element.26), channel_id=1, source_target_pairs={{0,2},{2,4},{4,6},{6,8},{8,10},{10,12},{12,14},{14,16},{16,18},{18... | collective-permute-start | bytes 98312 | tf_op jit(solution)/shard_map/ppermute | solution.py:569
  6.4 5.3 %collective-permute-start = (f32[64,128]{1,0:T(8,128)S(1)}, f32[64,128]{1,0:T(8,128)S(1)}, u32[]{:S(2)}, u32[]{:S(2)}) collective-permute-start(f32[64,128]{1,0:T(8,128)S(1)} %get-tuple-element.24.edge_ref), channel_id=1, source_target_pairs={{0,1},{1,0},{2,3},{3,2},{4,5},{5,4},{6,7},{7,6},{8,9},{9,8},{10,11... | collective-permute-start | bytes 98312 | tf_op jit(solution)/shard_map/ppermute | solution.py:568
  12.9 20.1 %all-to-all-start = ((f32[16,1,4224]{2,1,0:T(1,128)}), f32[16,1,4224]{2,1,0:T(1,128)S(1)}, u32[]{:S(2)}, u32[]{:S(2)}) async-start(f32[16,1,4224]{2,1,0:T(1,128)} %bitcast.3), calls=%async_computation | async-start | bytes 540672 | tf_op jit(solution)/shard_map/all_to_all | solution.py:532
  48.1 12.4 %all-to-all-start.2 = ((f32[16,1,1152]{2,1,0:T(1,128)}), f32[16,1,1152]{2,1,0:T(1,128)S(1)}, u32[]{:S(2)}, u32[]{:S(2)}) async-start(f32[16,1,1152]{2,1,0:T(1,128)} %bitcast.7), calls=%async_computation.2 | async-start | bytes 147456 | tf_op jit(solution)/shard_map/all_to_all | solution.py:532
